TPU v7x, 128 devices: a whole 4x4x4 slice. The times are simulated.
128 devices in a mesh: dp: 4 (over x), seq: 32 (over y, z, core).
Axes of the slice: x: 4, y: 4, z: 4, core: 2. Of those that a mesh axis runs over, the one named last changes fastest.
Arguments:
- hidden: bfloat16 [8, 6144, 3072], P('dp', 'seq'), may hold values from -6 to 6
- cotangent: bfloat16 [8, 6144, 1536], P('dp', 'seq'), may hold values from -6 to 6
- lengths: int32 [8], P('dp'), may hold values from 768 to 6144, as said below
- kernel: float32 [1536, 31], replicated, may hold values from -1 to 1
- conv_gain: float32 [1536], replicated, may hold values from 0.1 to 1.9
- w_out: bfloat16 [1536, 1536], replicated, may hold values from -0.15625 to 0.15625
Outputs:
- grad_hidden: bfloat16 [8, 6144, 3072], P('dp', 'seq')
- grad_w_out: float32 [1536, 1536], P(('dp', 'seq'))
- grad_kernel: float32 [1536, 31], P(('dp', 'seq'))
- grad_conv_gain: float32 [1536], P(('dp', 'seq'))
Inputs may be any that keep to these rules, and one draw needn't show every extreme that they name: `lengths`: the first utterance of every group of 2 on one index of dp fills all 6144 frames.
All inputs are finite; a program needn't handle non-finite values.
Results may differ from a plain program's by a relative error of at most 0.0055.
Values may be sent and summed in bfloat16 or wider, within the bound.
No kernel may reach another device: no remote copies, remote signals or barrier semaphores. Data moves between devices by JAX's collectives and lax.ppermute only.
A program may use at most 128 MiB of HBM per device.

v0:
```python
import math

import jax
import jax.numpy as jnp
from jax import lax
from jax.sharding import PartitionSpec as P

EPSILON = 1e-05


def extended(cells, sides, width):
    for axis, dim in sides:
        count = lax.axis_size(axis)
        ends = count - 1
        head = lax.slice_in_dim(cells, 0, width, axis=dim)
        tail = lax.slice_in_dim(cells, cells.shape[dim] - width, cells.shape[dim], axis=dim)
        cells = jnp.concatenate(
            [
                lax.ppermute(tail, axis, [(i, (i + 1) % count) for i in range(ends)]),
                cells,
                lax.ppermute(head, axis, [((i + 1) % count, i) for i in range(ends)]),
            ],
            axis=dim,
        )
    return cells


def normalize(values):
    centered = values - jnp.mean(values, axis=-1, keepdims=True)
    inverse = lax.rsqrt(jnp.mean(centered * centered, axis=-1, keepdims=True) + EPSILON)
    return (centered * inverse, inverse)


def norm_backward(grad_hat, normed, inverse):
    return inverse * (
        grad_hat
        - jnp.mean(grad_hat, axis=-1, keepdims=True)
        - normed * jnp.mean(grad_hat * normed, axis=-1, keepdims=True)
    )


def inner_rows(left_side, right_side):
    return lax.dot_general(
        left_side, right_side, (((0,), (0,)), ((), ())), preferred_element_type=jnp.float32
    )


def outer_cols(left_side, right_side):
    return lax.dot_general(
        left_side, right_side, (((1,), (1,)), ((), ())), preferred_element_type=jnp.float32
    )


def depthwise(padded, kernel, length):
    result = padded[:, 0:length] * kernel[:, 0]
    for offset in range(1, kernel.shape[1]):
        result = result + padded[:, offset : offset + length] * kernel[:, offset]
    return result


def transposed(grad_padded, kernel, length):
    last_tap = kernel.shape[1] - 1
    result = grad_padded[:, last_tap : last_tap + length] * kernel[:, 0]
    for offset in range(1, kernel.shape[1]):
        result = (
            result
            + grad_padded[:, last_tap - offset : last_tap - offset + length] * kernel[:, offset]
        )
    return result


def kernel_terms(grad_float, padded, length, kernel_taps):
    return jnp.stack(
        [
            jnp.sum(grad_float * padded[:, offset : offset + length], axis=(0, 1))
            for offset in range(kernel_taps)
        ],
        axis=1,
    )


def local(hidden, cotangent, lengths, kernel, conv_gain, w_out):
    groups, frames, double_width = hidden.shape
    model_width = double_width // 2
    kernel_taps = kernel.shape[1]
    half_width = kernel_taps // 2
    seq_count = lax.axis_size("seq")
    row_total = groups * frames
    positions = lax.axis_index("seq") * frames + jnp.arange(frames, dtype=jnp.int32)
    valid_frames = (positions[None, :] < lengths[:, None]).astype(jnp.float32)
    valid_rows = valid_frames.reshape(row_total, 1)
    hidden_rows = hidden.reshape(row_total, double_width).astype(jnp.float32)
    linear = hidden_rows[:, :model_width]
    gate_open = jax.nn.sigmoid(hidden_rows[:, model_width:])
    glu_out = (linear * gate_open * valid_rows).astype(jnp.bfloat16)
    glu_block = glu_out.reshape(groups, frames, model_width)
    padded = extended(glu_block, (("seq", 1),), half_width).astype(jnp.float32)
    conv_out = depthwise(padded, kernel, frames)
    conv_hat, conv_inverse = normalize(conv_out.reshape(row_total, model_width))
    pre_act = conv_hat * conv_gain
    act_gate = jax.nn.sigmoid(pre_act)
    swished = (pre_act * act_gate).astype(jnp.bfloat16)
    grad_out = (cotangent * valid_frames.astype(jnp.bfloat16)[:, :, None]).reshape(
        row_total, model_width
    )
    grad_swish = outer_cols(grad_out, w_out)
    grad_pre = grad_swish * act_gate * (1.0 + pre_act * (1.0 - act_gate))
    term_conv = jnp.sum(grad_pre * conv_hat, axis=0)
    grad_conv = norm_backward(grad_pre * conv_gain, conv_hat, conv_inverse).astype(jnp.bfloat16)
    grad_block = grad_conv.reshape(groups, frames, model_width)
    grad_padded = extended(grad_block, (("seq", 1),), half_width).astype(jnp.float32)
    grad_glu = transposed(grad_padded, kernel, frames)
    term_kernel = kernel_terms(grad_block.astype(jnp.float32), padded, frames, kernel_taps)
    grad_glu = grad_glu.reshape(row_total, model_width) * valid_rows
    grad_local = jnp.concatenate(
        [grad_glu * gate_open, grad_glu * linear * gate_open * (1.0 - gate_open)], axis=1
    ).astype(jnp.bfloat16)
    count_all = groups * lax.axis_size("dp") * frames * seq_count
    factor = 1.0 / math.sqrt(count_all)
    term_out = inner_rows(swished, grad_out)
    sum_out, sum_kernel, sum_conv = (
        lax.psum_scatter(term_out, ("dp", "seq"), scatter_dimension=0, tiled=True),
        lax.psum_scatter(term_kernel, ("dp", "seq"), scatter_dimension=0, tiled=True),
        lax.psum_scatter(term_conv, ("dp", "seq"), scatter_dimension=0, tiled=True),
    )
    grad_hidden = grad_local.reshape(groups, frames, double_width)
    return (grad_hidden, sum_out * factor, sum_kernel * factor, sum_conv * factor)


def solution(mesh):
    in_specs = (P("dp", "seq", None), P("dp", "seq", None), P("dp"), P(), P(), P())
    out_specs = (
        P("dp", "seq", None),
        P(("dp", "seq"), None),
        P(("dp", "seq"), None),
        P(("dp", "seq")),
    )
    return jax.shard_map(local, mesh=mesh, in_specs=in_specs, out_specs=out_specs, check_vma=False)
```

profile of v0, /device:TPU:1, one launch (start us, length us, event | category | flops | bytes accessed | tf_op | source)
XLA Modules:
  0.0 648.2 jit_solution(78086565130806551)
XLA Ops:
  13.6 4.9 collective-permute-start
  25.0 11.6 %fusion.73 = (f32[2,192]{1,0:T(2,128)S(1)}, f32[2,192,1536]{2,1,0:T(8,128)}) fusion(f32[1536]{0:T(1024)S(1)} %get-tuple-element.75, f32[2,222,1536]{2,1,0:T(8,128)S(1)} %maximum_convert_fusion, f32[1536]{0:T(1024)S(1)} %get-tuple-element.76, f32[1536]{0:T(1024)S(1)} %get-tuple-element.47, f32[1536]{0:T(1024)S(1)} %copy-done.37, f32[1536]{0:T(1024)S(1)} %copy-done.39, ...), kind=kLoop, calls=%fused_computation.194 | loop fusion | flops 36568704 | bytes 75689472 | tf_op jit(solution)/shard_map/reduce_sum | solution.py:29
  41.6 5.4 multiply_reduce_fusion
  47.8 6.2 fusion.32
  54.1 5.4 convolution_bitcast_fusion
  59.4 358.4 %fusion = f32[16,1536]{1,0:T(8,128)S(1)} fusion(f32[1536,1536]{1,0:T(8,128)} %convolution_bitcast_fusion), kind=kCustom, calls=%all-reduce-scatter | all-reduce-scatter fusion | flops 3145729 | bytes 9535488
  419.2 3.2 collective-permute-start.2
  422.5 8.1 %collective-permute-start.3 = (bf16[2,15,1536]{2,1,0:T(8,128)(2,1)S(1)}, bf16[2,15,1536]{2,1,0:T(8,128)(2,1)S(1)}, u32[]{:S(2)}, u32[]{:S(2)}) collective-permute-start(bf16[2,15,1536]{2,1,0:T(8,128)(2,1)S(1)} %get-tuple-element.82), channel_id=1, source_target_pairs={{1,0},{2,1},{3,2},{4,3},{5,4},{6,5},{7,6},{8,7},{9,8},{10,9},{11,1... | collective-permute-start | bytes 276488 | tf_op jit(solution)/shard_map/ppermute | solution.py:21
  432.1 4.9 fusion.31
  442.0 63.0 %all-reduce.2 = f32[1536]{0:T(1024)S(1)} all-reduce(f32[1536]{0:T(1024)} %get-tuple-element.12), channel_id=4, replica_groups=mesh['dp'=4,'seq'=32] {'dp','seq'}, use_global_device_ids=true, to_apply=%region_38.0.clone | all-reduce | flops 1536 | bytes 12288
  505.0 4.8 collective-permute-start.32
  509.8 4.6 collective-permute-start.31
  517.0 4.6 collective-permute-start.29
  527.3 4.4 collective-permute-start.25
  532.4 3.1 collective-permute-start.24
  542.5 4.5 collective-permute-start.21
  552.0 9.0 %fusion.33 = f32[2,192,1536]{2,1,0:T(8,128)S(1)} fusion(f32[2,222,1536]{2,1,0:T(8,128)S(1)} %maximum_convert_fusion.1, f32[1536]{0:T(1024)S(1)} %copy-done.92, f32[1536]{0:T(1024)S(1)} %copy-done.94, f32[1536]{0:T(1024)S(1)} %get-tuple-element.47, f32[1536]{0:T(1024)S(1)} %copy-done.38, f32[1536]{0:T(1024)S(1)} %copy-done.40, f32[1536]{0:T(1024)S(1)} %copy-done.42, ...), kind=kLoop, calls=%fused_computation.66 | loop fusion | flops 35979264 | bytes 75687936 | tf_op jit(solution)/shard_map/add | solution.py:66
  562.8 3.2 collective-permute-start.17
  571.8 4.4 collective-permute-start.14
  586.1 3.7 collective-permute-start.9
  594.4 3.7 collective-permute-start.7
  598.1 3.7 collective-permute-start.6
  604.1 3.6 collective-permute-start.4
  610.7 30.0 %concatenate.20 = f32[524,1536]{1,0:T(8,128)S(1)} concatenate(f32[12,1536]{1,0:T(8,128)S(1)} %collective-permute-done.35, f32[16,1536]{1,0:T(8,128)S(1)} %collective-permute-done.34, f32[16,1536]{1,0:T(8,128)} %copy-done.8, f32[16,1536]{1,0:T(8,128)} %copy-done.9, f32[16,1536]{1,0:T(8,128)} %copy-done.10, f32[16,1536]{1,0:T(8,128)} %copy-done.11, f32[16,1536]{1,0:T(8,128)} %copy-done.12, ...), dimensions={0} | concatenate | bytes 6438912
  (356 shorter events, 73.2 us)
Async XLA Ops:
  7.2 600.6 %all-reduce.6.cloned.1.call-start = ((), (), s32[]{:S(2)}) async-start(), calls=%async_computation | async-start | bytes 393216
  417.9 99.1 %collective-permute-start.34 = (f32[16,1536]{1,0:T(8,128)S(1)}, f32[16,1536]{1,0:T(8,128)S(1)}, u32[]{:S(2)}, u32[]{:S(2)}) collective-permute-start(f32[16,1536]{1,0:T(8,128)S(1)} %fusion), channel_id=1, source_target_pairs={{0,31},{1,32},{2,33},{3,34},{4,35},{5,36},{6,37},{7,38},{8,39},{9,... | collective-permute-start | bytes 294920
  419.2 90.6 %collective-permute-start.2 = (bf16[2,15,1536]{2,1,0:T(8,128)(2,1)S(1)}, bf16[2,15,1536]{2,1,0:T(8,128)(2,1)S(1)}, u32[]{:S(2)}, u32[]{:S(2)}) collective-permute-start(bf16[2,15,1536]{2,1,0:T(8,128)(2,1)S(1)} %get-tuple-element.81), channel_id=1, source_target_pairs={{0,1},{1,2},{2,3},{3,4},{4,5},{5,6},{6,7},{7,8},{8,9},{9,10},{10,1... | collective-permute-start | bytes 276488 | tf_op jit(solution)/shard_map/ppermute | solution.py:19
  422.5 91.8 %collective-permute-start.3 = (bf16[2,15,1536]{2,1,0:T(8,128)(2,1)S(1)}, bf16[2,15,1536]{2,1,0:T(8,128)(2,1)S(1)}, u32[]{:S(2)}, u32[]{:S(2)}) collective-permute-start(bf16[2,15,1536]{2,1,0:T(8,128)(2,1)S(1)} %get-tuple-element.82), channel_id=1, source_target_pairs={{1,0},{2,1},{3,2},{4,3},{5,4},{6,5},{7,6},{8,7},{9,8},{10,9},{11,1... | collective-permute-start | bytes 276488 | tf_op jit(solution)/shard_map/ppermute | solution.py:21
  430.6 74.4 %collective-permute-start.35 = (f32[12,1536]{1,0:T(8,128)S(1)}, f32[12,1536]{1,0:T(8,128)S(1)}, u32[]{:S(2)}, u32[]{:S(2)}) collective-permute-start(f32[12,1536]{1,0:T(8,128)S(1)} %slice.526), channel_id=1, source_target_pairs={{0,32},{1,33},{2,34},{3,35},{4,36},{5,37},{6,38},{7,39},{8,40},{9,... | collective-permute-start | bytes 221192
  437.0 85.1 %collective-permute-start.33 = (f32[16,1536]{1,0:T(8,128)S(1)}, f32[16,1536]{1,0:T(8,128)S(1)}, u32[]{:S(2)}, u32[]{:S(2)}) collective-permute-start(f32[16,1536]{1,0:T(8,128)S(1)} %fusion), channel_id=1, source_target_pairs={{0,30},{1,31},{2,32},{3,33},{4,34},{5,35},{6,36},{7,37},{8,38},{9,... | collective-permute-start | bytes 294920
  505.0 18.7 %collective-permute-start.32 = (f32[16,1536]{1,0:T(8,128)S(1)}, f32[16,1536]{1,0:T(8,128)S(1)}, u32[]{:S(2)}, u32[]{:S(2)}) collective-permute-start(f32[16,1536]{1,0:T(8,128)S(1)} %fusion), channel_id=1, source_target_pairs={{0,29},{1,30},{2,31},{3,32},{4,33},{5,34},{6,35},{7,36},{8,37},{9,... | collective-permute-start | bytes 294920
  523.7 16.0 %collective-permute-start.27 = (f32[16,1536]{1,0:T(8,128)S(1)}, f32[16,1536]{1,0:T(8,128)S(1)}, u32[]{:S(2)}, u32[]{:S(2)}) collective-permute-start(f32[16,1536]{1,0:T(8,128)S(1)} %fusion), channel_id=1, source_target_pairs={{0,24},{1,25},{2,26},{3,27},{4,28},{5,29},{6,30},{7,31},{8,32},{9,... | collective-permute-start | bytes 294920
  525.6 16.9 %collective-permute-start.26 = (f32[16,1536]{1,0:T(8,128)S(1)}, f32[16,1536]{1,0:T(8,128)S(1)}, u32[]{:S(2)}, u32[]{:S(2)}) collective-permute-start(f32[16,1536]{1,0:T(8,128)S(1)} %fusion), channel_id=1, source_target_pairs={{0,23},{1,24},{2,25},{3,26},{4,27},{5,28},{6,29},{7,30},{8,31},{9,... | collective-permute-start | bytes 294920
  527.3 19.7 %collective-permute-start.25 = (f32[16,1536]{1,0:T(8,128)S(1)}, f32[16,1536]{1,0:T(8,128)S(1)}, u32[]{:S(2)}, u32[]{:S(2)}) collective-permute-start(f32[16,1536]{1,0:T(8,128)S(1)} %fusion), channel_id=1, source_target_pairs={{0,22},{1,23},{2,24},{3,25},{4,26},{5,27},{6,28},{7,29},{8,30},{9,... | collective-permute-start | bytes 294920
  532.4 16.8 %collective-permute-start.24 = (f32[16,1536]{1,0:T(8,128)S(1)}, f32[16,1536]{1,0:T(8,128)S(1)}, u32[]{:S(2)}, u32[]{:S(2)}) collective-permute-start(f32[16,1536]{1,0:T(8,128)S(1)} %fusion), channel_id=1, source_target_pairs={{0,21},{1,22},{2,23},{3,24},{4,25},{5,26},{6,27},{7,28},{8,29},{9,... | collective-permute-start | bytes 294920
  537.3 23.7 %collective-permute-start.23 = (f32[16,1536]{1,0:T(8,128)S(1)}, f32[16,1536]{1,0:T(8,128)S(1)}, u32[]{:S(2)}, u32[]{:S(2)}) collective-permute-start(f32[16,1536]{1,0:T(8,128)S(1)} %fusion), channel_id=1, source_target_pairs={{0,20},{1,21},{2,22},{3,23},{4,24},{5,25},{6,26},{7,27},{8,28},{9,... | collective-permute-start | bytes 294920
  539.8 23.0 %collective-permute-start.22 = (f32[16,1536]{1,0:T(8,128)S(1)}, f32[16,1536]{1,0:T(8,128)S(1)}, u32[]{:S(2)}, u32[]{:S(2)}) collective-permute-start(f32[16,1536]{1,0:T(8,128)S(1)} %fusion), channel_id=1, source_target_pairs={{0,19},{1,20},{2,21},{3,22},{4,23},{5,24},{6,25},{7,26},{8,27},{9,... | collective-permute-start | bytes 294920
  542.5 23.5 %collective-permute-start.21 = (f32[16,1536]{1,0:T(8,128)S(1)}, f32[16,1536]{1,0:T(8,128)S(1)}, u32[]{:S(2)}, u32[]{:S(2)}) collective-permute-start(f32[16,1536]{1,0:T(8,128)S(1)} %fusion), channel_id=1, source_target_pairs={{0,18},{1,19},{2,20},{3,21},{4,22},{5,23},{6,24},{7,25},{8,26},{9,... | collective-permute-start | bytes 294920
  547.0 21.8 %collective-permute-start.20 = (f32[16,1536]{1,0:T(8,128)S(1)}, f32[16,1536]{1,0:T(8,128)S(1)}, u32[]{:S(2)}, u32[]{:S(2)}) collective-permute-start(f32[16,1536]{1,0:T(8,128)S(1)} %fusion), channel_id=1, source_target_pairs={{0,17},{1,18},{2,19},{3,20},{4,21},{5,22},{6,23},{7,24},{8,25},{9,... | collective-permute-start | bytes 294920
  549.8 22.0 %collective-permute-start.19 = (f32[16,1536]{1,0:T(8,128)S(1)}, f32[16,1536]{1,0:T(8,128)S(1)}, u32[]{:S(2)}, u32[]{:S(2)}) collective-permute-start(f32[16,1536]{1,0:T(8,128)S(1)} %fusion), channel_id=1, source_target_pairs={{0,16},{1,17},{2,18},{3,19},{4,20},{5,21},{6,22},{7,23},{8,24},{9,... | collective-permute-start | bytes 294920
  561.1 16.7 %collective-permute-start.18 = (f32[16,1536]{1,0:T(8,128)S(1)}, f32[16,1536]{1,0:T(8,128)S(1)}, u32[]{:S(2)}, u32[]{:S(2)}) collective-permute-start(f32[16,1536]{1,0:T(8,128)S(1)} %fusion), channel_id=1, source_target_pairs={{0,15},{1,16},{2,17},{3,18},{4,19},{5,20},{6,21},{7,22},{8,23},{9,... | collective-permute-start | bytes 294920
  562.8 16.4 %collective-permute-start.17 = (f32[16,1536]{1,0:T(8,128)S(1)}, f32[16,1536]{1,0:T(8,128)S(1)}, u32[]{:S(2)}, u32[]{:S(2)}) collective-permute-start(f32[16,1536]{1,0:T(8,128)S(1)} %fusion), channel_id=1, source_target_pairs={{0,14},{1,15},{2,16},{3,17},{4,18},{5,19},{6,20},{7,21},{8,22},{9,... | collective-permute-start | bytes 294920
  566.1 15.9 %collective-permute-start.16 = (f32[16,1536]{1,0:T(8,128)S(1)}, f32[16,1536]{1,0:T(8,128)S(1)}, u32[]{:S(2)}, u32[]{:S(2)}) collective-permute-start(f32[16,1536]{1,0:T(8,128)S(1)} %fusion), channel_id=1, source_target_pairs={{0,13},{1,14},{2,15},{3,16},{4,17},{5,18},{6,19},{7,20},{8,21},{9,... | collective-permute-start | bytes 294920
  568.8 15.9 %collective-permute-start.15 = (f32[16,1536]{1,0:T(8,128)S(1)}, f32[16,1536]{1,0:T(8,128)S(1)}, u32[]{:S(2)}, u32[]{:S(2)}) collective-permute-start(f32[16,1536]{1,0:T(8,128)S(1)} %fusion), channel_id=1, source_target_pairs={{0,12},{1,13},{2,14},{3,15},{4,16},{5,17},{6,18},{7,19},{8,20},{9,... | collective-permute-start | bytes 294920
  582.0 16.1 %collective-permute-start.11 = (f32[16,1536]{1,0:T(8,128)S(1)}, f32[16,1536]{1,0:T(8,128)S(1)}, u32[]{:S(2)}, u32[]{:S(2)}) collective-permute-start(f32[16,1536]{1,0:T(8,128)S(1)} %fusion), channel_id=1, source_target_pairs={{0,8},{1,9},{2,10},{3,11},{4,12},{5,13},{6,14},{7,15},{8,16},{9,17... | collective-permute-start | bytes 294920
  584.8 17.0 %collective-permute-start.10 = (f32[16,1536]{1,0:T(8,128)S(1)}, f32[16,1536]{1,0:T(8,128)S(1)}, u32[]{:S(2)}, u32[]{:S(2)}) collective-permute-start(f32[16,1536]{1,0:T(8,128)S(1)} %fusion), channel_id=1, source_target_pairs={{0,7},{1,8},{2,9},{3,10},{4,11},{5,12},{6,13},{7,14},{8,15},{9,16}... | collective-permute-start | bytes 294920
  586.1 17.3 %collective-permute-start.9 = (f32[16,1536]{1,0:T(8,128)S(1)}, f32[16,1536]{1,0:T(8,128)S(1)}, u32[]{:S(2)}, u32[]{:S(2)}) collective-permute-start(f32[16,1536]{1,0:T(8,128)S(1)} %fusion), channel_id=1, source_target_pairs={{0,6},{1,7},{2,8},{3,9},{4,10},{5,11},{6,12},{7,13},{8,14},{9,15},... | collective-permute-start | bytes 294920
  591.5 17.8 %collective-permute-start.8 = (f32[16,1536]{1,0:T(8,128)S(1)}, f32[16,1536]{1,0:T(8,128)S(1)}, u32[]{:S(2)}, u32[]{:S(2)}) collective-permute-start(f32[16,1536]{1,0:T(8,128)S(1)} %fusion), channel_id=1, source_target_pairs={{0,5},{1,6},{2,7},{3,8},{4,9},{5,10},{6,11},{7,12},{8,13},{9,14},{... | collective-permute-start | bytes 294920
  (131 other events, 4372.7 us)
Sparse Core Ops, SparseCore 0:
  442.1 141.1 all-reduce.5
where the time goes:
time: 651 us; the launch traced here: 648 us
  blocking collectives  421 us (65%)
  starting transfers between devices  107 us (16%)
  other arithmetic  48.8 us (7%)
  local copies, waits for them, and re-layouts  41.8 us (6%)
  between operations  16.6 us (3%)
  matrix products  10.8 us (2%)
    unnamed x2, blocking collectives  421 us
    unnamed x33, starting transfers between devices  89.1 us
    unnamed x239, local copies, waits for them, and re-layouts  37.5 us
  transfers between devices with their start and end apart: 37, of which 1 were waited for; matrix products, arithmetic and copies ran while one was open for 4% of the time, Pallas kernels for 0%

commit v1 on v0

v1 whole, which is shorter than its diff:
```python
import math

import jax
import jax.numpy as jnp
from jax import lax
from jax.sharding import PartitionSpec as P

EPSILON = 1e-05
AXES = ("dp", "seq")


def inner_rows(left_side, right_side):
    return lax.dot_general(
        left_side, right_side, (((0,), (0,)), ((), ())), preferred_element_type=jnp.float32
    )


def outer_cols(left_side, right_side):
    return lax.dot_general(
        left_side, right_side, (((1,), (1,)), ((), ())), preferred_element_type=jnp.float32
    )


def extended(cells, width):
    count = lax.axis_size("seq")
    ends = count - 1
    frames = cells.shape[1]
    head = cells[:, :width]
    tail = cells[:, frames - width :]
    return jnp.concatenate(
        [
            lax.ppermute(tail, "seq", [(i, i + 1) for i in range(ends)]),
            cells,
            lax.ppermute(head, "seq", [(i + 1, i) for i in range(ends)]),
        ],
        axis=1,
    )


def normalize(values):
    centered = values - jnp.mean(values, axis=-1, keepdims=True)
    inverse = lax.rsqrt(jnp.mean(centered * centered, axis=-1, keepdims=True) + EPSILON)
    return (centered * inverse, inverse)


def norm_backward(grad_hat, normed, inverse):
    return inverse * (
        grad_hat
        - jnp.mean(grad_hat, axis=-1, keepdims=True)
        - normed * jnp.mean(grad_hat * normed, axis=-1, keepdims=True)
    )


def local(hidden, cotangent, lengths, kernel, conv_gain, w_out):
    groups, frames, double_width = hidden.shape
    width = double_width // 2
    half = width // 2
    taps = kernel.shape[1]
    reach = taps // 2
    seq_count = lax.axis_size("seq")
    devices = lax.axis_size("dp") * seq_count
    own = width // devices
    rows = groups * frames
    swap = [(i, i ^ 1) for i in range(seq_count)]
    core = lax.axis_index("seq") % 2

    positions = lax.axis_index("seq") * frames + jnp.arange(frames, dtype=jnp.int32)
    valid = (positions[None, :] < lengths[:, None]).astype(jnp.float32)
    valid_rows = valid.reshape(rows, 1)

    grad_out = (cotangent * valid.astype(jnp.bfloat16)[:, :, None]).reshape(rows, width)
    low, high = grad_out[:, :half], grad_out[:, half:]
    mine = jnp.where(core == 0, low, high)
    other = lax.ppermute(jnp.where(core == 0, high, low), "seq", swap)

    hidden_rows = hidden.reshape(rows, double_width).astype(jnp.float32)
    linear = hidden_rows[:, :width]
    gate_open = jax.nn.sigmoid(hidden_rows[:, width:])
    glu = (linear * gate_open * valid_rows).astype(jnp.bfloat16)
    padded = extended(glu.reshape(groups, frames, width), reach).astype(jnp.float32)
    conv_out = padded[:, 0:frames] * kernel[:, 0]
    for j in range(1, taps):
        conv_out = conv_out + padded[:, j : j + frames] * kernel[:, j]
    conv_hat, inverse = normalize(conv_out.reshape(rows, width))
    pre_act = conv_hat * conv_gain
    act_gate = jax.nn.sigmoid(pre_act)
    swished = (pre_act * act_gate).astype(jnp.bfloat16)

    far = lax.ppermute(swished, "seq", swap)
    term_out = inner_rows(
        jnp.concatenate([swished, far], axis=0), jnp.concatenate([mine, other], axis=0)
    )
    blocks = half // 128
    pieces = (
        term_out.astype(jnp.bfloat16)
        .reshape(devices, own, blocks, 128)
        .transpose(0, 2, 1, 3)
        .reshape(devices, blocks * own, 128)
    )
    got = lax.all_to_all(pieces, AXES, 0, 0, tiled=True)

    grad_swish = outer_cols(grad_out, w_out)
    grad_pre = grad_swish * act_gate * (1.0 + pre_act * (1.0 - act_gate))
    term_conv = jnp.sum(grad_pre * conv_hat, axis=0)
    grad_conv = norm_backward(grad_pre * conv_gain, conv_hat, inverse).astype(jnp.bfloat16)
    grad_block = grad_conv.reshape(groups, frames, width)
    grad_float = grad_block.astype(jnp.float32)
    terms = jnp.stack(
        [jnp.sum(grad_float * padded[:, j : j + frames], axis=(0, 1)) for j in range(taps)]
        + [term_conv]
    )
    small = terms.T.reshape(devices, own * (taps + 1) // 128, 128)
    got_small = lax.all_to_all(small, AXES, 0, 0, tiled=True)

    grad_padded = extended(grad_block, reach).astype(jnp.float32)
    last = taps - 1
    grad_glu = grad_padded[:, last : last + frames] * kernel[:, 0]
    for j in range(1, taps):
        grad_glu = grad_glu + grad_padded[:, last - j : last - j + frames] * kernel[:, j]
    grad_glu = grad_glu.reshape(rows, width) * valid_rows
    grad_hidden = jnp.concatenate(
        [grad_glu * gate_open, grad_glu * linear * gate_open * (1.0 - gate_open)], axis=1
    ).astype(jnp.bfloat16)

    factor = 1.0 / math.sqrt(groups * lax.axis_size("dp") * frames * seq_count)
    summed = jnp.sum(
        got.reshape(devices // 2, 2, blocks, own, 128).astype(jnp.float32), axis=0
    )
    grad_w = summed.transpose(2, 0, 1, 3).reshape(own, width) * factor
    summed_small = jnp.sum(got_small, axis=0).reshape(own, taps + 1) * factor
    return (
        grad_hidden.reshape(groups, frames, double_width),
        grad_w,
        summed_small[:, :taps],
        summed_small[:, taps],
    )


def solution(mesh):
    in_specs = (P("dp", "seq", None), P("dp", "seq", None), P("dp"), P(), P(), P())
    out_specs = (P("dp", "seq", None), P(AXES, None), P(AXES, None), P(AXES))
    return jax.shard_map(local, mesh=mesh, in_specs=in_specs, out_specs=out_specs, check_vma=False)
```

time: 651 us -> 138 us (0.21)
  blocking collectives: 421 us -> 0 us
  starting transfers between devices: 107 us -> 33.5 us
  local copies, waits for them, and re-layouts: 41.8 us -> 20.7 us
  waiting for transfers between devices: 1.57 us -> 19.6 us
  between operations: 16.6 us -> 1.67 us
    unnamed x2 -> x0, blocking collectives: 421 us -> none
    unnamed x33 -> x0, starting transfers between devices: 89.1 us -> none
    unnamed x239 -> x78, local copies, waits for them, and re-layouts: 37.5 us -> 2.65 us
    all_to_all x0 -> x2, starting transfers between devices: none -> 20.5 us  [the longest x1 10.3 us: local(): got_small = lax.all_to_all(small, AXES, 0, 0, tiled=True)]
    all_to_all x0 -> x2, waiting for transfers between devices: none -> 17.5 us  [the longest x1 17.5 us: local(): got = lax.all_to_all(pieces, AXES, 0, 0, tiled=True)]
    reshape x0 -> x3, local copies, waits for them, and re-layouts: none -> 9.95 us  [the longest x2 8.94 us: local(): pieces = term_out.astype(jnp.bfloat16).reshape(devices, own, blocks, 128)...]
    ppermute x4 -> x6, starting transfers between devices: 18.1 us -> 12.9 us  [the longest x2 8.84 us: extended(): lax.ppermute(tail, 'seq', [(i, i + 1) for i in range(ends)])]
  transfers between devices with their start and end apart: 37 -> 8, of which waited for: 1 -> 2; matrix products, arithmetic and copies ran while one was open for 4% -> 51% of each run, Pallas kernels for 0% -> 0%
where the time goes in v1:
time: 138 us; the launch traced here: 137 us
  other arithmetic  51.4 us (37%)
  starting transfers between devices  33.5 us (24%)
  local copies, waits for them, and re-layouts  20.7 us (15%)
  waiting for transfers between devices  19.6 us (14%)
  matrix products  10.5 us (8%)
  between operations  1.67 us (1%)
    all_to_all x1, waiting for transfers between devices, local(): got = lax.all_to_all(pieces, AXES, 0, 0, tiled=True)  17.5 us
    reduce_sum x1, other arithmetic, normalize(): centered = values - jnp.mean(values, axis=-1, keepdims=True)  11.5 us
    all_to_all x1, starting transfers between devices, local(): got_small = lax.all_to_all(small, AXES, 0, 0, tiled=True)  10.3 us
    all_to_all x1, starting transfers between devices, local(): got = lax.all_to_all(pieces, AXES, 0, 0, tiled=True)  10.2 us
    reduce_sum x2, other arithmetic, local(): jnp.sum(grad_float * padded[:, j:j + frames], axis=(0, 1))  9.52 us
    add x1, other arithmetic, local(): grad_glu + grad_padded[:, last - j:last - j + frames] * kernel[:, j]  9 us
    reshape x2, local copies, waits for them, and re-layouts, local(): pieces = term_out.astype(jnp.bfloat16).reshape(devices, own, blocks, 128)...  8.94 us
    ppermute x2, starting transfers between devices, extended(): lax.ppermute(tail, 'seq', [(i, i + 1) for i in range(ends)])  8.84 us
  transfers between devices with their start and end apart: 8, of which 2 were waited for; matrix products, arithmetic and copies ran while one was open for 51% of the time, Pallas kernels for 0%

profile of v1, /device:TPU:1, one launch (start us, length us, event | category | flops | bytes accessed | tf_op | source)
XLA Modules:
  0.0 137.2 jit_solution(6907121763110296907)
XLA Ops:
  1.5 2.2 %bitcast_convert_fusion = f32[384,3072]{1,0:T(8,128)S(1)} fusion(bf16[2,192,3072]{2,1,0:T(8,128)(2,1)} %param.6), kind=kLoop, calls=%fused_computation.138 | loop fusion | flops 1179648 | bytes 7077888 | tf_op jit(solution)/shard_map/convert_element_type | solution.py:76
  6.9 4.9 %collective-permute-start = (bf16[2,15,1536]{2,1,0:T(8,128)(2,1)S(1)}, bf16[2,15,1536]{2,1,0:T(8,128)(2,1)S(1)}, u32[]{:S(2)}, u32[]{:S(2)}) collective-permute-start(bf16[2,15,1536]{2,1,0:T(8,128)(2,1)S(1)} %get-tuple-element.79), channel_id=1, source_target_pairs={{0,1},{1,2},{2,3},{3,4},{4,5},{5,6},{6,7},{7,8},{8,9},{9,10},{10,1... | collective-permute-start | bytes 276488 | tf_op jit(solution)/shard_map/ppermute | solution.py:32
  11.8 1.9 %collective-permute-start.1 = (bf16[2,15,1536]{2,1,0:T(8,128)(2,1)S(1)}, bf16[2,15,1536]{2,1,0:T(8,128)(2,1)S(1)}, u32[]{:S(2)}, u32[]{:S(2)}) collective-permute-start(bf16[2,15,1536]{2,1,0:T(8,128)(2,1)S(1)} %get-tuple-element.80), channel_id=1, source_target_pairs={{1,0},{2,1},{3,2},{4,3},{5,4},{6,5},{7,6},{8,7},{9,8},{10,9},{11,1... | collective-permute-start | bytes 276488 | tf_op jit(solution)/shard_map/ppermute | solution.py:34
  15.7 2.0 %collective-permute-done.1 = bf16[2,15,1536]{2,1,0:T(8,128)(2,1)S(1)} collective-permute-done((bf16[2,15,1536]{2,1,0:T(8,128)(2,1)S(1)}, bf16[2,15,1536]{2,1,0:T(8,128)(2,1)S(1)}, u32[]{:S(2)}, u32[]{:S(2)}) %collective-permute-start.1) | collective-permute-done | bytes 92192 | tf_op jit(solution)/shard_map/ppermute | solution.py:34
  18.1 11.5 %fusion.75 = (f32[2,192]{1,0:T(2,128)S(1)}, f32[2,192,1536]{2,1,0:T(8,128)}) fusion(f32[1536]{0:T(1024)S(1)} %get-tuple-element.67, f32[2,222,1536]{2,1,0:T(8,128)S(1)} %maximum_convert_fusion, f32[1536]{0:T(1024)S(1)} %get-tuple-element.68, f32[1536]{0:T(1024)S(1)} %get-tuple-element.39, f32[1536]{0:T(1024)S(1)} %get-tuple-element.40, ...), kind=kLoop, calls=%fused_computation.200 | loop fusion | flops 36568704 | bytes 75689472 | tf_op jit(solution)/shard_map/reduce_sum | solution.py:41
  29.9 2.0 %multiply_reduce_fusion.2 = f32[2,192]{1,0:T(2,128)S(1)} fusion(f32[2,192,1536]{2,1,0:T(8,128)} %get-tuple-element.72, f32[2,192]{1,0:T(2,128)S(1)} %broadcast_multiply_fusion.4), kind=kLoop, calls=%fused_computation.146 | loop fusion | flops 1769088 | bytes 2362368 | tf_op jit(solution)/shard_map/reduce_sum | solution.py:42
  32.0 3.6 %multiply_convert_fusion = (bf16[384,1536]{1,0:T(8,128)(2,1)}, f32[384,1536]{1,0:T(8,128)S(1)}) fusion(f32[1536]{0:T(1024)S(1)} %copy-done.35, f32[384]{0:T(512)S(1)} %rsqrt.12, f32[384]{0:T(512)S(1)} %div.23, f32[2,192,1536]{2,1,0:T(8,128)} %get-tuple-element.72), kind=kLoop, calls=%fused_computation.140 | loop fusion | flops 4718592 | bytes 5907456 | tf_op jit(solution)/shard_map/convert_element_type | solution.py:87
  35.7 5.2 %multiply_reduce_fusion = (f32[1536]{0:T(1024)S(1)}, f32[384]{0:T(512)S(1)}, f32[384]{0:T(512)S(1)}, f32[384,1536]{1,0:T(8,128)S(1)}) fusion(f32[384,1536]{1,0:T(8,128)S(1)} %get-tuple-element.70, f32[1536]{0:T(1024)S(1)} %copy-done.35, bf16[384,1536]{1,0:T(8,128)(2,1)S(1)} %bitcast.41, bf16[1536,1536]{1,0:T(8,128)(2,1)} %param.11), kind=kOutput, calls=%fused_computation.139 | convolution fusion | flops 1820784384 | bytes 10632192 | tf_op jit(solution)/shard_map/dot_general | solution.py:19
  41.4 5.6 %fusion.31 = (f32[1536]{0:T(1024)S(1)}, f32[1536]{0:T(1024)S(1)}, f32[1536]{0:T(1024)S(1)}, f32[1536]{0:T(1024)S(1)}, f32[1536]{0:T(1024)S(1)}, /*index=5*/f32[1...) fusion(bf16[2,192,1536]{2,1,0:T(8,128)(2,1)S(1)} %bitcast.29, ...), kind=kLoop, calls=%fused_computation.65 | loop fusion | flops 21795840 | bytes 43757568 | tf_op jit(solution)/shard_map/reduce_sum | solution.py:109
  47.2 3.9 %collective-permute-start.2 = (bf16[2,15,1536]{2,1,0:T(8,128)(2,1)S(1)}, bf16[2,15,1536]{2,1,0:T(8,128)(2,1)S(1)}, u32[]{:S(2)}, u32[]{:S(2)}) collective-permute-start(bf16[2,15,1536]{2,1,0:T(8,128)(2,1)S(1)} %get-tuple-element.77), channel_id=1, source_target_pairs={{0,1},{1,2},{2,3},{3,4},{4,5},{5,6},{6,7},{7,8},{8,9},{9,10},{10,1... | collective-permute-start | bytes 276488 | tf_op jit(solution)/shard_map/ppermute | solution.py:32
  51.1 2.1 %collective-permute-start.3 = (bf16[2,15,1536]{2,1,0:T(8,128)(2,1)S(1)}, bf16[2,15,1536]{2,1,0:T(8,128)(2,1)S(1)}, u32[]{:S(2)}, u32[]{:S(2)}) collective-permute-start(bf16[2,15,1536]{2,1,0:T(8,128)(2,1)S(1)} %get-tuple-element.78), channel_id=1, source_target_pairs={{1,0},{2,1},{3,2},{4,3},{5,4},{6,5},{7,6},{8,7},{9,8},{10,9},{11,1... | collective-permute-start | bytes 276488 | tf_op jit(solution)/shard_map/ppermute | solution.py:34
  53.2 4.0 %fusion.30 = (f32[1536]{0:T(1024)S(1)}, f32[1536]{0:T(1024)S(1)}, f32[1536]{0:T(1024)S(1)}, f32[1536]{0:T(1024)S(1)}, f32[1536]{0:T(1024)S(1)}, /*index=5*/f32[1...) fusion(bf16[2,192,1536]{2,1,0:T(8,128)(2,1)S(1)} %bitcast.31, ...), kind=kLoop, calls=%fused_computation.64 | loop fusion | flops 15905280 | bytes 31930368 | tf_op jit(solution)/shard_map/reduce_sum | solution.py:109
  59.2 10.3 %all-to-all-start.1 = ((f32[128,3,128]{2,1,0:T(4,128)}), f32[128,3,128]{2,1,0:T(4,128)S(1)}, u32[]{:S(2)}, u32[]{:S(2)}) async-start(f32[128,3,128]{2,1,0:T(4,128)} %reshape.179), calls=%async_computation.1 | async-start | bytes 524288 | tf_op jit(solution)/shard_map/all_to_all | solution.py:113
  69.6 1.7 %maximum_convert_fusion.1 = f32[2,222,1536]{2,1,0:T(8,128)S(1)} fusion(bf16[2,15,1536]{2,1,0:T(8,128)(2,1)S(1)} %collective-permute-done.3, bf16[2,192,1536]{2,1,0:T(8,128)(2,1)} %bitcast.32, bf16[2,15,1536]{2,1,0:T(8,128)(2,1)S(1)} %collective-permute-done.2), kind=kLoop, calls=%fused_computation.151 | loop fusion | flops 4091904 | bytes 4091904 | tf_op jit(solution)/shard_map/convert_element_type | solution.py:115
  71.3 5.2 %convolution_convert_fusion = bf16[1536,768]{1,0:T(8,128)(2,1)} fusion(bf16[384,1536]{1,0:T(8,128)(2,1)} %collective-permute-done.4, bf16[384,1536]{1,0:T(8,128)(2,1)} %get-tuple-element.69, bf16[384,768]{1,0:T(8,128)(2,1)} %collective-permute-done.5, bf16[384,768]{1,0:T(8,128)(2,1)S(1)} %copy-done.7), kind=kOutput, calls=%fused_computation.32 | convolution fusion | flops 1820196864 | bytes 5898240 | tf_op jit(solution)/shard_map/dot_general | solution.py:13
  76.6 6.0 %reshape.177 = bf16[128,12,6,128]{3,2,1,0:T(8,128)(2,1)} reshape(bf16[1536,768]{1,0:T(8,128)(2,1)} %convolution_convert_fusion) | data formatting | bytes 4718592 | tf_op jit(solution)/shard_map/reshape | solution.py:96
  82.5 2.8 %copy.13 = bf16[128,6,12,128]{3,0,2,1:T(8,128)(2,1)S(1)} copy(bf16[128,6,12,128]{3,1,2,0:T(8,128)(2,1)} %bitcast.33) | data formatting | bytes 4718592 | tf_op jit(solution)/shard_map/transpose | solution.py:97
  85.3 3.0 %copy.14 = bf16[128,72,128]{2,1,0:T(8,128)(2,1)} copy(bf16[128,72,128]{2,0,1:T(8,128)(2,1)S(1)} %bitcast.35) | data formatting | bytes 4718592 | tf_op jit(solution)/shard_map/reshape | solution.py:98
  88.4 10.2 %all-to-all-start = ((bf16[128,72,128]{2,1,0:T(8,128)(2,1)}), bf16[128,72,128]{2,1,0:T(8,128)(2,1)}, u32[]{:S(2)}, u32[]{:S(2)}) async-start(bf16[128,72,128]{2,1,0:T(8,128)(2,1)} %copy.14), calls=%async_computation | async-start | bytes 4718592 | tf_op jit(solution)/shard_map/all_to_all | solution.py:100
  98.8 9.0 %fusion.32 = f32[2,192,1536]{2,1,0:T(8,128)S(1)} fusion(f32[2,222,1536]{2,1,0:T(8,128)S(1)} %maximum_convert_fusion.1, f32[1536]{0:T(1024)S(1)} %copy-done.32, f32[1536]{0:T(1024)S(1)} %copy-done.34, f32[1536]{0:T(1024)S(1)} %get-tuple-element.39, f32[1536]{0:T(1024)S(1)} %get-tuple-element.40, f32[1536]{0:T(1024)S(1)} %get-tuple-element.41, ...), kind=kLoop, calls=%fused_computation.67 | loop fusion | flops 35979264 | bytes 75687936 | tf_op jit(solution)/shard_map/add | solution.py:119
  107.8 3.6 %multiply_convert_fusion.2 = (bf16[384,1536]{1,0:T(8,128)(2,1)S(1)}, bf16[384,1536]{1,0:T(8,128)(2,1)S(1)}) fusion(f32[2,192,1536]{2,1,0:T(8,128)S(1)} %fusion.32, f32[384]{0:T(512)S(1)} %copy-done.38, f32[384,3072]{1,0:T(8,128)} %copy-done), kind=kLoop, calls=%fused_computation.142 | loop fusion | flops 6488064 | bytes 9438720 | tf_op jit(solution)/shard_map/convert.6
  114.0 17.5 %all-to-all-done = bf16[128,72,128]{2,1,0:T(8,128)(2,1)} async-done(((bf16[128,72,128]{2,1,0:T(8,128)(2,1)}), bf16[128,72,128]{2,1,0:T(8,128)(2,1)}, u32[]{:S(2)}, u32[]{:S(2)}) %all-to-all-start) | async-done | bytes 2359328 | tf_op jit(solution)/shard_map/all_to_all | solution.py:100
  131.5 2.3 %copy.15 = bf16[128,72,128]{2,0,1:T(8,128)(2,1)S(1)} copy(bf16[128,72,128]{2,1,0:T(8,128)(2,1)} %all-to-all-done) | data formatting | bytes 4718592 | tf_op jit(solution)/shard_map/all_to_all | solution.py:100
  133.8 2.7 %convert_reduce_fusion = f32[2,6,12,128]{3,0,2,1:T(2,128)S(1)} fusion(bf16[64,2,6,12,128]{4,1,0,3,2:T(2,128)(2,1)S(1)} %bitcast.34), kind=kLoop, calls=%fused_computation.31 | loop fusion | flops 2340864 | bytes 2433024 | tf_op jit(solution)/shard_map/reduce_sum | solution.py:126
  (146 shorter events, 12.2 us)
Async XLA Ops:
  6.9 8.8 %collective-permute-start = (bf16[2,15,1536]{2,1,0:T(8,128)(2,1)S(1)}, bf16[2,15,1536]{2,1,0:T(8,128)(2,1)S(1)}, u32[]{:S(2)}, u32[]{:S(2)}) collective-permute-start(bf16[2,15,1536]{2,1,0:T(8,128)(2,1)S(1)} %get-tuple-element.79), channel_id=1, source_target_pairs={{0,1},{1,2},{2,3},{3,4},{4,5},{5,6},{6,7},{7,8},{8,9},{9,10},{10,1... | collective-permute-start | bytes 276488 | tf_op jit(solution)/shard_map/ppermute | solution.py:32
  11.8 5.9 %collective-permute-start.1 = (bf16[2,15,1536]{2,1,0:T(8,128)(2,1)S(1)}, bf16[2,15,1536]{2,1,0:T(8,128)(2,1)S(1)}, u32[]{:S(2)}, u32[]{:S(2)}) collective-permute-start(bf16[2,15,1536]{2,1,0:T(8,128)(2,1)S(1)} %get-tuple-element.80), channel_id=1, source_target_pairs={{1,0},{2,1},{3,2},{4,3},{5,4},{6,5},{7,6},{8,7},{9,8},{10,9},{11,1... | collective-permute-start | bytes 276488 | tf_op jit(solution)/shard_map/ppermute | solution.py:34
  15.0 56.3 %collective-permute-start.5 = (bf16[384,768]{1,0:T(8,128)(2,1)}, bf16[384,768]{1,0:T(8,128)(2,1)}, u32[]{:S(2)}, u32[]{:S(2)}) collective-permute-start(bf16[384,768]{1,0:T(8,128)(2,1)} %get-tuple-element.76), channel_id=1, source_target_pairs={{0,1},{1,0},{2,3},{3,2},{4,5},{5,4},{6,7},{7,6},{8,9},{9,8},{10,11... | collective-permute-start | bytes 1769480 | tf_op jit(solution)/shard_map/ppermute | solution.py:74
  15.3 14.3 %copy-start.9 = (f32[1536]{0:T(1024)}, f32[1536]{0:T(1024)S(1)}, u32[]{:S(2)}) copy-start(f32[1536]{0:T(1024)S(1)} %get-tuple-element.56) | copy-start | bytes 18436
  15.6 14.1 %copy-start.11 = (f32[1536]{0:T(1024)}, f32[1536]{0:T(1024)S(1)}, u32[]{:S(2)}) copy-start(f32[1536]{0:T(1024)S(1)} %get-tuple-element.57) | copy-start | bytes 18436
  15.6 14.1 %copy-start.13 = (f32[1536]{0:T(1024)}, f32[1536]{0:T(1024)S(1)}, u32[]{:S(2)}) copy-start(f32[1536]{0:T(1024)S(1)} %get-tuple-element.58) | copy-start | bytes 18436
  15.6 14.1 %copy-start.15 = (f32[1536]{0:T(1024)}, f32[1536]{0:T(1024)S(1)}, u32[]{:S(2)}) copy-start(f32[1536]{0:T(1024)S(1)} %get-tuple-element.59) | copy-start | bytes 18436
  15.6 14.1 %copy-start.17 = (f32[1536]{0:T(1024)}, f32[1536]{0:T(1024)S(1)}, u32[]{:S(2)}) copy-start(f32[1536]{0:T(1024)S(1)} %get-tuple-element.60) | copy-start | bytes 18436
  15.6 14.1 %copy-start.19 = (f32[1536]{0:T(1024)}, f32[1536]{0:T(1024)S(1)}, u32[]{:S(2)}) copy-start(f32[1536]{0:T(1024)S(1)} %get-tuple-element.61) | copy-start | bytes 18436
  15.6 14.1 %copy-start.21 = (f32[1536]{0:T(1024)}, f32[1536]{0:T(1024)S(1)}, u32[]{:S(2)}) copy-start(f32[1536]{0:T(1024)S(1)} %get-tuple-element.62) | copy-start | bytes 18436
  15.6 14.1 %copy-start.23 = (f32[1536]{0:T(1024)}, f32[1536]{0:T(1024)S(1)}, u32[]{:S(2)}) copy-start(f32[1536]{0:T(1024)S(1)} %get-tuple-element.63) | copy-start | bytes 18436
  15.6 14.1 %copy-start.25 = (f32[1536]{0:T(1024)}, f32[1536]{0:T(1024)S(1)}, u32[]{:S(2)}) copy-start(f32[1536]{0:T(1024)S(1)} %get-tuple-element.64) | copy-start | bytes 18436
  15.6 14.1 %copy-start.27 = (f32[1536]{0:T(1024)}, f32[1536]{0:T(1024)S(1)}, u32[]{:S(2)}) copy-start(f32[1536]{0:T(1024)S(1)} %get-tuple-element.65) | copy-start | bytes 18436
  15.6 14.1 %copy-start.29 = (f32[1536]{0:T(1024)}, f32[1536]{0:T(1024)S(1)}, u32[]{:S(2)}) copy-start(f32[1536]{0:T(1024)S(1)} %get-tuple-element.66) | copy-start | bytes 18436
  15.7 14.1 %copy-start.31 = (f32[1536]{0:T(1024)}, f32[1536]{0:T(1024)S(1)}, u32[]{:S(2)}) copy-start(f32[1536]{0:T(1024)S(1)} %get-tuple-element.67) | copy-start | bytes 18436
  15.7 14.1 %copy-start.33 = (f32[1536]{0:T(1024)}, f32[1536]{0:T(1024)S(1)}, u32[]{:S(2)}) copy-start(f32[1536]{0:T(1024)S(1)} %get-tuple-element.68) | copy-start | bytes 18436
  41.4 11.7 %copy-start.1 = (bf16[384,1536]{1,0:T(8,128)(2,1)}, bf16[384,1536]{1,0:T(8,128)(2,1)S(1)}, u32[]{:S(2)}) copy-start(bf16[384,1536]{1,0:T(8,128)(2,1)S(1)} %multiply_convert_fusion.3) | copy-start | bytes 3538948
  47.1 24.3 %collective-permute-start.4 = (bf16[384,1536]{1,0:T(8,128)(2,1)}, bf16[384,1536]{1,0:T(8,128)(2,1)}, u32[]{:S(2)}, u32[]{:S(2)}) collective-permute-start(bf16[384,1536]{1,0:T(8,128)(2,1)} %get-tuple-element.69), channel_id=1, source_target_pairs={{0,1},{1,0},{2,3},{3,2},{4,5},{5,4},{6,7},{7,6},{8,9},{9,8},{10,11... | collective-permute-start | bytes 3538952 | tf_op jit(solution)/shard_map/ppermute | solution.py:89
  47.2 22.4 %collective-permute-start.2 = (bf16[2,15,1536]{2,1,0:T(8,128)(2,1)S(1)}, bf16[2,15,1536]{2,1,0:T(8,128)(2,1)S(1)}, u32[]{:S(2)}, u32[]{:S(2)}) collective-permute-start(bf16[2,15,1536]{2,1,0:T(8,128)(2,1)S(1)} %get-tuple-element.77), channel_id=1, source_target_pairs={{0,1},{1,2},{2,3},{3,4},{4,5},{5,6},{6,7},{7,8},{8,9},{9,10},{10,1... | collective-permute-start | bytes 276488 | tf_op jit(solution)/shard_map/ppermute | solution.py:32
  51.1 18.5 %collective-permute-start.3 = (bf16[2,15,1536]{2,1,0:T(8,128)(2,1)S(1)}, bf16[2,15,1536]{2,1,0:T(8,128)(2,1)S(1)}, u32[]{:S(2)}, u32[]{:S(2)}) collective-permute-start(bf16[2,15,1536]{2,1,0:T(8,128)(2,1)S(1)} %get-tuple-element.78), channel_id=1, source_target_pairs={{1,0},{2,1},{3,2},{4,3},{5,4},{6,5},{7,6},{8,7},{9,8},{10,9},{11,1... | collective-permute-start | bytes 276488 | tf_op jit(solution)/shard_map/ppermute | solution.py:34
  59.2 29.2 %all-to-all-start.1 = ((f32[128,3,128]{2,1,0:T(4,128)}), f32[128,3,128]{2,1,0:T(4,128)S(1)}, u32[]{:S(2)}, u32[]{:S(2)}) async-start(f32[128,3,128]{2,1,0:T(4,128)} %reshape.179), calls=%async_computation.1 | async-start | bytes 524288 | tf_op jit(solution)/shard_map/all_to_all | solution.py:113
  88.3 10.3 %copy-start.18 = (f32[1536]{0:T(1024)S(1)}, f32[1536]{0:T(1024)}, u32[]{:S(2)}) copy-start(f32[1536]{0:T(1024)} %copy-done.17) | copy-start | bytes 18436
  88.4 43.1 %all-to-all-start = ((bf16[128,72,128]{2,1,0:T(8,128)(2,1)}), bf16[128,72,128]{2,1,0:T(8,128)(2,1)}, u32[]{:S(2)}, u32[]{:S(2)}) async-start(bf16[128,72,128]{2,1,0:T(8,128)(2,1)} %copy.14), calls=%async_computation | async-start | bytes 4718592 | tf_op jit(solution)/shard_map/all_to_all | solution.py:100
  113.3 20.5 %copy-start.36 = (f32[12,32]{1,0:T(8,128)}, f32[12,32]{1,0:T(8,128)S(1)}, u32[]{:S(2)}) copy-start(f32[12,32]{1,0:T(8,128)S(1)} %mul.895) | copy-start | bytes 4612
  (23 other events, 163.1 us)

commit v2 on v1

v2 whole, which is shorter than its diff:
```python
import functools
import math

import jax
import jax.numpy as jnp
from jax import lax
from jax.experimental import pallas as pl
from jax.experimental.pallas import tpu as pltpu
from jax.sharding import PartitionSpec as P

EPSILON = 1e-05
AXES = ("dp", "seq")
LANES = 128
PAD = 16
F32, BF16 = jnp.float32, jnp.bfloat16


def sigmoid(x):
    return 0.5 * jnp.tanh(0.5 * x) + 0.5


def depthwise(slab, weight, start, rows, order):
    total = None
    for j, row in enumerate(order):
        term = slab[pl.ds(start + 1 + j, rows), :] * weight[row]
        total = term if total is None else total + term
    return total


def forward_kernel(limit, hidden, left, right, weights, gain, slab, hat, inverse, swished, conv):
    taps = weights.shape[0] - 1
    frames, double = hidden.shape[1:]
    width = double // 2
    blocks = width // LANES
    u = pl.program_id(0)
    rows = lax.broadcasted_iota(jnp.int32, (frames, LANES), 0)
    keep = rows < limit[u]

    def channel(cb, _):
        here = pl.ds(pl.multiple_of(cb * LANES, LANES), LANES)
        there = pl.ds(pl.multiple_of(width + cb * LANES, LANES), LANES)
        linear = hidden[0, :, here].astype(F32)
        gate = sigmoid(hidden[0, :, there].astype(F32))
        glu = jnp.where(keep, linear * gate, 0.0).astype(BF16).astype(F32)
        block = slab.at[0, cb]
        block[0:PAD, :] = left[0, :, here].astype(F32)
        block[PAD : PAD + frames, :] = glu
        block[PAD + frames :, :] = right[0, :, here].astype(F32)
        weight = [weights[j : j + 1, here] for j in range(taps)]
        for start in range(0, frames, 64):
            conv[start : start + 64, here] = depthwise(block, weight, start, 64, range(taps))
        return 0

    lax.fori_loop(0, blocks, channel, 0)

    def normalize(i, _):
        at = pl.ds(pl.multiple_of(i * 16, 16), 16)
        values = conv[at, :]
        centered = values - jnp.sum(values, axis=-1, keepdims=True) * (1.0 / width)
        spread = jnp.sum(centered * centered, axis=-1, keepdims=True) * (1.0 / width)
        inv = lax.rsqrt(spread + EPSILON)
        normed = centered * inv
        hat[0, at, :] = normed
        inverse[0, at, :] = jnp.broadcast_to(inv, (16, LANES))
        pre = normed * gain[...]
        out = pre * sigmoid(pre)
        row = i * 16 + lax.broadcasted_iota(jnp.int32, (16, width), 0)
        swished[0, at, :] = jnp.where(row < limit[u], out, 0.0).astype(BF16)
        return 0

    lax.fori_loop(0, frames // 16, normalize, 0)


def forward(limit, hidden, left, right, weights, gain):
    groups, frames, double = hidden.shape
    width = double // 2
    blocks = width // LANES
    length = frames + 2 * PAD
    per = lambda *shape: pl.BlockSpec((1, *shape), lambda u, *_: (u,) + (0,) * len(shape))
    whole = lambda *shape: pl.BlockSpec(shape, lambda u, *_: (0,) * len(shape))
    return pl.pallas_call(
        forward_kernel,
        grid_spec=pltpu.PrefetchScalarGridSpec(
            num_scalar_prefetch=1,
            grid=(groups,),
            in_specs=[
                per(frames, double),
                per(PAD, width),
                per(PAD, width),
                whole(*weights.shape),
                whole(1, width),
            ],
            out_specs=[
                per(blocks, length, LANES),
                per(frames, width),
                per(frames, LANES),
                per(frames, width),
            ],
            scratch_shapes=[pltpu.VMEM((frames, width), F32)],
        ),
        out_shape=[
            jax.ShapeDtypeStruct((groups, blocks, length, LANES), F32),
            jax.ShapeDtypeStruct((groups, frames, width), F32),
            jax.ShapeDtypeStruct((groups, frames, LANES), F32),
            jax.ShapeDtypeStruct((groups, frames, width), BF16),
        ],
        name="forward",
        cost_estimate=pl.CostEstimate(flops=2 * 31 * 600000, bytes_accessed=9 << 20, transcendentals=1200000),
        compiler_params=pltpu.CompilerParams(vmem_limit_bytes=24 << 20),
    )(limit, hidden, left, right, weights, gain)


def product_kernel(core, near, far, mine, other, out, scratch):
    contract = (((0,), (0,)), ((), ()))
    result = lax.dot_general(near[...], mine[...], contract, preferred_element_type=F32)
    result = result + lax.dot_general(far[...], other[...], contract, preferred_element_type=F32)
    pairs = scratch.shape[0]
    first = lax.broadcasted_iota(jnp.int32, (pairs, 8, LANES), 1) < 4
    pick = lambda a, b: jnp.where(first, a, b)
    roll = lambda a: pltpu.roll(a, 4, 1)

    def parts(k):
        cut = result[:, k * LANES : (k + 1) * LANES].reshape(pairs, 3, 8, LANES)
        return cut[:, 0], cut[:, 1], cut[:, 2]

    for q in range(result.shape[1] // LANES // 2):
        a, b, c = parts(2 * q)
        d, e, f = parts(2 * q + 1)
        rb, rc, rd = roll(b), roll(c), roll(d)
        even = (a, pick(b, rd), pick(rd, roll(e)))
        odd = (pick(rb, rc), pick(rc, e), f)
        for side, tiles in enumerate((even, odd)):
            for i, tile in enumerate(tiles):
                scratch[:, side, 24 * q + 8 * i : 24 * q + 8 * i + 8, :] = tile
    out[...] = scratch[...].astype(BF16)


def product(core, near, far, cotangent, other, devices):
    rows, width = near.shape
    half = width // 2
    own = width // devices
    step = 32 * own
    pairs = 16
    deep = own * half // LANES
    return pl.pallas_call(
        product_kernel,
        grid_spec=pltpu.PrefetchScalarGridSpec(
            num_scalar_prefetch=1,
            grid=(width // step,),
            in_specs=[
                pl.BlockSpec((rows, step), lambda i, c: (0, i)),
                pl.BlockSpec((rows, step), lambda i, c: (0, i)),
                pl.BlockSpec((rows, half), lambda i, c: (0, c[0])),
                pl.BlockSpec((rows, half), lambda i, c: (0, 0)),
            ],
            out_specs=pl.BlockSpec((pairs, 2, deep, LANES), lambda i, c: (i, 0, 0, 0)),
            scratch_shapes=[pltpu.VMEM((pairs, 2, deep, LANES), F32)],
        ),
        out_shape=jax.ShapeDtypeStruct((devices // 2, 2, deep, LANES), BF16),
        name="product",
        cost_estimate=pl.CostEstimate(flops=4 * rows * width * half, bytes_accessed=6 << 20, transcendentals=0),
        compiler_params=pltpu.CompilerParams(vmem_limit_bytes=20 << 20),
    )(core, near, far, cotangent, other)


def backward_kernel(limit, cotangent, w_out, hat, inverse, gain, grad_conv, term, grad, sums):
    frames, width = hat.shape[1:]
    u = pl.program_id(0)
    grad[...] = lax.dot_general(
        cotangent[0], w_out[...], (((1,), (1,)), ((), ())), preferred_element_type=F32
    )

    @pl.when(u == 0)
    def _():
        sums[...] = jnp.zeros_like(sums)

    def norm(i, _):
        at = pl.ds(pl.multiple_of(i * 16, 16), 16)
        row = i * 16 + lax.broadcasted_iota(jnp.int32, (16, width), 0)
        swish = jnp.where(row < limit[u], grad[at, :], 0.0)
        normed = hat[0, at, :]
        pre = normed * gain[...]
        gate = sigmoid(pre)
        grad_pre = swish * gate * (1.0 + pre * (1.0 - gate))
        product = grad_pre * normed
        sums[...] += product[0:8] + product[8:16]
        scaled = grad_pre * gain[...]
        mean = jnp.sum(scaled, axis=-1, keepdims=True) * (1.0 / width)
        slope = jnp.sum(scaled * normed, axis=-1, keepdims=True) * (1.0 / width)
        inv = inverse[0, at, 0:1]
        grad_conv[0, at, :] = (inv * (scaled - mean - normed * slope)).astype(BF16)
        return 0

    lax.fori_loop(0, frames // 16, norm, 0)

    @pl.when(u == pl.num_programs(0) - 1)
    def _():
        term[...] = jnp.sum(sums[...], axis=0, keepdims=True)


def backward(limit, cotangent, w_out, hat, inverse, gain):
    groups, frames, width = hat.shape
    per = lambda *shape: pl.BlockSpec((1, *shape), lambda u, *_: (u,) + (0,) * len(shape))
    whole = lambda *shape: pl.BlockSpec(shape, lambda u, *_: (0,) * len(shape))
    return pl.pallas_call(
        backward_kernel,
        grid_spec=pltpu.PrefetchScalarGridSpec(
            num_scalar_prefetch=1,
            grid=(groups,),
            in_specs=[
                per(frames, width),
                whole(width, width),
                per(frames, width),
                per(frames, LANES),
                whole(1, width),
            ],
            out_specs=[per(frames, width), whole(1, width)],
            scratch_shapes=[pltpu.VMEM((frames, width), F32), pltpu.VMEM((8, width), F32)],
        ),
        out_shape=[
            jax.ShapeDtypeStruct((groups, frames, width), BF16),
            jax.ShapeDtypeStruct((1, width), F32),
        ],
        name="backward",
        cost_estimate=pl.CostEstimate(
            flops=2 * groups * frames * width * width, bytes_accessed=10 << 20, transcendentals=600000
        ),
        compiler_params=pltpu.CompilerParams(vmem_limit_bytes=30 << 20),
    )(limit, cotangent, w_out, hat, inverse, gain)


def terms_kernel(grad_conv, slab, term, out, grad):
    groups, frames = grad_conv.shape[:2]
    taps = out.shape[0] - 1
    grad[...] = grad_conv[...].astype(F32)
    for r in range(8):
        chosen = [j for j in range(r, taps, 8)]
        totals = [None] * len(chosen)
        for u in range(groups):
            for i in range(frames // 8):
                left = grad[u, 8 * i : 8 * i + 8, :]
                for n, j in enumerate(chosen):
                    value = left * slab[u, 0, pl.ds(8 * i + 1 + j, 8), :]
                    totals[n] = value if totals[n] is None else totals[n] + value
        for n, j in enumerate(chosen):
            out[j : j + 1, :] = jnp.sum(totals[n], axis=0, keepdims=True)
    out[taps : taps + 1, :] = term[...]


def kernel_terms(grad_conv, slab, term, taps):
    groups, frames, width = grad_conv.shape
    blocks, length = slab.shape[1:3]
    return pl.pallas_call(
        terms_kernel,
        grid=(blocks,),
        in_specs=[
            pl.BlockSpec((groups, frames, LANES), lambda c: (0, 0, c)),
            pl.BlockSpec((groups, 1, length, LANES), lambda c: (0, c, 0, 0)),
            pl.BlockSpec((1, LANES), lambda c: (0, c)),
        ],
        out_specs=pl.BlockSpec((taps + 1, LANES), lambda c: (0, c)),
        out_shape=jax.ShapeDtypeStruct((taps + 1, width), F32),
        scratch_shapes=[pltpu.VMEM((groups, frames, LANES), F32)],
        name="kernel_terms",
        cost_estimate=pl.CostEstimate(flops=2 * 31 * 600000, bytes_accessed=4 << 20, transcendentals=0),
        compiler_params=pltpu.CompilerParams(vmem_limit_bytes=16 << 20),
    )(grad_conv, slab, term)


def input_kernel(limit, grad_conv, left, right, hidden, weights, out, block):
    taps = weights.shape[0] - 1
    frames, width = grad_conv.shape[1:]
    blocks = width // LANES
    u = pl.program_id(0)

    def channel(cb, _):
        here = pl.ds(pl.multiple_of(cb * LANES, LANES), LANES)
        there = pl.ds(pl.multiple_of(width + cb * LANES, LANES), LANES)
        block[0:PAD, :] = left[0, :, here].astype(F32)
        block[PAD : PAD + frames, :] = grad_conv[0, :, here].astype(F32)
        block[PAD + frames :, :] = right[0, :, here].astype(F32)
        weight = [weights[j : j + 1, here] for j in range(taps)]
        for start in range(0, frames, 64):
            at = slice(start, start + 64)
            grad = depthwise(block, weight, start, 64, range(taps - 1, -1, -1))
            row = start + lax.broadcasted_iota(jnp.int32, (64, LANES), 0)
            grad = jnp.where(row < limit[u], grad, 0.0)
            linear = hidden[0, at, here].astype(F32)
            gate = sigmoid(hidden[0, at, there].astype(F32))
            opened = grad * gate
            out[0, at, here] = opened.astype(BF16)
            out[0, at, there] = (opened * linear * (1.0 - gate)).astype(BF16)
        return 0

    lax.fori_loop(0, blocks, channel, 0)


def input_gradient(limit, grad_conv, left, right, hidden, weights):
    groups, frames, double = hidden.shape
    width = double // 2
    per = lambda *shape: pl.BlockSpec((1, *shape), lambda u, *_: (u,) + (0,) * len(shape))
    whole = lambda *shape: pl.BlockSpec(shape, lambda u, *_: (0,) * len(shape))
    return pl.pallas_call(
        input_kernel,
        grid_spec=pltpu.PrefetchScalarGridSpec(
            num_scalar_prefetch=1,
            grid=(groups,),
            in_specs=[
                per(frames, width),
                per(PAD, width),
                per(PAD, width),
                per(frames, double),
                whole(*weights.shape),
            ],
            out_specs=per(frames, double),
            scratch_shapes=[pltpu.VMEM((frames + 2 * PAD, LANES), F32)],
        ),
        out_shape=jax.ShapeDtypeStruct((groups, frames, double), BF16),
        name="input_gradient",
        cost_estimate=pl.CostEstimate(flops=2 * 31 * 600000, bytes_accessed=6 << 20, transcendentals=600000),
        compiler_params=pltpu.CompilerParams(vmem_limit_bytes=20 << 20),
    )(limit, grad_conv, left, right, hidden, weights)


def sum_kernel(factor, got, out, total):
    i = pl.program_id(0)
    own = out.shape[0]

    @pl.when(i == 0)
    def _():
        total[...] = jnp.zeros_like(total)

    total[...] += jnp.sum(got[...].astype(F32), axis=0)

    @pl.when(i == pl.num_programs(0) - 1)
    def _():
        blocks = total.shape[1] // own
        for side in range(2):
            for k in range(blocks):
                lane = (side * blocks + k) * LANES
                out[:, lane : lane + LANES] = total[side, own * k : own * (k + 1), :] * factor


def sum_pieces(got, factor, own, width):
    pairs, sides, deep, _ = got.shape
    step = 8
    return pl.pallas_call(
        functools.partial(sum_kernel, factor),
        grid=(pairs // step,),
        in_specs=[pl.BlockSpec((step, sides, deep, LANES), lambda i: (i, 0, 0, 0))],
        out_specs=pl.BlockSpec((own, width), lambda i: (0, 0)),
        out_shape=jax.ShapeDtypeStruct((own, width), F32),
        scratch_shapes=[pltpu.VMEM((sides, deep, LANES), F32)],
        name="sum_pieces",
        compiler_params=pltpu.CompilerParams(vmem_limit_bytes=8 << 20),
    )(got)


def neighbours(tail, head):
    ends = lax.axis_size("seq") - 1
    left = lax.ppermute(tail, "seq", [(i, i + 1) for i in range(ends)])
    right = lax.ppermute(head, "seq", [(i + 1, i) for i in range(ends)])
    return left, right


def local(hidden, cotangent, lengths, kernel, conv_gain, w_out):
    groups, frames, double = hidden.shape
    width = double // 2
    half = width // 2
    taps = kernel.shape[1]
    seq_count = lax.axis_size("seq")
    devices = lax.axis_size("dp") * seq_count
    own = width // devices
    rows = groups * frames
    swap = [(i, i ^ 1) for i in range(seq_count)]
    place = lax.axis_index("seq")
    core = place % 2
    limit = lengths - place * frames
    weights = jnp.concatenate([kernel, jnp.zeros((width, 1), F32)], axis=1).T
    gain = conv_gain.reshape(1, width)

    def gated(start):
        cells = hidden[:, start : start + PAD].astype(F32)
        spots = start + jnp.arange(PAD, dtype=jnp.int32)
        keep = spots[None, :, None] < limit[:, None, None]
        return jnp.where(keep, cells[..., :width] * sigmoid(cells[..., width:]), 0.0).astype(BF16)

    left, right = neighbours(gated(frames - PAD), gated(0))
    flat = cotangent.reshape(rows, width)
    sent = jnp.where(core == 0, flat[:, half:], flat[:, :half])
    other = lax.ppermute(sent, "seq", swap)

    slab, hat, inverse, swished = forward(limit, hidden, left, right, weights, gain)
    near = swished.reshape(rows, width)
    far = lax.ppermute(near, "seq", swap)
    pieces = product(core.reshape(1), near, far, flat, other, devices)
    got = lax.all_to_all(
        pieces.reshape(devices, own * half // LANES, LANES), AXES, 0, 0, tiled=True
    )

    hat, pieces = lax.optimization_barrier((hat, pieces))
    grad_conv, term_conv = backward(limit, cotangent, w_out, hat, inverse, gain)
    grad_left, grad_right = neighbours(grad_conv[:, frames - PAD :], grad_conv[:, :PAD])
    terms = kernel_terms(grad_conv, slab, term_conv, taps)
    small = terms.T.reshape(devices, own * (taps + 1) // LANES, LANES)
    got_small = lax.all_to_all(small, AXES, 0, 0, tiled=True)
    grad_hidden = input_gradient(limit, grad_conv, grad_left, grad_right, hidden, weights)

    factor = 1.0 / math.sqrt(groups * lax.axis_size("dp") * frames * seq_count)
    grad_w = sum_pieces(got.reshape(devices // 2, 2, -1, LANES), factor, own, width)
    summed = jnp.sum(got_small, axis=0).reshape(own, taps + 1) * factor
    return grad_hidden, grad_w, summed[:, :taps], summed[:, taps]


def solution(mesh):
    in_specs = (P("dp", "seq", None), P("dp", "seq", None), P("dp"), P(), P(), P())
    out_specs = (P("dp", "seq", None), P(AXES, None), P(AXES, None), P(AXES))
    return jax.shard_map(local, mesh=mesh, in_specs=in_specs, out_specs=out_specs, check_vma=False)
```

time: 138 us -> 135 us (0.978)
  the two profiles are of different devices: /device:TPU:1 before, /device:TPU:22 now
where the time goes in v2:
time: 135 us
  Pallas kernels  44.7 us (33%)
  waiting for transfers between devices  27.5 us (20%)
  starting transfers between devices  23.9 us (18%)
  blocking collectives  18 us (13%)
  local copies, waits for them, and re-layouts  13.4 us (10%)
  other arithmetic  6.31 us (5%)
    ppermute x2, waiting for transfers between devices, neighbours(): right = lax.ppermute(head, 'seq', [(i + 1, i) for i in range(ends)])  19.1 us
    all_to_all x1, blocking collectives, local(): got_small = lax.all_to_all(small, AXES, 0, 0, tiled=True)  18 us
    pallas_call x1, Pallas kernels, forward(): pl.pallas_call(forward_kernel, grid_spec=pltpu.PrefetchScalarGridSpec(num...  13.1 us
    ppermute x2, starting transfers between devices, neighbours(): right = lax.ppermute(head, 'seq', [(i + 1, i) for i in range(ends)])  10.8 us
    all_to_all x1, starting transfers between devices, local(): lax.all_to_all(pieces.reshape(devices, own * half // LANES, LANES), AXES,...  8.7 us
    pallas_call x1, Pallas kernels, input_gradient(): pl.pallas_call(input_kernel, grid_spec=pltpu.PrefetchScalarGridSpec(num_s...  7.98 us
    pallas_call x1, Pallas kernels, backward(): pl.pallas_call(backward_kernel, grid_spec=pltpu.PrefetchScalarGridSpec(nu...  7.7 us
    unnamed x30, local copies, waits for them, and re-layouts  6.71 us
  transfers between devices with their start and end apart: 7, of which 4 were waited for; matrix products, arithmetic and copies ran while one was open for 4% of the time, Pallas kernels for 6%

profile of v2, /device:TPU:22, one launch (start us, length us, event | category | flops | bytes accessed | tf_op | source)
XLA Modules:
  0.0 134.7 jit_solution(15767060093336913634)
XLA Ops:
  0.7 2.1 %slice_convert_fusion = (f32[2,16,3072]{2,1,0:T(8,128)}, f32[2,16,3072]{2,1,0:T(8,128)}) fusion(bf16[2,192,3072]{2,1,0:T(8,128)(2,1)} %hidden.3), kind=kLoop, calls=%fused_computation.16 | loop fusion | flops 196608 | bytes 1179648 | tf_op jit(solution)/shard_map/convert_element_type | solution.py:383
  3.6 1.1 fusion.11
  4.7 1.9 %collective-permute-start = (bf16[2,16,1536]{2,1,0:T(8,128)(2,1)S(1)}, bf16[2,16,1536]{2,1,0:T(8,128)(2,1)S(1)}, u32[]{:S(2)}, u32[]{:S(2)}) collective-permute-start(bf16[2,16,1536]{2,1,0:T(8,128)(2,1)S(1)} %fusion.11), channel_id=1, source_target_pairs={{0,1},{1,2},{2,3},{3,4},{4,5},{5,6},{6,7},{7,8},{8,9},{9,10},{10,1... | collective-permute-start | bytes 294920 | tf_op jit(solution)/shard_map/ppermute | solution.py:361
  6.6 1.1 fusion.5
  7.7 5.8 %collective-permute-start.1 = (bf16[2,16,1536]{2,1,0:T(8,128)(2,1)S(1)}, bf16[2,16,1536]{2,1,0:T(8,128)(2,1)S(1)}, u32[]{:S(2)}, u32[]{:S(2)}) collective-permute-start(bf16[2,16,1536]{2,1,0:T(8,128)(2,1)S(1)} %fusion.5), channel_id=1, source_target_pairs={{1,0},{2,1},{3,2},{4,3},{5,4},{6,5},{7,6},{8,7},{9,8},{10,9},{11,1... | collective-permute-start | bytes 294920 | tf_op jit(solution)/shard_map/ppermute | solution.py:362
  15.7 13.1 %forward.1 = (f32[2,12,224,128]{3,2,1,0:T(8,128)S(1)}, f32[2,192,1536]{2,1,0:T(8,128)S(1)}, f32[2,192,128]{2,1,0:T(8,128)S(1)}, bf16[2,192,1536]{2,1,0:T(8,128)(2,1)}) custom-call(s32[2]{0:T(128)S(1)} %broadcast_subtract_fusion.limit, bf16[2,192,3072]{2,1,0:T(8,128)(2,1)S(1)} %copy-done, bf16[2,16,1536]{2,1,0:T(8,128)(2,1)S(1)} %collective-permute-done.left, ...), custom_call_target="tpu_custom_call" | custom-call | flops 37200000 | bytes 9437184 | tf_op jit(solution)/shard_map/forward/pallas_call | solution.py:81
  28.8 1.6 %copy-done.4 = f32[2,12,224,128]{3,2,1,0:T(8,128)} copy-done((f32[2,12,224,128]{3,2,1,0:T(8,128)}, f32[2,12,224,128]{3,2,1,0:T(8,128)S(1)}, u32[]{:S(2)}) %copy-start.4) | copy-done | bytes 2752536
  30.3 1.4 %copy-done.7 = f32[2,192,1536]{2,1,0:T(8,128)} copy-done((f32[2,192,1536]{2,1,0:T(8,128)}, f32[2,192,1536]{2,1,0:T(8,128)S(1)}, u32[]{:S(2)}) %copy-start.7) | copy-done | bytes 2359320
  33.1 3.2 %collective-permute-done.3.other = bf16[384,768]{1,0:T(8,128)(2,1)S(1)} collective-permute-done((bf16[384,768]{1,0:T(8,128)(2,1)S(1)}, bf16[384,768]{1,0:T(8,128)(2,1)S(1)}, u32[]{:S(2)}, u32[]{:S(2)}) %collective-permute-start.3) | collective-permute-done | bytes 589856 | tf_op jit(solution)/shard_map/ppermute | solution.py:391
  36.3 4.9 %product.1 = bf16[64,2,72,128]{3,2,1,0:T(8,128)(2,1)S(1)} custom-call(s32[1]{0:T(128)} %bitcast.1.core, bf16[384,1536]{1,0:T(8,128)(2,1)} %bitcast.2.near, bf16[384,1536]{1,0:T(8,128)(2,1)} %collective-permute-done.2.far, bf16[384,1536]{1,0:T(8,128)(2,1)S(1)} %bitcast.10, bf16[384,768]{1,0:T(8,128)(2,1)S(1)} %collective-permute-done.3.other), custom_call_target="tpu_custom_call" | custom-call | flops 1811939328 | bytes 6291456 | tf_op jit(solution)/shard_map/product/pallas_call | solution.py:145
  41.2 1.4 %copy-done.6 = bf16[64,2,72,128]{3,2,1,0:T(8,128)(2,1)} copy-done((bf16[64,2,72,128]{3,2,1,0:T(8,128)(2,1)}, bf16[64,2,72,128]{3,2,1,0:T(8,128)(2,1)S(1)}, u32[]{:S(2)}) %copy-start.6) | copy-done | bytes 2359320
  42.7 7.7 %backward.1 = (bf16[2,192,1536]{2,1,0:T(8,128)(2,1)S(1)}, f32[1,1536]{1,0:T(1,128)S(1)}) custom-call(s32[2]{0:T(128)S(1)} %broadcast_subtract_fusion.limit, bf16[2,192,1536]{2,1,0:T(8,128)(2,1)S(1)} %copy-done.2, bf16[1536,1536]{1,0:T(8,128)(2,1)S(1)} %copy-done.3, f32[2,192,1536]{2,1,0:T(8,128)S(1)} %copy-done.8, f32[2,192,128]{2,1,0:T(8,128)S(1)} %copy-done.13, ...), custom_call_target="tpu_custom_call" | custom-call | flops 1811939328 | bytes 10485760 | tf_op jit(solution)/shard_map/backward/pallas_call | solution.py:205
  50.4 6.3 %kernel_terms.1 = f32[32,1536]{1,0:T(8,128)S(1)} custom-call(bf16[2,192,1536]{2,1,0:T(8,128)(2,1)S(1)} %get-tuple-element.15.grad_conv, f32[2,12,224,128]{3,2,1,0:T(8,128)S(1)} %copy-done.5, f32[1,1536]{1,0:T(1,128)S(1)} %get-tuple-element.17.term), custom_call_target="tpu_custom_call" | custom-call | flops 37200000 | bytes 4194304 | tf_op jit(solution)/shard_map/kernel_terms/pallas_call | solution.py:253
  57.4 2.1 %copy.10 = f32[1536,32]{1,0:T(8,128)} copy(f32[1536,32]{0,1:T(8,128)} %bitcast.12) | data formatting | bytes 393216 | tf_op jit(solution)/shard_map/transpose | solution.py:405
  59.4 2.1 %reshape.96 = f32[128,3,128]{2,1,0:T(4,128)} reshape(f32[1536,32]{1,0:T(8,128)} %copy.10) | data formatting | bytes 393216 | tf_op jit(solution)/shard_map/reshape | solution.py:405
  61.5 18.0 %all_to_all.10 = f32[128,3,128]{2,1,0:T(4,128)} all-to-all(f32[128,3,128]{2,1,0:T(4,128)} %reshape.96), channel_id=1, replica_groups=mesh['dp'=4,'seq'=32] {'dp','seq'}, dimensions={0} | all-to-all | bytes 393216 | tf_op jit(solution)/shard_map/all_to_all | solution.py:406
  79.6 8.7 %all-to-all-start = ((bf16[128,72,128]{2,1,0:T(8,128)(2,1)}), bf16[128,72,128]{2,1,0:T(8,128)(2,1)}, u32[]{:S(2)}, u32[]{:S(2)}) async-start(bf16[128,72,128]{2,1,0:T(8,128)(2,1)} %bitcast.11), calls=%async_computation | async-start | bytes 4718592 | tf_op jit(solution)/shard_map/all_to_all | solution.py:397
  88.3 5.1 %collective-permute-start.5 = (bf16[2,16,1536]{2,1,0:T(8,128)(2,1)S(1)}, bf16[2,16,1536]{2,1,0:T(8,128)(2,1)S(1)}, u32[]{:S(2)}, u32[]{:S(2)}) collective-permute-start(bf16[2,16,1536]{2,1,0:T(8,128)(2,1)S(1)} %get-tuple-element.20), channel_id=1, source_target_pairs={{1,0},{2,1},{3,2},{4,3},{5,4},{6,5},{7,6},{8,7},{9,8},{10,9},{11,1... | collective-permute-start | bytes 294920 | tf_op jit(solution)/shard_map/ppermute | solution.py:362
  93.4 1.9 %collective-permute-start.4 = (bf16[2,16,1536]{2,1,0:T(8,128)(2,1)S(1)}, bf16[2,16,1536]{2,1,0:T(8,128)(2,1)S(1)}, u32[]{:S(2)}, u32[]{:S(2)}) collective-permute-start(bf16[2,16,1536]{2,1,0:T(8,128)(2,1)S(1)} %get-tuple-element.21), channel_id=1, source_target_pairs={{0,1},{1,2},{2,3},{3,4},{4,5},{5,6},{6,7},{7,8},{8,9},{9,10},{10,1... | collective-permute-start | bytes 294920 | tf_op jit(solution)/shard_map/ppermute | solution.py:361
  95.3 18.6 %collective-permute-done.5.right = bf16[2,16,1536]{2,1,0:T(8,128)(2,1)S(1)} collective-permute-done((bf16[2,16,1536]{2,1,0:T(8,128)(2,1)S(1)}, bf16[2,16,1536]{2,1,0:T(8,128)(2,1)S(1)}, u32[]{:S(2)}, u32[]{:S(2)}) %collective-permute-start.5) | collective-permute-done | bytes 98336 | tf_op jit(solution)/shard_map/ppermute | solution.py:362
  113.9 5.1 %collective-permute-done.4.left = bf16[2,16,1536]{2,1,0:T(8,128)(2,1)S(1)} collective-permute-done((bf16[2,16,1536]{2,1,0:T(8,128)(2,1)S(1)}, bf16[2,16,1536]{2,1,0:T(8,128)(2,1)S(1)}, u32[]{:S(2)}, u32[]{:S(2)}) %collective-permute-start.4) | collective-permute-done | bytes 98336 | tf_op jit(solution)/shard_map/ppermute | solution.py:361
  119.9 8.0 %input_gradient.1 = bf16[2,192,3072]{2,1,0:T(8,128)(2,1)} custom-call(s32[2]{0:T(128)S(1)} %broadcast_subtract_fusion.limit, bf16[2,192,1536]{2,1,0:T(8,128)(2,1)S(1)} %get-tuple-element.15.grad_conv, bf16[2,16,1536]{2,1,0:T(8,128)(2,1)S(1)} %collective-permute-done.4.left, bf16[2,16,1536]{2,1,0:T(8,128)(2,1)S(1)} %collective-permute-done.5.right, ...), custom_call_target="tpu_custom_call" | custom-call | flops 37200000 | bytes 6291456 | tf_op jit(solution)/shard_map/input_gradient/pallas_call | solution.py:303
  127.9 1.1 reduce_sum.9
  129.8 4.9 %sum_pieces.1 = f32[12,1536]{1,0:T(8,128)} custom-call(bf16[64,2,72,128]{3,2,1,0:T(8,128)(2,1)} %bitcast.5.got), custom_call_target="tpu_custom_call" | custom-call | tf_op jit(solution)/shard_map/sum_pieces/pallas_call | solution.py:347
  (43 shorter events, 6.8 us)
Async XLA Ops:
  0.6 15.1 %copy-start = (bf16[2,192,3072]{2,1,0:T(8,128)(2,1)S(1)}, bf16[2,192,3072]{2,1,0:T(8,128)(2,1)}, u32[]{:S(2)}) copy-start(bf16[2,192,3072]{2,1,0:T(8,128)(2,1)} %hidden.3) | copy-start | bytes 7077892
  2.8 29.7 %copy-start.1 = (bf16[2,192,1536]{2,1,0:T(8,128)(2,1)S(1)}, bf16[2,192,1536]{2,1,0:T(8,128)(2,1)}, u32[]{:S(2)}) copy-start(bf16[2,192,1536]{2,1,0:T(8,128)(2,1)} %cotangent.1) | copy-start | bytes 3538948
  4.7 10.5 %collective-permute-start = (bf16[2,16,1536]{2,1,0:T(8,128)(2,1)S(1)}, bf16[2,16,1536]{2,1,0:T(8,128)(2,1)S(1)}, u32[]{:S(2)}, u32[]{:S(2)}) collective-permute-start(bf16[2,16,1536]{2,1,0:T(8,128)(2,1)S(1)} %fusion.11), channel_id=1, source_target_pairs={{0,1},{1,2},{2,3},{3,4},{4,5},{5,6},{6,7},{7,8},{8,9},{9,10},{10,1... | collective-permute-start | bytes 294920 | tf_op jit(solution)/shard_map/ppermute | solution.py:361
  7.7 8.0 %collective-permute-start.1 = (bf16[2,16,1536]{2,1,0:T(8,128)(2,1)S(1)}, bf16[2,16,1536]{2,1,0:T(8,128)(2,1)S(1)}, u32[]{:S(2)}, u32[]{:S(2)}) collective-permute-start(bf16[2,16,1536]{2,1,0:T(8,128)(2,1)S(1)} %fusion.5), channel_id=1, source_target_pairs={{1,0},{2,1},{3,2},{4,3},{5,4},{6,5},{7,6},{8,7},{9,8},{10,9},{11,1... | collective-permute-start | bytes 294920 | tf_op jit(solution)/shard_map/ppermute | solution.py:362
  14.4 14.3 %copy-start.9 = (f32[32,1536]{1,0:T(8,128)}, f32[32,1536]{1,0:T(8,128)S(1)}, u32[]{:S(2)}) copy-start(f32[32,1536]{1,0:T(8,128)S(1)} %pad_bitcast_fusion.weights) | copy-start | bytes 589828
  28.8 1.6 %copy-start.4 = (f32[2,12,224,128]{3,2,1,0:T(8,128)}, f32[2,12,224,128]{3,2,1,0:T(8,128)S(1)}, u32[]{:S(2)}) copy-start(f32[2,12,224,128]{3,2,1,0:T(8,128)S(1)} %get-tuple-element.16.slab) | copy-start | bytes 8257540
  30.3 1.4 %copy-start.7 = (f32[2,192,1536]{2,1,0:T(8,128)}, f32[2,192,1536]{2,1,0:T(8,128)S(1)}, u32[]{:S(2)}) copy-start(f32[2,192,1536]{2,1,0:T(8,128)S(1)} %get-tuple-element.13.hat) | copy-start | bytes 7077892
  31.7 0.7 copy-start.12
  32.4 3.9 %collective-permute-start.2 = (bf16[384,1536]{1,0:T(8,128)(2,1)}, bf16[384,1536]{1,0:T(8,128)(2,1)}, u32[]{:S(2)}, u32[]{:S(2)}) collective-permute-start(bf16[384,1536]{1,0:T(8,128)(2,1)} %bitcast.2.near), channel_id=1, source_target_pairs={{0,1},{1,0},{2,3},{3,2},{4,5},{5,4},{6,7},{7,6},{8,9},{9,8},{10,11... | collective-permute-start | bytes 3538952 | tf_op jit(solution)/shard_map/ppermute | solution.py:395
  32.4 10.2 %copy-start.8 = (f32[2,192,1536]{2,1,0:T(8,128)S(1)}, f32[2,192,1536]{2,1,0:T(8,128)}, u32[]{:S(2)}) copy-start(f32[2,192,1536]{2,1,0:T(8,128)} %copy-done.7) | copy-start | bytes 7077892
  32.5 3.8 %collective-permute-start.3 = (bf16[384,768]{1,0:T(8,128)(2,1)S(1)}, bf16[384,768]{1,0:T(8,128)(2,1)S(1)}, u32[]{:S(2)}, u32[]{:S(2)}) collective-permute-start(bf16[384,768]{1,0:T(8,128)(2,1)S(1)} %slice_select_fusion), channel_id=1, source_target_pairs={{0,1},{1,0},{2,3},{3,2},{4,5},{5,4},{6,7},{7,6},{8,9},{9,8},{10,11... | collective-permute-start | bytes 1769480 | tf_op jit(solution)/shard_map/ppermute | solution.py:391
  36.3 6.3 %copy-start.2 = (bf16[2,192,1536]{2,1,0:T(8,128)(2,1)S(1)}, bf16[2,192,1536]{2,1,0:T(8,128)(2,1)}, u32[]{:S(2)}) copy-start(bf16[2,192,1536]{2,1,0:T(8,128)(2,1)} %cotangent.1) | copy-start | bytes 3538948
  36.3 6.3 %copy-start.3 = (bf16[1536,1536]{1,0:T(8,128)(2,1)S(1)}, bf16[1536,1536]{1,0:T(8,128)(2,1)}, u32[]{:S(2)}) copy-start(bf16[1536,1536]{1,0:T(8,128)(2,1)} %w_out.1) | copy-start | bytes 14155780
  36.3 6.3 %copy-start.13 = (f32[2,192,128]{2,1,0:T(8,128)S(1)}, f32[2,192,128]{2,1,0:T(8,128)}, u32[]{:S(2)}) copy-start(f32[2,192,128]{2,1,0:T(8,128)} %copy-done.12) | copy-start | bytes 589828
  41.2 1.4 %copy-start.6 = (bf16[64,2,72,128]{3,2,1,0:T(8,128)(2,1)}, bf16[64,2,72,128]{3,2,1,0:T(8,128)(2,1)S(1)}, u32[]{:S(2)}) copy-start(bf16[64,2,72,128]{3,2,1,0:T(8,128)(2,1)S(1)} %product.1) | copy-start | bytes 7077892
  42.7 7.7 %copy-start.5 = (f32[2,12,224,128]{3,2,1,0:T(8,128)S(1)}, f32[2,12,224,128]{3,2,1,0:T(8,128)}, u32[]{:S(2)}) copy-start(f32[2,12,224,128]{3,2,1,0:T(8,128)} %copy-done.4) | copy-start | bytes 8257540
  56.7 0.7 copy-start.11
  79.6 50.2 %all-to-all-start = ((bf16[128,72,128]{2,1,0:T(8,128)(2,1)}), bf16[128,72,128]{2,1,0:T(8,128)(2,1)}, u32[]{:S(2)}, u32[]{:S(2)}) async-start(bf16[128,72,128]{2,1,0:T(8,128)(2,1)} %bitcast.11), calls=%async_computation | async-start | bytes 4718592 | tf_op jit(solution)/shard_map/all_to_all | solution.py:397
  88.3 25.6 %collective-permute-start.5 = (bf16[2,16,1536]{2,1,0:T(8,128)(2,1)S(1)}, bf16[2,16,1536]{2,1,0:T(8,128)(2,1)S(1)}, u32[]{:S(2)}, u32[]{:S(2)}) collective-permute-start(bf16[2,16,1536]{2,1,0:T(8,128)(2,1)S(1)} %get-tuple-element.20), channel_id=1, source_target_pairs={{1,0},{2,1},{3,2},{4,3},{5,4},{6,5},{7,6},{8,7},{9,8},{10,9},{11,1... | collective-permute-start | bytes 294920 | tf_op jit(solution)/shard_map/ppermute | solution.py:362
  93.4 25.7 %collective-permute-start.4 = (bf16[2,16,1536]{2,1,0:T(8,128)(2,1)S(1)}, bf16[2,16,1536]{2,1,0:T(8,128)(2,1)S(1)}, u32[]{:S(2)}, u32[]{:S(2)}) collective-permute-start(bf16[2,16,1536]{2,1,0:T(8,128)(2,1)S(1)} %get-tuple-element.21), channel_id=1, source_target_pairs={{0,1},{1,2},{2,3},{3,4},{4,5},{5,6},{6,7},{7,8},{8,9},{9,10},{10,1... | collective-permute-start | bytes 294920 | tf_op jit(solution)/shard_map/ppermute | solution.py:361
  119.0 0.9 copy-start.10
  129.1 5.6 %copy-start.14 = (f32[12,32]{1,0:T(8,128)}, f32[12,32]{1,0:T(8,128)S(1)}, u32[]{:S(2)}) copy-start(f32[12,32]{1,0:T(8,128)S(1)} %mul.39) | copy-start | bytes 4612

commit v3 on v1

v3 whole, which is shorter than its diff:
```python
import functools
import math

import jax
import jax.numpy as jnp
from jax import lax
from jax.experimental import pallas as pl
from jax.experimental.pallas import tpu as pltpu
from jax.sharding import PartitionSpec as P

EPSILON = 1e-05
AXES = ("dp", "seq")
LANES = 128
HALF_PAD = 16
PAD = 32
TILE = 16
F32, BF16 = jnp.float32, jnp.bfloat16
VMEM = pl.BlockSpec(memory_space=pltpu.VMEM)
SMEM = pl.BlockSpec(memory_space=pltpu.SMEM)


def sigmoid(x):
    return 0.5 * jnp.tanh(0.5 * x) + 0.5


def lane(block):
    return pl.ds(pl.multiple_of(block * LANES, LANES), LANES)


def call(kernel, in_specs, out_shape, scratch, flops, limit, aliases=None):
    return pl.pallas_call(
        kernel,
        in_specs=in_specs,
        out_specs=jax.tree.map(lambda _: VMEM, out_shape),
        out_shape=out_shape,
        scratch_shapes=scratch,
        input_output_aliases=aliases or {},
        cost_estimate=pl.CostEstimate(flops=flops, bytes_accessed=8 << 20, transcendentals=0),
        compiler_params=pltpu.CompilerParams(vmem_limit_bytes=limit << 20),
    )


def shape(dims, dtype):
    return jax.ShapeDtypeStruct(dims, dtype)


def depthwise(slab, weight, start, rows, order):
    total = None
    for j, row in enumerate(order):
        term = slab[pl.ds(start + 1 + j, rows), :] * weight[row]
        total = term if total is None else total + term
    return total


def edges_kernel(limit, hidden, cotangent, tail, head):
    groups, frames, double = hidden.shape
    width = double // 2
    for u in range(groups):
        for out, start, near in ((tail, frames - PAD, frames - HALF_PAD), (head, 0, 0)):
            for cb in range(width // LANES):
                here = slice(cb * LANES, (cb + 1) * LANES)
                there = slice(width + cb * LANES, width + (cb + 1) * LANES)
                row = start + lax.broadcasted_iota(jnp.int32, (PAD, LANES), 0)
                linear = hidden[u, start : start + PAD, here].astype(F32)
                gate = sigmoid(hidden[u, start : start + PAD, there].astype(F32))
                glu = jnp.where(row < limit[u], linear * gate, 0.0)
                out[u, 0:PAD, here] = glu.astype(BF16)
            out[u, PAD:, :] = cotangent[u, near : near + HALF_PAD, :]


def gate_kernel(limit, hidden, slab):
    groups, frames, double = hidden.shape
    width = double // 2
    blocks = width // LANES
    for u in range(groups):

        def channel(cb, _):
            row = lax.broadcasted_iota(jnp.int32, (frames, LANES), 0)
            linear = hidden[u, :, lane(cb)].astype(F32)
            gate = sigmoid(hidden[u, :, lane(blocks + cb)].astype(F32))
            glu = jnp.where(row < limit[u], linear * gate, 0.0)
            slab[u, cb, PAD : PAD + frames, :] = glu.astype(BF16).astype(F32)
            return 0

        lax.fori_loop(0, blocks, channel, 0)


def forward_kernel(limit, gated, left, right, weights, gain, slab, hat, inverse, swished):
    groups, blocks, length = slab.shape[:3]
    taps = weights.shape[0] - 1
    width = blocks * LANES
    frames = length - 2 * PAD
    span = frames + 2 * HALF_PAD
    chunk = span // 4
    for u in range(groups):

        def channel(cb, _):
            block = slab.at[u, cb]
            block[0:PAD, :] = left[u, 0:PAD, lane(cb)].astype(F32)
            block[PAD + frames :, :] = right[u, 0:PAD, lane(cb)].astype(F32)
            weight = [weights[j : j + 1, lane(cb)] for j in range(taps)]
            for start in range(0, span, chunk):
                at = slice(u * span + start, u * span + start + chunk)
                hat[at, lane(cb)] = depthwise(block, weight, start, chunk, range(taps))
            return 0

        lax.fori_loop(0, blocks, channel, 0)

        def normalize(i, _):
            at = pl.ds(pl.multiple_of(u * span + i * TILE, TILE), TILE)
            values = hat[at, :]
            centered = values - jnp.sum(values, axis=-1, keepdims=True) * (1.0 / width)
            spread = jnp.sum(centered * centered, axis=-1, keepdims=True) * (1.0 / width)
            inv = lax.rsqrt(spread + EPSILON)
            normed = centered * inv
            hat[at, :] = normed
            inverse[at, :] = jnp.broadcast_to(inv, (TILE, LANES))

            @pl.when((i >= 1) & (i <= frames // TILE))
            def _():
                pre = normed * gain[...]
                out = pre * sigmoid(pre)
                row = (i - 1) * TILE + lax.broadcasted_iota(jnp.int32, (TILE, width), 0)
                to = pl.ds(pl.multiple_of(u * frames + (i - 1) * TILE, TILE), TILE)
                swished[to, :] = jnp.where(row < limit[u], out, 0.0).astype(BF16)

            return 0

        lax.fori_loop(0, span // TILE, normalize, 0)


CONTRACT_ROWS = (((0,), (0,)), ((), ()))


def product_kernel(core, near, cotangent, far, other, packed, out, scratch):
    width = near.shape[1]
    half = width // 2
    pairs = scratch.shape[0]
    step = 24 * pairs
    deep = out.shape[2] - 8
    first = lax.broadcasted_iota(jnp.int32, (pairs, 8, LANES), 1) < 4
    pick = lambda a, b: jnp.where(first, a, b)
    roll = lambda a: pltpu.roll(a, 4, 1)
    mine = pl.ds(pl.multiple_of(core[0] * half, LANES), half)

    def rows(s, _):
        at = pl.ds(pl.multiple_of(s * step, step), step)
        result = lax.dot_general(
            near[:, at], cotangent[:, mine], CONTRACT_ROWS, preferred_element_type=F32
        ) + lax.dot_general(far[:, at], other[...], CONTRACT_ROWS, preferred_element_type=F32)

        def parts(k):
            cut = result[:, k * LANES : (k + 1) * LANES].reshape(pairs, 3, 8, LANES)
            return cut[:, 0], cut[:, 1], cut[:, 2]

        for q in range(half // LANES // 2):
            a, b, c = parts(2 * q)
            d, e, f = parts(2 * q + 1)
            rb, rc, rd = roll(b), roll(c), roll(d)
            even = (a, pick(b, rd), pick(rd, roll(e)))
            odd = (pick(rb, rc), pick(rc, e), f)
            for side, tiles in enumerate((even, odd)):
                for i, tile in enumerate(tiles):
                    scratch[:, side, 24 * q + 8 * i : 24 * q + 8 * i + 8, :] = tile
        small = packed[pl.ds(s * pairs, pairs)]
        scratch[:, :, deep:, :] = small
        out[pl.ds(s * pairs, pairs)] = scratch[...].astype(BF16)
        return 0

    lax.fori_loop(0, width // step, rows, 0)


def backward_kernel(limit, cotangent, left, right, w_out, hat, inverse, gain, slab, term, held, grad, sums):
    groups, frames, width = cotangent.shape
    span = frames + 2 * HALF_PAD
    blocks = width // LANES
    for u in range(groups):
        base = u * span
        held[base : base + HALF_PAD, :] = left[u, PAD:, :]
        held[base + HALF_PAD : base + HALF_PAD + frames, :] = cotangent[u]
        held[base + HALF_PAD + frames : base + span, :] = right[u, PAD:, :]
    step = 2 * LANES

    def columns(n, _):
        at = pl.ds(pl.multiple_of(n * step, step), step)
        grad[:, at] = lax.dot_general(
            held[...], w_out[at, :], (((1,), (1,)), ((), ())), preferred_element_type=F32
        )
        return 0

    lax.fori_loop(0, width // step, columns, 0)
    sums[...] = jnp.zeros_like(sums)
    for u in range(groups):

        def norm(i, _):
            at = pl.ds(pl.multiple_of(u * span + i * TILE, TILE), TILE)
            row = i * TILE - HALF_PAD + lax.broadcasted_iota(jnp.int32, (TILE, width), 0)
            swish = jnp.where(row < limit[u], grad[at, :], 0.0)
            normed = hat[at, :]
            pre = normed * gain[...]
            gate = sigmoid(pre)
            grad_pre = swish * gate * (1.0 + pre * (1.0 - gate))

            @pl.when((i >= 1) & (i <= frames // TILE))
            def _():
                product = grad_pre * normed
                sums[...] += product[0:8] + product[8:16]

            scaled = grad_pre * gain[...]
            mean = jnp.sum(scaled, axis=-1, keepdims=True) * (1.0 / width)
            slope = jnp.sum(scaled * normed, axis=-1, keepdims=True) * (1.0 / width)
            inv = inverse[at, 0:1]
            result = (inv * (scaled - mean - normed * slope)).astype(BF16).astype(F32)
            to = pl.ds(pl.multiple_of(i * TILE, TILE), TILE)
            for cb in range(blocks):
                slab[u, cb, to, :] = result[:, cb * LANES : (cb + 1) * LANES]
            return 0

        lax.fori_loop(0, span // TILE, norm, 0)
    term[...] = jnp.sum(sums[...], axis=0, keepdims=True)


def terms_kernel(grad, slab, term, packed, square, columns, rounded, rest):
    groups, blocks, span = grad.shape[:3]
    frames = span - 2 * HALF_PAD
    taps = 31
    square[...] = jnp.zeros_like(square)

    def channel(cb, _):
        for r in range(8):
            chosen = [j for j in range(r, taps, 8)]
            totals = [None] * len(chosen)
            for u in range(groups):
                for i in range(frames // 8):
                    value = grad[u, cb, HALF_PAD + 8 * i : HALF_PAD + 8 * i + 8, :]
                    for n, j in enumerate(chosen):
                        place = PAD - taps // 2 + 8 * i + j
                        part = value * slab[u, cb, pl.ds(place, 8), :]
                        totals[n] = part if totals[n] is None else totals[n] + part
            for n, j in enumerate(chosen):
                square[j : j + 1, :] = jnp.sum(totals[n], axis=0, keepdims=True)
        square[taps : taps + 1, :] = term[:, lane(cb)]
        columns[lane(cb), :] = square[...].T
        return 0

    lax.fori_loop(0, blocks, channel, 0)
    quarter = columns.shape[0] // 4
    total = columns[pl.ds(0, quarter, stride=4), :]
    for m in range(1, 4):
        total = total + pltpu.roll(columns[pl.ds(m, quarter, stride=4), :], 32 * m, 1)
    high = total.astype(BF16).astype(F32)
    rounded[0:quarter, :] = high
    rest[8 : 8 + quarter, :] = total - high
    row = lax.broadcasted_iota(jnp.int32, (8, LANES), 0)
    pairs, sides = packed.shape[:2]
    for d in range(pairs * sides):
        upper = rounded[3 * d : 3 * d + 8, :]
        lower = rest[3 * d + 5 : 3 * d + 13, :]
        tile = jnp.where(row < 3, upper, jnp.where(row < 6, lower, 0.0))
        packed[d // 2, d % 2] = tile


def input_kernel(limit, grad, hidden, weights, out):
    groups, frames, _ = hidden.shape
    blocks = grad.shape[1]
    taps = weights.shape[0] - 1
    chunk = 64
    for u in range(groups):

        def channel(cb, _):
            block = grad.at[u, cb]
            weight = [weights[j : j + 1, lane(cb)] for j in range(taps)]
            for start in range(0, frames, chunk):
                at = slice(start, start + chunk)
                total = depthwise(block, weight, start, chunk, range(taps - 1, -1, -1))
                row = start + lax.broadcasted_iota(jnp.int32, (chunk, LANES), 0)
                total = jnp.where(row < limit[u], total, 0.0)
                linear = hidden[u, at, lane(cb)].astype(F32)
                gate = sigmoid(hidden[u, at, lane(blocks + cb)].astype(F32))
                opened = total * gate
                out[u, at, lane(cb)] = opened.astype(BF16)
                out[u, at, lane(blocks + cb)] = (opened * linear * (1.0 - gate)).astype(BF16)
            return 0

        lax.fori_loop(0, blocks, channel, 0)


def sum_kernel(factor, got, out, taps_out, gain_out, total):
    own = out.shape[0]
    pairs, _, tall, _ = got.shape
    step = 4
    total[...] = jnp.zeros_like(total)

    def add(i, _):
        total[...] += jnp.sum(got[pl.ds(i * step, step)].astype(F32), axis=0)
        return 0

    lax.fori_loop(0, pairs // step, add, 0)
    deep = tall - 8
    blocks = deep // own
    for side in range(2):
        for k in range(blocks):
            at = (side * blocks + k) * LANES
            out[:, at : at + LANES] = total[side, own * k : own * (k + 1), :] * factor
    both = total[0, deep:, :] + total[1, deep:, :]
    small = (both[0:3] + both[3:6]) * factor
    taps = taps_out.shape[1]
    spot = lax.broadcasted_iota(jnp.int32, (1, LANES), 1)
    gains = jnp.zeros((1, LANES), F32)
    for r in range(3):
        for m in range(4):
            c = 4 * r + m
            turned = pltpu.roll(small[r : r + 1, :], (LANES - 32 * m) % LANES, 1)
            taps_out[c : c + 1, :] = turned[:, :taps]
            gains = jnp.where(spot == c, pltpu.roll(turned, (c - taps) % LANES, 1), gains)
    gain_out[...] = gains[:, :own]


def local(hidden, cotangent, lengths, kernel, conv_gain, w_out):
    groups, frames, double = hidden.shape
    width = double // 2
    half = width // 2
    blocks = width // LANES
    taps = kernel.shape[1]
    seq_count = lax.axis_size("seq")
    devices = lax.axis_size("dp") * seq_count
    own = width // devices
    rows = groups * frames
    span = frames + 2 * HALF_PAD
    length = frames + 2 * PAD
    deep = own * half // LANES
    ends = seq_count - 1
    swap = [(i, i ^ 1) for i in range(seq_count)]
    place = lax.axis_index("seq")
    core = place & 1
    conv_flops = 2 * taps * rows * width

    limit = lengths - place * frames
    flat = cotangent.reshape(rows, width)
    tail, head = call(
        edges_kernel,
        [SMEM, VMEM, VMEM],
        [shape((groups, PAD + HALF_PAD, width), BF16)] * 2,
        [],
        1 << 20,
        4,
    )(limit, hidden, cotangent)
    left = lax.ppermute(tail, "seq", [(i, i + 1) for i in range(ends)])
    right = lax.ppermute(head, "seq", [(i + 1, i) for i in range(ends)])
    sent = jnp.where(core == 0, flat[:, half:], flat[:, :half])
    other = lax.ppermute(sent, "seq", swap)
    gated = call(
        gate_kernel, [SMEM, VMEM], shape((groups, blocks, length, LANES), F32), [], 8 << 20, 4
    )(limit, hidden)
    weights = jnp.concatenate([kernel, jnp.zeros((width, 1), F32)], axis=1).T
    gain = conv_gain.reshape(1, width)
    slab, hat, inverse, swished = call(
        forward_kernel,
        [SMEM] + [VMEM] * 5,
        [
            shape((groups, blocks, length, LANES), F32),
            shape((groups * span, width), F32),
            shape((groups * span, LANES), F32),
            shape((rows, width), BF16),
        ],
        [],
        conv_flops,
        4,
        {1: 0},
    )(limit, gated, left, right, weights, gain)
    far = lax.ppermute(swished, "seq", swap)
    grad, term_conv = call(
        backward_kernel,
        [SMEM] + [VMEM] * 7,
        [shape((groups, blocks, span, LANES), F32), shape((1, width), F32)],
        [
            pltpu.VMEM((groups * span, width), BF16),
            pltpu.VMEM((groups * span, width), F32),
            pltpu.VMEM((8, width), F32),
        ],
        2 * rows * width * width,
        10,
    )(limit, cotangent, left, right, w_out, hat, inverse, gain)
    packed = call(
        terms_kernel,
        [VMEM] * 3,
        shape((devices // 2, 2, 8, LANES), F32),
        [
            pltpu.VMEM((LANES, LANES), F32),
            pltpu.VMEM((width, LANES), F32),
            pltpu.VMEM((width // 4 + 8, LANES), F32),
            pltpu.VMEM((width // 4 + 16, LANES), F32),
        ],
        conv_flops,
        6,
    )(grad, slab, term_conv)
    pieces = call(
        product_kernel,
        [SMEM] + [VMEM] * 5,
        shape((devices // 2, 2, deep + 8, LANES), BF16),
        [pltpu.VMEM((16, 2, deep + 8, LANES), F32)],
        4 * rows * width * half,
        8,
    )(core.reshape(1), swished, flat, far, other, packed)
    got = lax.all_to_all(pieces.reshape(devices, deep + 8, LANES), AXES, 0, 0, tiled=True)
    grad_hidden = call(
        input_kernel, [SMEM] + [VMEM] * 3, shape((groups, frames, double), BF16), [], conv_flops, 4
    )(limit, grad, hidden, weights)

    factor = 1.0 / math.sqrt(groups * lax.axis_size("dp") * frames * seq_count)
    grad_w, grad_kernel, grad_gain = call(
        functools.partial(sum_kernel, factor),
        [VMEM],
        [shape((own, width), F32), shape((own, taps), F32), shape((1, own), F32)],
        [pltpu.VMEM((2, deep + 8, LANES), F32)],
        1 << 20,
        4,
    )(got.reshape(devices // 2, 2, deep + 8, LANES))
    return grad_hidden, grad_w, grad_kernel, grad_gain.reshape(own)


def solution(mesh):
    in_specs = (P("dp", "seq", None), P("dp", "seq", None), P("dp"), P(), P(), P())
    out_specs = (P("dp", "seq", None), P(AXES, None), P(AXES, None), P(AXES))
    return jax.shard_map(local, mesh=mesh, in_specs=in_specs, out_specs=out_specs, check_vma=False)
```

time: 138 us -> 116 us (0.84)
  other arithmetic: 51.4 us -> 1.97 us
  Pallas kernels: 0 us -> 47.4 us
  starting transfers between devices: 33.5 us -> 18 us
  waiting for transfers between devices: 19.6 us -> 30.2 us
  matrix products: 10.5 us -> 0 us
  local copies, waits for them, and re-layouts: 20.7 us -> 16.7 us
    pallas_call x0 -> x8, Pallas kernels: none -> 47.4 us  [the longest x1 13.6 us: local(): call(forward_kernel, [SMEM] + [VMEM] * 5, [shape((groups, blocks, length,...]
    reduce_sum x6 -> x0, other arithmetic: 25.9 us -> none  [the longest x1 11.5 us: normalize(): centered = values - jnp.mean(values, axis=-1, keepdims=True)]
    unnamed x78 -> x38, local copies, waits for them, and re-layouts: 2.65 us -> 16.7 us
    dot_general x2 -> x0, matrix products: 10.5 us -> none  [the longest x1 5.23 us: outer_cols(): lax.dot_general(left_side, right_side, (((1,), (1,)), ((), ())), preferre...]
    reshape x3 -> x1, local copies, waits for them, and re-layouts: 9.95 us -> 0.01 us  [local(): gain = conv_gain.reshape(1, width)]
    all_to_all x2 -> x1, starting transfers between devices: 20.5 us -> 10.6 us  [local(): lax.all_to_all(pieces.reshape(devices, deep + 8, LANES), AXES, 0, 0, tile...]
    convert_element_type x7 -> x0, other arithmetic: 9.86 us -> none  [the longest x1 3.64 us: local(): swished = (pre_act * act_gate).astype(jnp.bfloat16)]
    add x2 -> x0, other arithmetic: 9 us -> none  [the longest x1 9 us: local(): grad_glu + grad_padded[:, last - j:last - j + frames] * kernel[:, j]]
  transfers between devices with their start and end apart: 8 -> 5, of which waited for: 2 -> 2; matrix products, arithmetic and copies ran while one was open for 51% -> 1% of each run, Pallas kernels for 0% -> 22%
where the time goes in v3:
time: 116 us; the launch traced here: 115 us
  Pallas kernels  47.4 us (41%)
  waiting for transfers between devices  30.2 us (26%)
  starting transfers between devices  18 us (16%)
  local copies, waits for them, and re-layouts  16.7 us (14%)
  other arithmetic  1.97 us (2%)
    all_to_all x1, waiting for transfers between devices, local(): lax.all_to_all(pieces.reshape(devices, deep + 8, LANES), AXES, 0, 0, tile...  25.7 us
    unnamed x38, local copies, waits for them, and re-layouts  16.7 us
    pallas_call x1, Pallas kernels, local(): call(forward_kernel, [SMEM] + [VMEM] * 5, [shape((groups, blocks, length,...  13.6 us
    all_to_all x1, starting transfers between devices, local(): lax.all_to_all(pieces.reshape(devices, deep + 8, LANES), AXES, 0, 0, tile...  10.6 us
    pallas_call x1, Pallas kernels, local(): call(backward_kernel, [SMEM] + [VMEM] * 7, [shape((groups, blocks, span,...  8.73 us
    pallas_call x1, Pallas kernels, local(): call(input_kernel, [SMEM] + [VMEM] * 3, shape((groups, frames, double), B...  8.24 us
    pallas_call x1, Pallas kernels, local(): call(terms_kernel, [VMEM] * 3, shape((devices // 2, 2, 8, LANES), F32), [...  6.7 us
    ppermute x1, starting transfers between devices, local(): left = lax.ppermute(tail, 'seq', [(i, i + 1) for i in range(ends)])  4.92 us
  transfers between devices with their start and end apart: 5, of which 2 were waited for; matrix products, arithmetic and copies ran while one was open for 1% of the time, Pallas kernels for 22%

profile of v3, /device:TPU:1, one launch (start us, length us, event | category | flops | bytes accessed | tf_op | source)
XLA Modules:
  0.0 115.1 jit_solution(15849919804025621294)
XLA Ops:
  1.3 1.7 %copy-done = bf16[2,192,3072]{2,1,0:T(8,128)(2,1)S(1)} copy-done((bf16[2,192,3072]{2,1,0:T(8,128)(2,1)S(1)}, bf16[2,192,3072]{2,1,0:T(8,128)(2,1)}, u32[]{:S(2)}) %copy-start) | copy-done | bytes 2359320
  3.0 1.3 %copy-done.3 = bf16[2,192,1536]{2,1,0:T(8,128)(2,1)S(1)} copy-done((bf16[2,192,1536]{2,1,0:T(8,128)(2,1)S(1)}, bf16[2,192,1536]{2,1,0:T(8,128)(2,1)}, u32[]{:S(2)}) %copy-start.3) | copy-done | bytes 1179672
  5.0 4.9 %collective-permute-start = (bf16[2,48,1536]{2,1,0:T(8,128)(2,1)S(1)}, bf16[2,48,1536]{2,1,0:T(8,128)(2,1)S(1)}, u32[]{:S(2)}, u32[]{:S(2)}) collective-permute-start(bf16[2,48,1536]{2,1,0:T(8,128)(2,1)S(1)} %get-tuple-element.15), channel_id=1, source_target_pairs={{0,1},{1,2},{2,3},{3,4},{4,5},{5,6},{6,7},{7,8},{8,9},{9,10},{10,1... | collective-permute-start | bytes 884744 | tf_op jit(solution)/shard_map/ppermute | solution.py:348
  10.0 1.9 %collective-permute-start.1 = (bf16[2,48,1536]{2,1,0:T(8,128)(2,1)S(1)}, bf16[2,48,1536]{2,1,0:T(8,128)(2,1)S(1)}, u32[]{:S(2)}, u32[]{:S(2)}) collective-permute-start(bf16[2,48,1536]{2,1,0:T(8,128)(2,1)S(1)} %get-tuple-element.16), channel_id=1, source_target_pairs={{1,0},{2,1},{3,2},{4,3},{5,4},{6,5},{7,6},{8,7},{9,8},{10,9},{11,1... | collective-permute-start | bytes 884744 | tf_op jit(solution)/shard_map/ppermute | solution.py:349
  11.9 1.6 %shard_map.94.gated = f32[2,12,256,128]{3,2,1,0:T(8,128)S(1)} custom-call(s32[2]{0:T(128)S(1)} %broadcast_subtract_fusion.limit, bf16[2,192,3072]{2,1,0:T(8,128)(2,1)S(1)} %copy-done.1), custom_call_target="tpu_custom_call" | custom-call | flops 8388608 | bytes 8388608 | tf_op jit(solution)/shard_map/pallas_call | solution.py:352
  13.6 4.4 %collective-permute-done.1.right = bf16[2,48,1536]{2,1,0:T(8,128)(2,1)S(1)} collective-permute-done((bf16[2,48,1536]{2,1,0:T(8,128)(2,1)S(1)}, bf16[2,48,1536]{2,1,0:T(8,128)(2,1)S(1)}, u32[]{:S(2)}, u32[]{:S(2)}) %collective-permute-start.1) | collective-permute-done | bytes 294944 | tf_op jit(solution)/shard_map/ppermute | solution.py:349
  18.0 13.6 %shard_map.95 = (f32[2,12,256,128]{3,2,1,0:T(8,128)S(1)}, f32[448,1536]{1,0:T(8,128)S(1)}, f32[448,128]{1,0:T(8,128)S(1)}, bf16[384,1536]{1,0:T(8,128)(2,1)}) custom-call(s32[2]{0:T(128)S(1)} %broadcast_subtract_fusion.limit, f32[2,12,256,128]{3,2,1,0:T(8,128)S(1)} %shard_map.94.gated, ...), custom_call_target="tpu_custom_call", output_to_operand_aliasing={{0}: (1, {})} | custom-call | flops 36569088 | bytes 8388608 | tf_op jit(solution)/shard_map/pallas_call | solution.py:357
  31.6 1.5 %copy-done.9 = f32[448,1536]{1,0:T(8,128)} copy-done((f32[448,1536]{1,0:T(8,128)}, f32[448,1536]{1,0:T(8,128)S(1)}, u32[]{:S(2)}) %copy-start.9) | copy-done | bytes 2752536
  33.8 1.3 %slice_select_fusion = bf16[384,768]{1,0:T(8,128)(2,1)S(1)} fusion(bf16[384,1536]{1,0:T(8,128)(2,1)} %bitcast.7, pred[]{:T(512)S(6)} %eq.3), kind=kLoop, calls=%fused_computation | loop fusion | flops 294912 | bytes 1769473 | tf_op jit(solution)/shard_map/jit(_where)/select_n | solution.py:350
  35.7 1.3 %copy-done.4 = bf16[2,192,1536]{2,1,0:T(8,128)(2,1)S(1)} copy-done((bf16[2,192,1536]{2,1,0:T(8,128)(2,1)S(1)}, bf16[2,192,1536]{2,1,0:T(8,128)(2,1)}, u32[]{:S(2)}) %copy-start.4) | copy-done | bytes 1179672
  37.0 2.3 %copy-done.8 = bf16[1536,1536]{1,0:T(8,128)(2,1)S(1)} copy-done((bf16[1536,1536]{1,0:T(8,128)(2,1)S(1)}, bf16[1536,1536]{1,0:T(8,128)(2,1)}, u32[]{:S(2)}) %copy-start.8) | copy-done | bytes 4718616
  39.3 1.8 %copy-done.10 = f32[448,1536]{1,0:T(8,128)S(1)} copy-done((f32[448,1536]{1,0:T(8,128)S(1)}, f32[448,1536]{1,0:T(8,128)}, u32[]{:S(2)}) %copy-start.10) | copy-done | bytes 2752536
  41.1 1.0 copy-done.12
  42.0 1.0 copy-done.14
  43.0 0.9 copy-done.16
  43.9 8.7 %shard_map.96 = (f32[2,12,224,128]{3,2,1,0:T(8,128)S(1)}, f32[1,1536]{1,0:T(1,128)S(1)}) custom-call(s32[2]{0:T(128)S(1)} %broadcast_subtract_fusion.limit, bf16[2,192,1536]{2,1,0:T(8,128)(2,1)S(1)} %copy-done.4, bf16[2,48,1536]{2,1,0:T(8,128)(2,1)S(1)} %copy-done.12, bf16[2,48,1536]{2,1,0:T(8,128)(2,1)S(1)} %copy-done.14, bf16[1536,1536]{1,0:T(8,128)(2,1)S(1)} %copy-done.8, ...), custom_call_target="tpu_custom_call" | custom-call | flops 1811939328 | bytes 8388608 | tf_op jit(solution)/shard_map/pallas_call | solution.py:372
  52.7 6.7 %shard_map.98.packed = f32[64,2,8,128]{3,2,1,0:T(8,128)S(1)} custom-call(f32[2,12,224,128]{3,2,1,0:T(8,128)S(1)} %get-tuple-element.19.grad, f32[2,12,256,128]{3,2,1,0:T(8,128)S(1)} %get-tuple-element.21.slab, f32[1,1536]{1,0:T(1,128)S(1)} %get-tuple-element.22.term), custom_call_target="tpu_custom_call" | custom-call | flops 36569088 | bytes 8388608 | tf_op jit(solution)/shard_map/pallas_call | solution.py:384
  59.4 4.9 %shard_map.99 = bf16[64,2,80,128]{3,2,1,0:T(8,128)(2,1)S(1)} custom-call(s32[1]{0:T(128)} %bitcast.1.core, bf16[384,1536]{1,0:T(8,128)(2,1)} %get-tuple-element.20.near, bf16[384,1536]{1,0:T(8,128)(2,1)S(1)} %bitcast.8, bf16[384,1536]{1,0:T(8,128)(2,1)} %collective-permute-done.2.far, bf16[384,768]{1,0:T(8,128)(2,1)S(1)} %collective-permute-done.3.other, ...), custom_call_target="tpu_custom_call" | custom-call | flops 1811939328 | bytes 8388608 | tf_op jit(solution)/shard_map/pallas_call | solution.py:397
  64.3 1.5 %copy-done.7 = bf16[64,2,80,128]{3,2,1,0:T(8,128)(2,1)} copy-done((bf16[64,2,80,128]{3,2,1,0:T(8,128)(2,1)}, bf16[64,2,80,128]{3,2,1,0:T(8,128)(2,1)S(1)}, u32[]{:S(2)}) %copy-start.7) | copy-done | bytes 2621464
  65.8 10.6 %all-to-all-start = ((bf16[128,80,128]{2,1,0:T(8,128)(2,1)}), bf16[128,80,128]{2,1,0:T(8,128)(2,1)}, u32[]{:S(2)}, u32[]{:S(2)}) async-start(bf16[128,80,128]{2,1,0:T(8,128)(2,1)} %bitcast.9), calls=%async_computation | async-start | bytes 5242880 | tf_op jit(solution)/shard_map/all_to_all | solution.py:405
  76.5 1.8 %copy-done.6 = f32[2,12,224,128]{3,2,1,0:T(8,128)S(1)} copy-done((f32[2,12,224,128]{3,2,1,0:T(8,128)S(1)}, f32[2,12,224,128]{3,2,1,0:T(8,128)}, u32[]{:S(2)}) %copy-start.6) | copy-done | bytes 2752536
  78.2 8.2 %shard_map.97 = bf16[2,192,3072]{2,1,0:T(8,128)(2,1)} custom-call(s32[2]{0:T(128)S(1)} %broadcast_subtract_fusion.limit, f32[2,12,224,128]{3,2,1,0:T(8,128)S(1)} %copy-done.6, bf16[2,192,3072]{2,1,0:T(8,128)(2,1)S(1)} %copy-done.2, f32[32,1536]{1,0:T(8,128)S(1)} %pad_bitcast_fusion.weights), custom_call_target="tpu_custom_call" | custom-call | flops 36569088 | bytes 8388608 | tf_op jit(solution)/shard_map/pallas_call | solution.py:406
  86.5 25.7 %all-to-all-done = bf16[128,80,128]{2,1,0:T(8,128)(2,1)} async-done(((bf16[128,80,128]{2,1,0:T(8,128)(2,1)}), bf16[128,80,128]{2,1,0:T(8,128)(2,1)}, u32[]{:S(2)}, u32[]{:S(2)}) %all-to-all-start) | async-done | bytes 2621472 | tf_op jit(solution)/shard_map/all_to_all | solution.py:405
  112.2 2.9 %shard_map.100 = (f32[12,1536]{1,0:T(8,128)}, f32[12,31]{1,0:T(8,128)}, f32[1,12]{1,0:T(1,128)}) custom-call(bf16[64,2,80,128]{3,2,1,0:T(8,128)(2,1)} %bitcast.4.got), custom_call_target="tpu_custom_call" | custom-call | flops 1048576 | bytes 8388608 | tf_op jit(solution)/shard_map/pallas_call | solution.py:411
  (36 shorter events, 2.8 us)
Async XLA Ops:
  0.6 11.3 %copy-start.18 = (f32[1536]{0:T(1024)S(1)}, f32[1536]{0:T(1024)}, u32[]{:S(2)}) copy-start(f32[1536]{0:T(1024)} %param.10) | copy-start | bytes 18436
  1.3 1.7 %copy-start = (bf16[2,192,3072]{2,1,0:T(8,128)(2,1)S(1)}, bf16[2,192,3072]{2,1,0:T(8,128)(2,1)}, u32[]{:S(2)}) copy-start(bf16[2,192,3072]{2,1,0:T(8,128)(2,1)} %hidden.5) | copy-start | bytes 7077892
  3.0 1.3 %copy-start.3 = (bf16[2,192,1536]{2,1,0:T(8,128)(2,1)S(1)}, bf16[2,192,1536]{2,1,0:T(8,128)(2,1)}, u32[]{:S(2)}) copy-start(bf16[2,192,1536]{2,1,0:T(8,128)(2,1)} %cotangent.3) | copy-start | bytes 3538948
  4.2 7.7 %copy-start.1 = (bf16[2,192,3072]{2,1,0:T(8,128)(2,1)S(1)}, bf16[2,192,3072]{2,1,0:T(8,128)(2,1)}, u32[]{:S(2)}) copy-start(bf16[2,192,3072]{2,1,0:T(8,128)(2,1)} %hidden.5) | copy-start | bytes 7077892
  5.0 8.6 %collective-permute-start = (bf16[2,48,1536]{2,1,0:T(8,128)(2,1)S(1)}, bf16[2,48,1536]{2,1,0:T(8,128)(2,1)S(1)}, u32[]{:S(2)}, u32[]{:S(2)}) collective-permute-start(bf16[2,48,1536]{2,1,0:T(8,128)(2,1)S(1)} %get-tuple-element.15), channel_id=1, source_target_pairs={{0,1},{1,2},{2,3},{3,4},{4,5},{5,6},{6,7},{7,8},{8,9},{9,10},{10,1... | collective-permute-start | bytes 884744 | tf_op jit(solution)/shard_map/ppermute | solution.py:348
  10.0 8.0 %collective-permute-start.1 = (bf16[2,48,1536]{2,1,0:T(8,128)(2,1)S(1)}, bf16[2,48,1536]{2,1,0:T(8,128)(2,1)S(1)}, u32[]{:S(2)}, u32[]{:S(2)}) collective-permute-start(bf16[2,48,1536]{2,1,0:T(8,128)(2,1)S(1)} %get-tuple-element.16), channel_id=1, source_target_pairs={{1,0},{2,1},{3,2},{4,3},{5,4},{6,5},{7,6},{8,7},{9,8},{10,9},{11,1... | collective-permute-start | bytes 884744 | tf_op jit(solution)/shard_map/ppermute | solution.py:349
  11.9 1.6 %copy-start.17 = (f32[1536,31]{0,1:T(8,128)S(1)}, f32[1536,31]{0,1:T(8,128)}, u32[]{:S(2)}) copy-start(f32[1536,31]{0,1:T(8,128)} %param.9) | copy-start | bytes 571396
  13.6 18.0 %copy-start.11 = (bf16[2,48,1536]{2,1,0:T(8,128)(2,1)}, bf16[2,48,1536]{2,1,0:T(8,128)(2,1)S(1)}, u32[]{:S(2)}) copy-start(bf16[2,48,1536]{2,1,0:T(8,128)(2,1)S(1)} %collective-permute-done.left) | copy-start | bytes 884740
  18.0 15.8 %copy-start.13 = (bf16[2,48,1536]{2,1,0:T(8,128)(2,1)}, bf16[2,48,1536]{2,1,0:T(8,128)(2,1)S(1)}, u32[]{:S(2)}) copy-start(bf16[2,48,1536]{2,1,0:T(8,128)(2,1)S(1)} %collective-permute-done.1.right) | copy-start | bytes 884740
  31.6 1.5 %copy-start.9 = (f32[448,1536]{1,0:T(8,128)}, f32[448,1536]{1,0:T(8,128)S(1)}, u32[]{:S(2)}) copy-start(f32[448,1536]{1,0:T(8,128)S(1)} %get-tuple-element.17.hat) | copy-start | bytes 8257540
  33.1 0.7 copy-start.15
  33.8 25.6 %collective-permute-start.2 = (bf16[384,1536]{1,0:T(8,128)(2,1)}, bf16[384,1536]{1,0:T(8,128)(2,1)}, u32[]{:S(2)}, u32[]{:S(2)}) collective-permute-start(bf16[384,1536]{1,0:T(8,128)(2,1)} %get-tuple-element.20.near), channel_id=1, source_target_pairs={{0,1},{1,0},{2,3},{3,2},{4,5},{5,4},{6,7},{7,6},{8,9},{9,8},{10,11... | collective-permute-start | bytes 3538952 | tf_op jit(solution)/shard_map/ppermute | solution.py:371
  35.1 24.3 %collective-permute-start.3 = (bf16[384,768]{1,0:T(8,128)(2,1)S(1)}, bf16[384,768]{1,0:T(8,128)(2,1)S(1)}, u32[]{:S(2)}, u32[]{:S(2)}) collective-permute-start(bf16[384,768]{1,0:T(8,128)(2,1)S(1)} %slice_select_fusion), channel_id=1, source_target_pairs={{0,1},{1,0},{2,3},{3,2},{4,5},{5,4},{6,7},{7,6},{8,9},{9,8},{10,11... | collective-permute-start | bytes 1769480 | tf_op jit(solution)/shard_map/ppermute | solution.py:351
  35.7 1.3 %copy-start.4 = (bf16[2,192,1536]{2,1,0:T(8,128)(2,1)S(1)}, bf16[2,192,1536]{2,1,0:T(8,128)(2,1)}, u32[]{:S(2)}) copy-start(bf16[2,192,1536]{2,1,0:T(8,128)(2,1)} %cotangent.3) | copy-start | bytes 3538948
  37.0 2.3 %copy-start.8 = (bf16[1536,1536]{1,0:T(8,128)(2,1)S(1)}, bf16[1536,1536]{1,0:T(8,128)(2,1)}, u32[]{:S(2)}) copy-start(bf16[1536,1536]{1,0:T(8,128)(2,1)} %w_out.1) | copy-start | bytes 14155780
  39.3 1.8 %copy-start.10 = (f32[448,1536]{1,0:T(8,128)S(1)}, f32[448,1536]{1,0:T(8,128)}, u32[]{:S(2)}) copy-start(f32[448,1536]{1,0:T(8,128)} %copy-done.9) | copy-start | bytes 8257540
  41.1 1.0 copy-start.12
  42.0 1.0 copy-start.14
  43.0 0.9 copy-start.16
  52.7 6.7 %copy-start.5 = (f32[2,12,224,128]{3,2,1,0:T(8,128)}, f32[2,12,224,128]{3,2,1,0:T(8,128)S(1)}, u32[]{:S(2)}) copy-start(f32[2,12,224,128]{3,2,1,0:T(8,128)S(1)} %get-tuple-element.19.grad) | copy-start | bytes 8257540
  64.3 1.5 %copy-start.7 = (bf16[64,2,80,128]{3,2,1,0:T(8,128)(2,1)}, bf16[64,2,80,128]{3,2,1,0:T(8,128)(2,1)S(1)}, u32[]{:S(2)}) copy-start(bf16[64,2,80,128]{3,2,1,0:T(8,128)(2,1)S(1)} %shard_map.99) | copy-start | bytes 7864324
  65.8 10.6 %copy-start.2 = (bf16[2,192,3072]{2,1,0:T(8,128)(2,1)S(1)}, bf16[2,192,3072]{2,1,0:T(8,128)(2,1)}, u32[]{:S(2)}) copy-start(bf16[2,192,3072]{2,1,0:T(8,128)(2,1)} %hidden.5) | copy-start | bytes 7077892
  65.8 46.4 %all-to-all-start = ((bf16[128,80,128]{2,1,0:T(8,128)(2,1)}), bf16[128,80,128]{2,1,0:T(8,128)(2,1)}, u32[]{:S(2)}, u32[]{:S(2)}) async-start(bf16[128,80,128]{2,1,0:T(8,128)(2,1)} %bitcast.9), calls=%async_computation | async-start | bytes 5242880 | tf_op jit(solution)/shard_map/all_to_all | solution.py:405
  76.5 1.8 %copy-start.6 = (f32[2,12,224,128]{3,2,1,0:T(8,128)S(1)}, f32[2,12,224,128]{3,2,1,0:T(8,128)}, u32[]{:S(2)}) copy-start(f32[2,12,224,128]{3,2,1,0:T(8,128)} %copy-done.5) | copy-start | bytes 8257540

commit v4 on v3

v4 whole, which is shorter than its diff:
```python
import functools
import math

import jax
import jax.numpy as jnp
from jax import lax
from jax.experimental import pallas as pl
from jax.experimental.pallas import tpu as pltpu
from jax.sharding import PartitionSpec as P

EPSILON = 1e-05
AXES = ("dp", "seq")
LANES = 128
HALF_PAD = 16
PAD = 32
TILE = 16
F32, BF16 = jnp.float32, jnp.bfloat16
VMEM = pl.BlockSpec(memory_space=pltpu.VMEM)
SMEM = pl.BlockSpec(memory_space=pltpu.SMEM)
HBM = pl.BlockSpec(memory_space=pltpu.HBM)


def sigmoid(x):
    return 0.5 * jnp.tanh(0.5 * x) + 0.5


def left_of(lengths, place, u, frames):
    return lengths[u] - place[0] * frames


def lane(block):
    return pl.ds(pl.multiple_of(block * LANES, LANES), LANES)


def call(kernel, in_specs, out_shape, scratch, flops, limit, aliases=None, out_specs=None):
    return pl.pallas_call(
        kernel,
        in_specs=in_specs,
        out_specs=out_specs or jax.tree.map(lambda _: VMEM, out_shape),
        out_shape=out_shape,
        scratch_shapes=scratch,
        input_output_aliases=aliases or {},
        cost_estimate=pl.CostEstimate(flops=flops, bytes_accessed=8 << 20, transcendentals=0),
        compiler_params=pltpu.CompilerParams(vmem_limit_bytes=limit << 20),
    )


def shape(dims, dtype):
    return jax.ShapeDtypeStruct(dims, dtype)


def far_memory(array):
    return pltpu.with_memory_space_constraint(array, pltpu.HBM)


def depthwise(slab, weight, start, rows, order):
    total = None
    for j, row in enumerate(order):
        term = slab[pl.ds(start + 1 + j, rows), :] * weight[row]
        total = term if total is None else total + term
    return total


def edges_kernel(lengths, place, hidden, cotangent, tail, head, cells, upstream, arrived):
    groups, frames, double = hidden.shape
    width = double // 2
    copies = []
    for side, (start, near) in enumerate(((frames - PAD, frames - HALF_PAD), (0, 0))):
        for u in range(groups):
            copies.append(
                (
                    pltpu.make_async_copy(
                        hidden.at[u, start : start + PAD], cells.at[side, u], arrived.at[0, side, u]
                    ),
                    pltpu.make_async_copy(
                        cotangent.at[u, near : near + HALF_PAD],
                        upstream.at[side, u],
                        arrived.at[1, side, u],
                    ),
                )
            )
    for first, second in copies:
        first.start()
        second.start()
    n = 0
    for side, (out, start) in enumerate(((tail, frames - PAD), (head, 0))):
        for u in range(groups):
            limit = left_of(lengths, place, u, frames)
            copies[n][0].wait()
            row = start + lax.broadcasted_iota(jnp.int32, (PAD, LANES), 0)
            for cb in range(width // LANES):
                here = slice(cb * LANES, (cb + 1) * LANES)
                there = slice(width + cb * LANES, width + (cb + 1) * LANES)
                linear = cells[side, u, :, here].astype(F32)
                gate = sigmoid(cells[side, u, :, there].astype(F32))
                glu = jnp.where(row < limit, linear * gate, 0.0)
                out[u, 0:PAD, here] = glu.astype(BF16)
            copies[n][1].wait()
            out[u, PAD:, :] = upstream[side, u]
            n += 1


def gate_kernel(lengths, place, hidden, slab):
    groups, frames, double = hidden.shape
    width = double // 2
    blocks = width // LANES
    for u in range(groups):
        limit = left_of(lengths, place, u, frames)

        def channel(cb, _):
            row = lax.broadcasted_iota(jnp.int32, (frames, LANES), 0)
            linear = hidden[u, :, lane(cb)].astype(F32)
            gate = sigmoid(hidden[u, :, lane(blocks + cb)].astype(F32))
            glu = jnp.where(row < limit, linear * gate, 0.0)
            slab[u, cb, PAD : PAD + frames, :] = glu.astype(BF16).astype(F32)
            return 0

        lax.fori_loop(0, blocks, channel, 0)


def row_mean(values, width):
    mean = jnp.sum(values, axis=-1, keepdims=True) * (1.0 / width)
    return jnp.broadcast_to(mean, values.shape)


def forward_kernel(
    lengths, place, gated, left, right, weights, gain, cotangent, slab, hat, inverse, message, mean
):
    groups, blocks, length = slab.shape[:3]
    taps = weights.shape[0] - 1
    width = blocks * LANES
    half = width // 2
    frames = length - 2 * PAD
    span = frames + 2 * HALF_PAD
    chunk = span // 4
    theirs = pl.ds(pl.multiple_of((1 - (place[0] & 1)) * half, LANES), half)
    message[:, width:] = cotangent[:, theirs]
    for u in range(groups):
        limit = left_of(lengths, place, u, frames)
        base = u * span

        def channel(cb, _):
            block = slab.at[u, cb]
            block[0:PAD, :] = left[u, 0:PAD, lane(cb)].astype(F32)
            block[PAD + frames :, :] = right[u, 0:PAD, lane(cb)].astype(F32)
            weight = [weights[j : j + 1, lane(cb)] for j in range(taps)]
            for start in range(0, span, chunk):
                at = slice(base + start, base + start + chunk)
                hat[at, lane(cb)] = depthwise(block, weight, start, chunk, range(taps))
            return 0

        lax.fori_loop(0, blocks, channel, 0)
        rows = slice(base, base + span)
        total = hat[rows, 0:LANES]
        for cb in range(1, blocks):
            total = total + hat[rows, cb * LANES : (cb + 1) * LANES]
        mean[...] = row_mean(total, width)
        total = None
        for cb in range(blocks):
            centered = hat[rows, cb * LANES : (cb + 1) * LANES] - mean[...]
            total = centered * centered if total is None else total + centered * centered
        inverse[rows, :] = lax.rsqrt(row_mean(total, width) + EPSILON)

        def normalize(cb, _):
            normed = (hat[rows, lane(cb)] - mean[...]) * inverse[rows, :]
            hat[rows, lane(cb)] = normed
            pre = normed[HALF_PAD : HALF_PAD + frames] * (0.5 * gain[:, lane(cb)])
            out = pre * jnp.tanh(pre) + pre
            row = lax.broadcasted_iota(jnp.int32, (frames, LANES), 0)
            out = jnp.where(row < limit, out, 0.0).astype(BF16)
            message[u * frames : (u + 1) * frames, lane(cb)] = out
            return 0

        lax.fori_loop(0, blocks, normalize, 0)


CONTRACT_ROWS = (((0,), (0,)), ((), ()))


def product_kernel(place, near, cotangent, far, packed, out, scratch, held, sent):
    half = cotangent.shape[1] // 2
    width = 2 * half
    pairs = scratch.shape[0]
    step = 24 * pairs
    deep = scratch.shape[2] - 8
    first = lax.broadcasted_iota(jnp.int32, (pairs, 8, LANES), 1) < 4
    pick = lambda a, b: jnp.where(first, a, b)
    roll = lambda a: pltpu.roll(a, 4, 1)
    mine = pl.ds(pl.multiple_of((place[0] & 1) * half, LANES), half)

    def copy(s):
        return pltpu.make_async_copy(held.at[s], out.at[pl.ds(s * pairs, pairs)], sent.at[s])

    def rows(s, _):
        at = pl.ds(pl.multiple_of(s * step, step), step)
        result = lax.dot_general(
            near[:, at], cotangent[:, mine], CONTRACT_ROWS, preferred_element_type=F32
        ) + lax.dot_general(far[:, at], far[:, width:], CONTRACT_ROWS, preferred_element_type=F32)

        def parts(k):
            cut = result[:, k * LANES : (k + 1) * LANES].reshape(pairs, 3, 8, LANES)
            return cut[:, 0], cut[:, 1], cut[:, 2]

        for q in range(half // LANES // 2):
            a, b, c = parts(2 * q)
            d, e, f = parts(2 * q + 1)
            rb, rc, rd = roll(b), roll(c), roll(d)
            even = (a, pick(b, rd), pick(rd, roll(e)))
            odd = (pick(rb, rc), pick(rc, e), f)
            for side, tiles in enumerate((even, odd)):
                for i, tile in enumerate(tiles):
                    scratch[:, side, 24 * q + 8 * i : 24 * q + 8 * i + 8, :] = tile
        scratch[:, :, deep:, :] = packed[pl.ds(s * pairs, pairs)]
        held[s] = scratch[...].astype(BF16)
        copy(s).start()
        return 0

    lax.fori_loop(0, width // step, rows, 0)
    for s in range(width // step):
        copy(s).wait()


def backward_kernel(
    lengths, place, cotangent, left, right, w_out, hat, inverse, gain, slab, term, held, grad, sums
):
    groups, frames, width = cotangent.shape
    span = frames + 2 * HALF_PAD
    blocks = width // LANES
    for u in range(groups):
        base = u * span
        held[base : base + HALF_PAD, :] = left[u, PAD:, :]
        held[base + HALF_PAD : base + HALF_PAD + frames, :] = cotangent[u]
        held[base + HALF_PAD + frames : base + span, :] = right[u, PAD:, :]
    step = 2 * LANES

    def columns(n, _):
        at = pl.ds(pl.multiple_of(n * step, step), step)
        grad[:, at] = lax.dot_general(
            held[...], w_out[at, :], (((1,), (1,)), ((), ())), preferred_element_type=F32
        )
        return 0

    lax.fori_loop(0, width // step, columns, 0)
    sums[...] = jnp.zeros_like(sums)
    part = span // 2

    def norm(n, _):
        u, start = n // 2, (n % 2) * part
        at = pl.ds(pl.multiple_of(n * part, TILE), part)
        limit = left_of(lengths, place, u, frames)
        row = start - HALF_PAD + lax.broadcasted_iota(jnp.int32, (part, LANES), 0)
        keep = row < limit
        inside = (row >= 0) & (row < frames)
        first = second = None
        for cb in range(blocks):
            here = slice(cb * LANES, (cb + 1) * LANES)
            normed = hat[at, here]
            halved = normed * (0.5 * gain[:, here])
            turn = jnp.tanh(halved)
            gate = 0.5 * turn + 0.5
            grad_pre = jnp.where(keep, grad[at, here], 0.0) * (gate * (1.0 + halved * (1.0 - turn)))
            term_part = jnp.where(inside, grad_pre * normed, 0.0)
            sums[:, here] += jnp.sum(term_part.reshape(part // 8, 8, LANES), axis=0)
            scaled = grad_pre * gain[:, here]
            grad[at, here] = scaled
            first = scaled if first is None else first + scaled
            second = scaled * normed if second is None else second + scaled * normed
        mean = row_mean(first, width)
        slope = row_mean(second, width)
        inv = inverse[at, :]
        for cb in range(blocks):
            here = slice(cb * LANES, (cb + 1) * LANES)
            result = inv * (grad[at, here] - mean - hat[at, here] * slope)
            to = pl.ds(pl.multiple_of(start, TILE), part)
            slab[u, cb, to, :] = result.astype(BF16).astype(F32)
        return 0

    lax.fori_loop(0, 2 * groups, norm, 0)
    term[...] = jnp.sum(sums[...], axis=0, keepdims=True)


def terms_kernel(grad, slab, term, packed, square, columns, rounded, rest):
    groups, blocks, span = grad.shape[:3]
    frames = span - 2 * HALF_PAD
    taps = 31
    square[...] = jnp.zeros_like(square)

    def channel(cb, _):
        for r in range(8):
            chosen = [j for j in range(r, taps, 8)]
            totals = [None] * len(chosen)
            for u in range(groups):
                for i in range(frames // 8):
                    value = grad[u, cb, HALF_PAD + 8 * i : HALF_PAD + 8 * i + 8, :]
                    for n, j in enumerate(chosen):
                        place = PAD - taps // 2 + 8 * i + j
                        part = value * slab[u, cb, pl.ds(place, 8), :]
                        totals[n] = part if totals[n] is None else totals[n] + part
            for n, j in enumerate(chosen):
                square[j : j + 1, :] = jnp.sum(totals[n], axis=0, keepdims=True)
        square[taps : taps + 1, :] = term[:, lane(cb)]
        columns[lane(cb), :] = square[...].T
        return 0

    lax.fori_loop(0, blocks, channel, 0)
    quarter = columns.shape[0] // 4
    total = columns[pl.ds(0, quarter, stride=4), :]
    for m in range(1, 4):
        total = total + pltpu.roll(columns[pl.ds(m, quarter, stride=4), :], 32 * m, 1)
    high = total.astype(BF16).astype(F32)
    rounded[0:quarter, :] = high
    rest[8 : 8 + quarter, :] = total - high
    row = lax.broadcasted_iota(jnp.int32, (8, LANES), 0)
    pairs, sides = packed.shape[:2]
    for d in range(pairs * sides):
        upper = rounded[3 * d : 3 * d + 8, :]
        lower = rest[3 * d + 5 : 3 * d + 13, :]
        tile = jnp.where(row < 3, upper, jnp.where(row < 6, lower, 0.0))
        packed[d // 2, d % 2] = tile


def input_kernel(lengths, place, grad, hidden, weights, out):
    groups, frames, _ = hidden.shape
    blocks = grad.shape[1]
    taps = weights.shape[0] - 1
    chunk = 64
    for u in range(groups):
        limit = left_of(lengths, place, u, frames)

        def channel(cb, _):
            block = grad.at[u, cb]
            weight = [weights[j : j + 1, lane(cb)] for j in range(taps)]
            for start in range(0, frames, chunk):
                at = slice(start, start + chunk)
                total = depthwise(block, weight, start, chunk, range(taps - 1, -1, -1))
                row = start + lax.broadcasted_iota(jnp.int32, (chunk, LANES), 0)
                total = jnp.where(row < limit, total, 0.0)
                linear = hidden[u, at, lane(cb)].astype(F32)
                gate = sigmoid(hidden[u, at, lane(blocks + cb)].astype(F32))
                opened = total * gate
                out[u, at, lane(cb)] = opened.astype(BF16)
                out[u, at, lane(blocks + cb)] = (opened * linear * (1.0 - gate)).astype(BF16)
            return 0

        lax.fori_loop(0, blocks, channel, 0)


def sum_kernel(factor, got, out, taps_out, gain_out, total, held, arrived):
    own = out.shape[0]
    slots, step, _, tall, _ = held.shape

    def copy(i):
        return pltpu.make_async_copy(got.at[pl.ds(i * step, step)], held.at[i], arrived.at[i])

    for i in range(slots):
        copy(i).start()
    total[...] = jnp.zeros_like(total)

    def add(i, _):
        copy(i).wait()
        for k in range(0, step, 4):
            total[...] += jnp.sum(held[i, k : k + 4].astype(F32), axis=0)
        return 0

    lax.fori_loop(0, slots, add, 0)
    deep = tall - 8
    blocks = deep // own
    for side in range(2):
        for k in range(blocks):
            at = (side * blocks + k) * LANES
            out[:, at : at + LANES] = total[side, own * k : own * (k + 1), :] * factor
    both = total[0, deep:, :] + total[1, deep:, :]
    small = (both[0:3] + both[3:6]) * factor
    taps = taps_out.shape[1]
    spot = lax.broadcasted_iota(jnp.int32, (1, LANES), 1)
    gains = jnp.zeros((1, LANES), F32)
    for r in range(3):
        for m in range(4):
            c = 4 * r + m
            turned = pltpu.roll(small[r : r + 1, :], (LANES - 32 * m) % LANES, 1)
            taps_out[c : c + 1, :] = turned[:, :taps]
            gains = jnp.where(spot == c, pltpu.roll(turned, (c - taps) % LANES, 1), gains)
    gain_out[...] = gains[:, :own]


def local(hidden, cotangent, lengths, kernel, conv_gain, w_out):
    groups, frames, double = hidden.shape
    width = double // 2
    half = width // 2
    blocks = width // LANES
    taps = kernel.shape[1]
    seq_count = lax.axis_size("seq")
    devices = lax.axis_size("dp") * seq_count
    own = width // devices
    rows = groups * frames
    span = frames + 2 * HALF_PAD
    length = frames + 2 * PAD
    deep = own * half // LANES
    ends = seq_count - 1
    swap = [(i, i ^ 1) for i in range(seq_count)]
    place = lax.axis_index("seq")
    conv_flops = 2 * taps * rows * width

    spot = place.reshape(1)
    flat = cotangent.reshape(rows, width)
    tail, head = call(
        edges_kernel,
        [SMEM, SMEM, HBM, HBM],
        [shape((groups, PAD + HALF_PAD, width), BF16)] * 2,
        [
            pltpu.VMEM((2, groups, PAD, double), BF16),
            pltpu.VMEM((2, groups, HALF_PAD, width), BF16),
            pltpu.SemaphoreType.DMA((2, 2, groups)),
        ],
        1 << 20,
        4,
    )(lengths, spot, far_memory(hidden), far_memory(cotangent))
    left = lax.ppermute(tail, "seq", [(i, i + 1) for i in range(ends)])
    right = lax.ppermute(head, "seq", [(i + 1, i) for i in range(ends)])
    gated = call(
        gate_kernel, [SMEM, SMEM, VMEM], shape((groups, blocks, length, LANES), F32), [], 8 << 20, 4
    )(lengths, spot, hidden)
    weights = jnp.concatenate([kernel, jnp.zeros((width, 1), F32)], axis=1).T
    gain = conv_gain.reshape(1, width)
    slab, hat, inverse, message = call(
        forward_kernel,
        [SMEM, SMEM] + [VMEM] * 6,
        [
            shape((groups, blocks, length, LANES), F32),
            shape((groups * span, width), F32),
            shape((groups * span, LANES), F32),
            shape((rows, width + half), BF16),
        ],
        [pltpu.VMEM((span, LANES), F32)],
        conv_flops,
        4,
        {2: 0},
    )(lengths, spot, gated, left, right, weights, gain, flat)
    far = lax.ppermute(message, "seq", swap)
    grad, term_conv = call(
        backward_kernel,
        [SMEM, SMEM] + [VMEM] * 7,
        [shape((groups, blocks, span, LANES), F32), shape((1, width), F32)],
        [
            pltpu.VMEM((groups * span, width), BF16),
            pltpu.VMEM((groups * span, width), F32),
            pltpu.VMEM((8, width), F32),
        ],
        2 * rows * width * width,
        10,
    )(lengths, spot, cotangent, left, right, w_out, hat, inverse, gain)
    packed = call(
        terms_kernel,
        [VMEM] * 3,
        shape((devices // 2, 2, 8, LANES), F32),
        [
            pltpu.VMEM((LANES, LANES), F32),
            pltpu.VMEM((width, LANES), F32),
            pltpu.VMEM((width // 4 + 8, LANES), F32),
            pltpu.VMEM((width // 4 + 16, LANES), F32),
        ],
        conv_flops,
        6,
    )(grad, slab, term_conv)
    steps = devices // 32
    pieces = call(
        product_kernel,
        [SMEM] + [VMEM] * 4,
        pltpu.HBM((devices // 2, 2, deep + 8, LANES), BF16),
        [
            pltpu.VMEM((16, 2, deep + 8, LANES), F32),
            pltpu.VMEM((steps, 16, 2, deep + 8, LANES), BF16),
            pltpu.SemaphoreType.DMA((steps,)),
        ],
        4 * rows * width * half,
        10,
        out_specs=HBM,
    )(spot, message, flat, far, packed)
    got = lax.all_to_all(pieces.reshape(devices, deep + 8, LANES), AXES, 0, 0, tiled=True)
    grad_hidden = call(
        input_kernel,
        [SMEM, SMEM] + [VMEM] * 3,
        shape((groups, frames, double), BF16),
        [],
        conv_flops,
        4,
    )(lengths, spot, grad, hidden, weights)

    factor = 1.0 / math.sqrt(groups * lax.axis_size("dp") * frames * seq_count)
    slots = 4
    grad_w, grad_kernel, grad_gain = call(
        functools.partial(sum_kernel, factor),
        [HBM],
        [shape((own, width), F32), shape((own, taps), F32), shape((1, own), F32)],
        [
            pltpu.VMEM((2, deep + 8, LANES), F32),
            pltpu.VMEM((slots, devices // 2 // slots, 2, deep + 8, LANES), BF16),
            pltpu.SemaphoreType.DMA((slots,)),
        ],
        1 << 20,
        6,
    )(far_memory(got.reshape(devices // 2, 2, deep + 8, LANES)))
    return grad_hidden, grad_w, grad_kernel, grad_gain.reshape(own)


def solution(mesh):
    in_specs = (P("dp", "seq", None), P("dp", "seq", None), P("dp"), P(), P(), P())
    out_specs = (P("dp", "seq", None), P(AXES, None), P(AXES, None), P(AXES))
    return jax.shard_map(local, mesh=mesh, in_specs=in_specs, out_specs=out_specs, check_vma=False)
```

time: 116 us -> 93.2 us (0.80)
  local copies, waits for them, and re-layouts: 16.7 us -> 2.63 us
  Pallas kernels: 47.4 us -> 41.4 us
  other arithmetic: 1.97 us -> 0 us
    unnamed x38 -> x18, local copies, waits for them, and re-layouts: 16.7 us -> 2.6 us
    pallas_call x7, Pallas kernels: 40.7 us -> 33.8 us  [the longest x1 8.39 us: local(): call(forward_kernel, [SMEM, SMEM] + [VMEM] * 6, [shape((groups, blocks, l...]
    select_n x1 -> x0, other arithmetic: 1.31 us -> none  [local(): sent = jnp.where(core == 0, flat[:, half:], flat[:, :half])]
  transfers between devices with their start and end apart: 5 -> 4, of which waited for: 2 -> 2; matrix products, arithmetic and copies ran while one was open for 1% -> 0% of each run, Pallas kernels for 22% -> 26%
where the time goes in v4:
time: 93.2 us; the launch traced here: 92.9 us
  Pallas kernels  41.4 us (44%)
  waiting for transfers between devices  30.1 us (32%)
  starting transfers between devices  17.9 us (19%)
  local copies, waits for them, and re-layouts  2.63 us (3%)
    all_to_all x1, waiting for transfers between devices, local(): lax.all_to_all(pieces.reshape(devices, deep + 8, LANES), AXES, 0, 0, tile...  25.8 us
    all_to_all x1, starting transfers between devices, local(): lax.all_to_all(pieces.reshape(devices, deep + 8, LANES), AXES, 0, 0, tile...  11 us
    pallas_call x1, Pallas kernels, local(): call(forward_kernel, [SMEM, SMEM] + [VMEM] * 6, [shape((groups, blocks, l...  8.39 us
    pallas_call x1, Pallas kernels, local(): call(input_kernel, [SMEM, SMEM] + [VMEM] * 3, shape((groups, frames, doub...  8.22 us
    pallas_call x1, Pallas kernels, local(): call(terms_kernel, [VMEM] * 3, shape((devices // 2, 2, 8, LANES), F32), [...  7.58 us
    pallas_call x1, Pallas kernels, local(): call(backward_kernel, [SMEM, SMEM] + [VMEM] * 7, [shape((groups, blocks,...  6.87 us
    ppermute x1, starting transfers between devices, local(): left = lax.ppermute(tail, 'seq', [(i, i + 1) for i in range(ends)])  4.92 us
    ppermute x1, waiting for transfers between devices, local(): right = lax.ppermute(head, 'seq', [(i + 1, i) for i in range(ends)])  4.32 us
  transfers between devices with their start and end apart: 4, of which 2 were waited for; matrix products, arithmetic and copies ran while one was open for 0% of the time, Pallas kernels for 26%

profile of v4, /device:TPU:1, one launch (start us, length us, event | category | flops | bytes accessed | tf_op | source)
XLA Modules:
  0.0 92.9 jit_solution(13496070159359032773)
XLA Ops:
  0.6 0.0 copy-start
  0.7 0.8 copy-done.5
  1.5 2.0 %shard_map.93 = (bf16[2,48,1536]{2,1,0:T(8,128)(2,1)S(1)}, bf16[2,48,1536]{2,1,0:T(8,128)(2,1)S(1)}) custom-call(s32[2]{0:T(128)S(1)} %copy-done.5, s32[1]{0:T(128)} %bitcast.place, bf16[2,192,3072]{2,1,0:T(8,128)(2,1)} %hidden.5, bf16[2,192,1536]{2,1,0:T(8,128)(2,1)} %cotangent.3), custom_call_target="tpu_custom_call" | custom-call | flops 1048576 | bytes 8388608 | tf_op jit(solution)/shard_map/pallas_call | solution.py:406
  3.4 4.9 %collective-permute-start = (bf16[2,48,1536]{2,1,0:T(8,128)(2,1)S(1)}, bf16[2,48,1536]{2,1,0:T(8,128)(2,1)S(1)}, u32[]{:S(2)}, u32[]{:S(2)}) collective-permute-start(bf16[2,48,1536]{2,1,0:T(8,128)(2,1)S(1)} %get-tuple-element.15), channel_id=1, source_target_pairs={{0,1},{1,2},{2,3},{3,4},{4,5},{5,6},{6,7},{7,8},{8,9},{9,10},{10,1... | collective-permute-start | bytes 884744 | tf_op jit(solution)/shard_map/ppermute | solution.py:418
  8.4 1.9 %collective-permute-start.1 = (bf16[2,48,1536]{2,1,0:T(8,128)(2,1)S(1)}, bf16[2,48,1536]{2,1,0:T(8,128)(2,1)S(1)}, u32[]{:S(2)}, u32[]{:S(2)}) collective-permute-start(bf16[2,48,1536]{2,1,0:T(8,128)(2,1)S(1)} %get-tuple-element.16), channel_id=1, source_target_pairs={{1,0},{2,1},{3,2},{4,3},{5,4},{6,5},{7,6},{8,7},{9,8},{10,9},{11,1... | collective-permute-start | bytes 884744 | tf_op jit(solution)/shard_map/ppermute | solution.py:419
  10.3 0.0 copy-done.8
  10.3 0.0 copy-start.7
  10.3 0.0 copy-start.1
  10.4 1.7 %shard_map.94.gated = f32[2,12,256,128]{3,2,1,0:T(8,128)S(1)} custom-call(s32[2]{0:T(128)S(1)} %copy-done.6, s32[1]{0:T(128)} %bitcast.place, bf16[2,192,3072]{2,1,0:T(8,128)(2,1)S(1)} %copy-done), custom_call_target="tpu_custom_call" | custom-call | flops 8388608 | bytes 8388608 | tf_op jit(solution)/shard_map/pallas_call | solution.py:420
  12.1 0.0 copy-start.4
  12.1 0.0 collective-permute-done.left
  12.1 4.3 %collective-permute-done.1.right = bf16[2,48,1536]{2,1,0:T(8,128)(2,1)S(1)} collective-permute-done((bf16[2,48,1536]{2,1,0:T(8,128)(2,1)S(1)}, bf16[2,48,1536]{2,1,0:T(8,128)(2,1)S(1)}, u32[]{:S(2)}, u32[]{:S(2)}) %collective-permute-start.1) | collective-permute-done | bytes 294944 | tf_op jit(solution)/shard_map/ppermute | solution.py:419
  16.4 8.4 %shard_map.95 = (f32[2,12,256,128]{3,2,1,0:T(8,128)S(1)}, f32[448,1536]{1,0:T(8,128)S(1)}, f32[448,128]{1,0:T(8,128)S(1)}, bf16[384,2304]{1,0:T(8,128)(2,1)S(1)}) custom-call(s32[2]{0:T(128)S(1)} %copy-done.6, s32[1]{0:T(128)} %bitcast.place, f32[2,12,256,128]{3,2,1,0:T(8,128)S(1)} %shard_map.94.gated, ...), custom_call_target="tpu_custom_call", output_to_operand_aliasing={{0}: (2, {})} | custom-call | flops 36569088 | bytes 8388608 | tf_op jit(solution)/shard_map/pallas_call | solution.py:425
  24.8 0.1 collective-permute-start.2
  24.9 0.0 copy-done.4
  24.9 6.9 %shard_map.96 = (f32[2,12,224,128]{3,2,1,0:T(8,128)S(1)}, f32[1,1536]{1,0:T(1,128)S(1)}) custom-call(s32[2]{0:T(128)S(1)} %copy-done.6, s32[1]{0:T(128)} %bitcast.place, bf16[2,192,1536]{2,1,0:T(8,128)(2,1)S(1)} %copy-done.1, bf16[2,48,1536]{2,1,0:T(8,128)(2,1)S(1)} %collective-permute-done.left, bf16[2,48,1536]{2,1,0:T(8,128)(2,1)S(1)} %collective-permute-done.1.right, ...), custom_call_target="tpu_custom_call" | custom-call | flops 1811939328 | bytes 8388608 | tf_op jit(solution)/shard_map/pallas_call | solution.py:440
  31.8 7.6 %shard_map.98.packed = f32[64,2,8,128]{3,2,1,0:T(8,128)S(1)} custom-call(f32[2,12,224,128]{3,2,1,0:T(8,128)S(1)} %get-tuple-element.19.grad, f32[2,12,256,128]{3,2,1,0:T(8,128)S(1)} %get-tuple-element.21.slab, f32[1,1536]{1,0:T(1,128)S(1)} %get-tuple-element.22.term), custom_call_target="tpu_custom_call" | custom-call | flops 36569088 | bytes 8388608 | tf_op jit(solution)/shard_map/pallas_call | solution.py:452
  39.4 0.0 collective-permute-done.2.far
  39.4 4.2 %shard_map.99 = bf16[64,2,80,128]{3,2,1,0:T(8,128)(2,1)} custom-call(s32[1]{0:T(128)} %bitcast.place, bf16[384,2304]{1,0:T(8,128)(2,1)S(1)} %get-tuple-element.20.near, bf16[384,1536]{1,0:T(8,128)(2,1)S(1)} %bitcast.8, bf16[384,2304]{1,0:T(8,128)(2,1)S(1)} %collective-permute-done.2.far, f32[64,2,8,128]{3,2,1,0:T(8,128)S(1)} %shard_map.98.packed), custom_call_target="tpu_custom_call" | custom-call | flops 1811939328 | bytes 8388608 | tf_op jit(solution)/shard_map/pallas_call | solution.py:466
  43.6 11.0 %all-to-all-start = ((bf16[128,80,128]{2,1,0:T(8,128)(2,1)}), bf16[128,80,128]{2,1,0:T(8,128)(2,1)}, u32[]{:S(2)}, u32[]{:S(2)}) async-start(bf16[128,80,128]{2,1,0:T(8,128)(2,1)} %bitcast.9), calls=%async_computation | async-start | bytes 5242880 | tf_op jit(solution)/shard_map/all_to_all | solution.py:479
  54.6 1.8 %copy-done.3 = f32[2,12,224,128]{3,2,1,0:T(8,128)S(1)} copy-done((f32[2,12,224,128]{3,2,1,0:T(8,128)S(1)}, f32[2,12,224,128]{3,2,1,0:T(8,128)}, u32[]{:S(2)}) %copy-start.3) | copy-done | bytes 2752536
  56.4 8.2 %shard_map.97 = bf16[2,192,3072]{2,1,0:T(8,128)(2,1)} custom-call(s32[2]{0:T(128)S(1)} %copy-done.6, s32[1]{0:T(128)} %bitcast.place, f32[2,12,224,128]{3,2,1,0:T(8,128)S(1)} %copy-done.3, bf16[2,192,3072]{2,1,0:T(8,128)(2,1)S(1)} %copy-done, f32[32,1536]{1,0:T(8,128)S(1)} %pad_bitcast_fusion.weights), custom_call_target="tpu_custom_call" | custom-call | flops 36569088 | bytes 8388608 | tf_op jit(solution)/shard_map/pallas_call | solution.py:480
  64.6 25.8 %all-to-all-done = bf16[128,80,128]{2,1,0:T(8,128)(2,1)} async-done(((bf16[128,80,128]{2,1,0:T(8,128)(2,1)}), bf16[128,80,128]{2,1,0:T(8,128)(2,1)}, u32[]{:S(2)}, u32[]{:S(2)}) %all-to-all-start) | async-done | bytes 2621472 | tf_op jit(solution)/shard_map/all_to_all | solution.py:479
  90.3 2.5 %shard_map.100 = (f32[12,1536]{1,0:T(8,128)}, f32[12,31]{1,0:T(8,128)}, f32[1,12]{1,0:T(1,128)}) custom-call(bf16[64,2,80,128]{3,2,1,0:T(8,128)(2,1)} %bitcast.4.got), custom_call_target="tpu_custom_call" | custom-call | flops 1048576 | bytes 8388608 | tf_op jit(solution)/shard_map/pallas_call | solution.py:491
  (12 shorter events, 0.0 us)
Async XLA Ops:
  0.6 9.7 %copy-start = (bf16[2,192,3072]{2,1,0:T(8,128)(2,1)S(1)}, bf16[2,192,3072]{2,1,0:T(8,128)(2,1)}, u32[]{:S(2)}) copy-start(bf16[2,192,3072]{2,1,0:T(8,128)(2,1)} %hidden.5) | copy-start | bytes 7077892
  0.6 0.8 copy-start.5
  1.5 8.8 %copy-start.8 = (f32[1536]{0:T(1024)S(1)}, f32[1536]{0:T(1024)}, u32[]{:S(2)}) copy-start(f32[1536]{0:T(1024)} %param.10) | copy-start | bytes 18436
  1.5 8.9 %copy-start.6 = (s32[2]{0:T(128)S(1)}, s32[2]{0:T(128)}, u32[]{:S(2)}) copy-start(s32[2]{0:T(128)} %lengths.9) | copy-start | bytes 28
  3.4 8.6 %collective-permute-start = (bf16[2,48,1536]{2,1,0:T(8,128)(2,1)S(1)}, bf16[2,48,1536]{2,1,0:T(8,128)(2,1)S(1)}, u32[]{:S(2)}, u32[]{:S(2)}) collective-permute-start(bf16[2,48,1536]{2,1,0:T(8,128)(2,1)S(1)} %get-tuple-element.15), channel_id=1, source_target_pairs={{0,1},{1,2},{2,3},{3,4},{4,5},{5,6},{6,7},{7,8},{8,9},{9,10},{10,1... | collective-permute-start | bytes 884744 | tf_op jit(solution)/shard_map/ppermute | solution.py:418
  8.4 8.0 %collective-permute-start.1 = (bf16[2,48,1536]{2,1,0:T(8,128)(2,1)S(1)}, bf16[2,48,1536]{2,1,0:T(8,128)(2,1)S(1)}, u32[]{:S(2)}, u32[]{:S(2)}) collective-permute-start(bf16[2,48,1536]{2,1,0:T(8,128)(2,1)S(1)} %get-tuple-element.16), channel_id=1, source_target_pairs={{1,0},{2,1},{3,2},{4,3},{5,4},{6,5},{7,6},{8,7},{9,8},{10,9},{11,1... | collective-permute-start | bytes 884744 | tf_op jit(solution)/shard_map/ppermute | solution.py:419
  10.3 1.7 %copy-start.7 = (f32[1536,31]{0,1:T(8,128)S(1)}, f32[1536,31]{0,1:T(8,128)}, u32[]{:S(2)}) copy-start(f32[1536,31]{0,1:T(8,128)} %param.9) | copy-start | bytes 571396
  10.3 6.1 %copy-start.1 = (bf16[2,192,1536]{2,1,0:T(8,128)(2,1)S(1)}, bf16[2,192,1536]{2,1,0:T(8,128)(2,1)}, u32[]{:S(2)}) copy-start(bf16[2,192,1536]{2,1,0:T(8,128)(2,1)} %cotangent.3) | copy-start | bytes 3538948
  12.1 12.8 %copy-start.4 = (bf16[1536,1536]{1,0:T(8,128)(2,1)S(1)}, bf16[1536,1536]{1,0:T(8,128)(2,1)}, u32[]{:S(2)}) copy-start(bf16[1536,1536]{1,0:T(8,128)(2,1)} %w_out.1) | copy-start | bytes 14155780
  24.8 14.6 %collective-permute-start.2 = (bf16[384,2304]{1,0:T(8,128)(2,1)S(1)}, bf16[384,2304]{1,0:T(8,128)(2,1)S(1)}, u32[]{:S(2)}, u32[]{:S(2)}) collective-permute-start(bf16[384,2304]{1,0:T(8,128)(2,1)S(1)} %get-tuple-element.20.near), channel_id=1, source_target_pairs={{0,1},{1,0},{2,3},{3,2},{4,5},{5,4},{6,7},{7,6},{8,9},{9,8},{10,11... | collective-permute-start | bytes 5308424 | tf_op jit(solution)/shard_map/ppermute | solution.py:439
  31.8 7.6 %copy-start.2 = (f32[2,12,224,128]{3,2,1,0:T(8,128)}, f32[2,12,224,128]{3,2,1,0:T(8,128)S(1)}, u32[]{:S(2)}) copy-start(f32[2,12,224,128]{3,2,1,0:T(8,128)S(1)} %get-tuple-element.19.grad) | copy-start | bytes 8257540
  43.6 46.8 %all-to-all-start = ((bf16[128,80,128]{2,1,0:T(8,128)(2,1)}), bf16[128,80,128]{2,1,0:T(8,128)(2,1)}, u32[]{:S(2)}, u32[]{:S(2)}) async-start(bf16[128,80,128]{2,1,0:T(8,128)(2,1)} %bitcast.9), calls=%async_computation | async-start | bytes 5242880 | tf_op jit(solution)/shard_map/all_to_all | solution.py:479
  54.6 1.8 %copy-start.3 = (f32[2,12,224,128]{3,2,1,0:T(8,128)S(1)}, f32[2,12,224,128]{3,2,1,0:T(8,128)}, u32[]{:S(2)}) copy-start(f32[2,12,224,128]{3,2,1,0:T(8,128)} %copy-done.2) | copy-start | bytes 8257540

commit v5 on v4

--- a/solution.py
+++ b/solution.py
@@ -61,7 +61,7 @@
     return total
 
 
-def edges_kernel(lengths, place, hidden, cotangent, tail, head, cells, upstream, arrived):
+def edges_kernel(hidden, cotangent, tail, head, cells, upstream, arrived):
     groups, frames, double = hidden.shape
     width = double // 2
     copies = []
@@ -83,39 +83,66 @@
         first.start()
         second.start()
     n = 0
-    for side, (out, start) in enumerate(((tail, frames - PAD), (head, 0))):
+    for side, out in enumerate((tail, head)):
         for u in range(groups):
-            limit = left_of(lengths, place, u, frames)
             copies[n][0].wait()
-            row = start + lax.broadcasted_iota(jnp.int32, (PAD, LANES), 0)
             for cb in range(width // LANES):
                 here = slice(cb * LANES, (cb + 1) * LANES)
                 there = slice(width + cb * LANES, width + (cb + 1) * LANES)
                 linear = cells[side, u, :, here].astype(F32)
                 gate = sigmoid(cells[side, u, :, there].astype(F32))
-                glu = jnp.where(row < limit, linear * gate, 0.0)
-                out[u, 0:PAD, here] = glu.astype(BF16)
+                out[u, 0:PAD, here] = (linear * gate).astype(BF16)
             copies[n][1].wait()
             out[u, PAD:, :] = upstream[side, u]
             n += 1
 
 
-def gate_kernel(lengths, place, hidden, slab):
+CONTRACT_COLUMNS = (((1,), (1,)), ((), ()))
+
+
+def gate_kernel(
+    lengths, place, hidden, weights, cotangent, source, slab, hat, grad, w_out, arrived
+):
     groups, frames, double = hidden.shape
+    taps = weights.shape[0] - 1
     width = double // 2
     blocks = width // LANES
-    for u in range(groups):
-        limit = left_of(lengths, place, u, frames)
-
-        def channel(cb, _):
-            row = lax.broadcasted_iota(jnp.int32, (frames, LANES), 0)
-            linear = hidden[u, :, lane(cb)].astype(F32)
-            gate = sigmoid(hidden[u, :, lane(blocks + cb)].astype(F32))
-            glu = jnp.where(row < limit, linear * gate, 0.0)
-            slab[u, cb, PAD : PAD + frames, :] = glu.astype(BF16).astype(F32)
-            return 0
-
-        lax.fori_loop(0, blocks, channel, 0)
+    span = frames + 2 * HALF_PAD
+    chunk = (span - 2 * PAD) // 2
+
+    def copy(n):
+        at = pl.ds(pl.multiple_of(n * 2 * LANES, 2 * LANES), 2 * LANES)
+        return pltpu.make_async_copy(source.at[at], w_out.at[at], arrived.at[n])
+
+    for n in range(blocks // 2):
+        copy(n).start()
+
+    def pair(n, _):
+        at = pl.ds(pl.multiple_of(n * 2 * LANES, 2 * LANES), 2 * LANES)
+        copy(n).wait()
+        swish = lax.dot_general(
+            cotangent[...], w_out[at, :], CONTRACT_COLUMNS, preferred_element_type=F32
+        )
+        for u in range(groups):
+            limit = left_of(lengths, place, u, frames)
+            base = u * span
+            for cb in (2 * n, 2 * n + 1):
+                row = lax.broadcasted_iota(jnp.int32, (frames, LANES), 0)
+                linear = hidden[u, :, lane(cb)].astype(F32)
+                gate = sigmoid(hidden[u, :, lane(blocks + cb)].astype(F32))
+                glu = jnp.where(row < limit, linear * gate, 0.0)
+                block = slab.at[u, cb]
+                block[PAD : PAD + frames, :] = glu.astype(BF16).astype(F32)
+                weight = [weights[j : j + 1, lane(cb)] for j in range(taps)]
+                for start in range(PAD, span - PAD, chunk):
+                    to = slice(base + start, base + start + chunk)
+                    hat[to, lane(cb)] = depthwise(block, weight, start, chunk, range(taps))
+        for u in range(groups):
+            to = u * span + HALF_PAD
+            grad[to : to + frames, at] = swish[u * frames : (u + 1) * frames]
+        return 0
+
+    lax.fori_loop(0, blocks // 2, pair, 0)
 
 
 def row_mean(values, width):
@@ -124,7 +151,24 @@
 
 
 def forward_kernel(
-    lengths, place, gated, left, right, weights, gain, cotangent, slab, hat, inverse, message, mean
+    lengths,
+    place,
+    gated,
+    inner,
+    swish,
+    left,
+    right,
+    weights,
+    gain,
+    cotangent,
+    w_out,
+    slab,
+    hat,
+    grad,
+    inverse,
+    message,
+    mean,
+    held,
 ):
     groups, blocks, length = slab.shape[:3]
     taps = weights.shape[0] - 1
@@ -132,24 +176,44 @@
     half = width // 2
     frames = length - 2 * PAD
     span = frames + 2 * HALF_PAD
-    chunk = span // 4
     theirs = pl.ds(pl.multiple_of((1 - (place[0] & 1)) * half, LANES), half)
     message[:, width:] = cotangent[:, theirs]
     for u in range(groups):
+        held[2 * u * HALF_PAD : (2 * u + 1) * HALF_PAD, :] = left[u, PAD:, :]
+        held[(2 * u + 1) * HALF_PAD : (2 * u + 2) * HALF_PAD, :] = right[u, PAD:, :]
+
+    def pair(n, _):
+        at = pl.ds(pl.multiple_of(n * 2 * LANES, 2 * LANES), 2 * LANES)
+        result = lax.dot_general(
+            held[...], w_out[at, :], CONTRACT_COLUMNS, preferred_element_type=F32
+        )
+        row = lax.broadcasted_iota(jnp.int32, (PAD, LANES), 0)
+        for u in range(groups):
+            limit = left_of(lengths, place, u, frames)
+            base = u * span
+            for cb in (2 * n, 2 * n + 1):
+                block = slab.at[u, cb]
+                before = left[u, 0:PAD, lane(cb)].astype(F32)
+                after = right[u, 0:PAD, lane(cb)].astype(F32)
+                block[0:PAD, :] = jnp.where(row - PAD < limit, before, 0.0)
+                block[PAD + frames :, :] = jnp.where(row + frames < limit, after, 0.0)
+                weight = [weights[j : j + 1, lane(cb)] for j in range(taps)]
+                for start in (0, span - PAD):
+                    to = slice(base + start, base + start + PAD)
+                    hat[to, lane(cb)] = depthwise(block, weight, start, PAD, range(taps))
+        for u in range(groups):
+            base = u * span
+            near = 2 * u * HALF_PAD
+            grad[base : base + HALF_PAD, at] = result[near : near + HALF_PAD]
+            grad[base + span - HALF_PAD : base + span, at] = result[
+                near + HALF_PAD : near + 2 * HALF_PAD
+            ]
+        return 0
+
+    lax.fori_loop(0, blocks // 2, pair, 0)
+    for u in range(groups):
         limit = left_of(lengths, place, u, frames)
         base = u * span
-
-        def channel(cb, _):
-            block = slab.at[u, cb]
-            block[0:PAD, :] = left[u, 0:PAD, lane(cb)].astype(F32)
-            block[PAD + frames :, :] = right[u, 0:PAD, lane(cb)].astype(F32)
-            weight = [weights[j : j + 1, lane(cb)] for j in range(taps)]
-            for start in range(0, span, chunk):
-                at = slice(base + start, base + start + chunk)
-                hat[at, lane(cb)] = depthwise(block, weight, start, chunk, range(taps))
-            return 0
-
-        lax.fori_loop(0, blocks, channel, 0)
         rows = slice(base, base + span)
         total = hat[rows, 0:LANES]
         for cb in range(1, blocks):
@@ -220,27 +284,10 @@
         copy(s).wait()
 
 
-def backward_kernel(
-    lengths, place, cotangent, left, right, w_out, hat, inverse, gain, slab, term, held, grad, sums
-):
-    groups, frames, width = cotangent.shape
-    span = frames + 2 * HALF_PAD
-    blocks = width // LANES
-    for u in range(groups):
-        base = u * span
-        held[base : base + HALF_PAD, :] = left[u, PAD:, :]
-        held[base + HALF_PAD : base + HALF_PAD + frames, :] = cotangent[u]
-        held[base + HALF_PAD + frames : base + span, :] = right[u, PAD:, :]
-    step = 2 * LANES
-
-    def columns(n, _):
-        at = pl.ds(pl.multiple_of(n * step, step), step)
-        grad[:, at] = lax.dot_general(
-            held[...], w_out[at, :], (((1,), (1,)), ((), ())), preferred_element_type=F32
-        )
-        return 0
-
-    lax.fori_loop(0, width // step, columns, 0)
+def backward_kernel(lengths, place, grad, hat, inverse, gain, slab, term, work, sums):
+    groups, blocks, span = slab.shape[:3]
+    width = blocks * LANES
+    frames = span - 2 * HALF_PAD
     sums[...] = jnp.zeros_like(sums)
     part = span // 2
 
@@ -262,7 +309,7 @@
             term_part = jnp.where(inside, grad_pre * normed, 0.0)
             sums[:, here] += jnp.sum(term_part.reshape(part // 8, 8, LANES), axis=0)
             scaled = grad_pre * gain[:, here]
-            grad[at, here] = scaled
+            work[at, here] = scaled
             first = scaled if first is None else first + scaled
             second = scaled * normed if second is None else second + scaled * normed
         mean = row_mean(first, width)
@@ -270,7 +317,7 @@
         inv = inverse[at, :]
         for cb in range(blocks):
             here = slice(cb * LANES, (cb + 1) * LANES)
-            result = inv * (grad[at, here] - mean - hat[at, here] * slope)
+            result = inv * (work[at, here] - mean - hat[at, here] * slope)
             to = pl.ds(pl.multiple_of(start, TILE), part)
             slab[u, cb, to, :] = result.astype(BF16).astype(F32)
         return 0
@@ -405,7 +452,7 @@
     flat = cotangent.reshape(rows, width)
     tail, head = call(
         edges_kernel,
-        [SMEM, SMEM, HBM, HBM],
+        [HBM, HBM],
         [shape((groups, PAD + HALF_PAD, width), BF16)] * 2,
         [
             pltpu.VMEM((2, groups, PAD, double), BF16),
@@ -414,41 +461,45 @@
         ],
         1 << 20,
         4,
-    )(lengths, spot, far_memory(hidden), far_memory(cotangent))
+    )(far_memory(hidden), far_memory(cotangent))
     left = lax.ppermute(tail, "seq", [(i, i + 1) for i in range(ends)])
     right = lax.ppermute(head, "seq", [(i + 1, i) for i in range(ends)])
-    gated = call(
-        gate_kernel, [SMEM, SMEM, VMEM], shape((groups, blocks, length, LANES), F32), [], 8 << 20, 4
-    )(lengths, spot, hidden)
     weights = jnp.concatenate([kernel, jnp.zeros((width, 1), F32)], axis=1).T
     gain = conv_gain.reshape(1, width)
-    slab, hat, inverse, message = call(
+    slab_shape = shape((groups, blocks, length, LANES), F32)
+    wide_shape = shape((groups * span, width), F32)
+    gated, inner, swish, w_near = call(
+        gate_kernel,
+        [SMEM, SMEM] + [VMEM] * 3 + [HBM],
+        [slab_shape, wide_shape, wide_shape, shape((width, width), BF16)],
+        [pltpu.SemaphoreType.DMA((blocks // 2,))],
+        conv_flops,
+        4,
+    )(lengths, spot, hidden, weights, flat, far_memory(w_out))
+    slab, hat, grad_swish, inverse, message = call(
         forward_kernel,
-        [SMEM, SMEM] + [VMEM] * 6,
+        [SMEM, SMEM] + [VMEM] * 9,
         [
-            shape((groups, blocks, length, LANES), F32),
-            shape((groups * span, width), F32),
+            slab_shape,
+            wide_shape,
+            wide_shape,
             shape((groups * span, LANES), F32),
             shape((rows, width + half), BF16),
         ],
-        [pltpu.VMEM((span, LANES), F32)],
+        [pltpu.VMEM((span, LANES), F32), pltpu.VMEM((2 * groups * HALF_PAD, width), BF16)],
         conv_flops,
         4,
-        {2: 0},
-    )(lengths, spot, gated, left, right, weights, gain, flat)
+        {2: 0, 3: 1, 4: 2},
+    )(lengths, spot, gated, inner, swish, left, right, weights, gain, flat, w_near)
     far = lax.ppermute(message, "seq", swap)
     grad, term_conv = call(
         backward_kernel,
-        [SMEM, SMEM] + [VMEM] * 7,
+        [SMEM, SMEM] + [VMEM] * 4,
         [shape((groups, blocks, span, LANES), F32), shape((1, width), F32)],
-        [
-            pltpu.VMEM((groups * span, width), BF16),
-            pltpu.VMEM((groups * span, width), F32),
-            pltpu.VMEM((8, width), F32),
-        ],
-        2 * rows * width * width,
-        10,
-    )(lengths, spot, cotangent, left, right, w_out, hat, inverse, gain)
+        [pltpu.VMEM((groups * span, width), F32), pltpu.VMEM((8, width), F32)],
+        20 * rows * width,
+        6,
+    )(lengths, spot, grad_swish, hat, inverse, gain)
     packed = call(
         terms_kernel,
         [VMEM] * 3,

time: 93.2 us -> 89.9 us (0.965)
  waiting for transfers between devices: 30.1 us -> 25.6 us
  Pallas kernels: 41.4 us -> 42.8 us
    ppermute x1, waiting for transfers between devices: 4.32 us -> 0.01 us  [local(): right = lax.ppermute(head, 'seq', [(i + 1, i) for i in range(ends)])]
    pallas_call x4, Pallas kernels: 18.9 us -> 20.1 us  [the longest x1 8.1 us: local(): call(gate_kernel, [SMEM, SMEM] + [VMEM] * 3 + [HBM], [slab_shape, wide_sh...]
    unnamed x18 -> x16, local copies, waits for them, and re-layouts: 2.6 us -> 1.8 us
  transfers between devices with their start and end apart: 4 -> 4, of which waited for: 2 -> 1; matrix products, arithmetic and copies ran while one was open for 0% -> 1% of each run, Pallas kernels for 26% -> 31%
where the time goes in v5:
time: 89.9 us; the launch traced here: 89.6 us
  Pallas kernels  42.8 us (48%)
  waiting for transfers between devices  25.6 us (28%)
  starting transfers between devices  17.6 us (20%)
  local copies, waits for them, and re-layouts  2.75 us (3%)
    all_to_all x1, waiting for transfers between devices, local(): lax.all_to_all(pieces.reshape(devices, deep + 8, LANES), AXES, 0, 0, tile...  25.6 us
    all_to_all x1, starting transfers between devices, local(): lax.all_to_all(pieces.reshape(devices, deep + 8, LANES), AXES, 0, 0, tile...  10.7 us
    pallas_call x1, Pallas kernels, local(): call(input_kernel, [SMEM, SMEM] + [VMEM] * 3, shape((groups, frames, doub...  8.41 us
    pallas_call x1, Pallas kernels, local(): call(gate_kernel, [SMEM, SMEM] + [VMEM] * 3 + [HBM], [slab_shape, wide_sh...  8.1 us
    pallas_call x1, Pallas kernels, local(): call(terms_kernel, [VMEM] * 3, shape((devices // 2, 2, 8, LANES), F32), [...  7.54 us
    pallas_call x1, Pallas kernels, local(): call(forward_kernel, [SMEM, SMEM] + [VMEM] * 9, [slab_shape, wide_shape,...  6.28 us
    ppermute x1, starting transfers between devices, local(): left = lax.ppermute(tail, 'seq', [(i, i + 1) for i in range(ends)])  4.93 us
    pallas_call x1, Pallas kernels, local(): call(product_kernel, [SMEM] + [VMEM] * 4, pltpu.HBM((devices // 2, 2, dee...  4.15 us
  transfers between devices with their start and end apart: 4, of which 1 were waited for; matrix products, arithmetic and copies ran while one was open for 1% of the time, Pallas kernels for 31%

profile of v5, /device:TPU:1, one launch (start us, length us, event | category | flops | bytes accessed | tf_op | source)
XLA Modules:
  0.0 89.6 jit_solution(16368387407027394601)
XLA Ops:
  0.6 0.0 copy-start
  0.6 0.0 copy-start.1
  0.7 0.0 copy-start.7
  0.7 0.0 copy-start.6
  0.7 2.4 %shard_map.94 = (bf16[2,48,1536]{2,1,0:T(8,128)(2,1)}, bf16[2,48,1536]{2,1,0:T(8,128)(2,1)}) custom-call(bf16[2,192,3072]{2,1,0:T(8,128)(2,1)} %hidden.5, bf16[2,192,1536]{2,1,0:T(8,128)(2,1)} %cotangent.1), custom_call_target="tpu_custom_call" | custom-call | flops 1048576 | bytes 8388608 | tf_op jit(solution)/shard_map/pallas_call | solution.py:453
  3.0 4.9 %collective-permute-start = (bf16[2,48,1536]{2,1,0:T(8,128)(2,1)}, bf16[2,48,1536]{2,1,0:T(8,128)(2,1)}, u32[]{:S(2)}, u32[]{:S(2)}) collective-permute-start(bf16[2,48,1536]{2,1,0:T(8,128)(2,1)} %get-tuple-element.23), channel_id=1, source_target_pairs={{0,1},{1,2},{2,3},{3,4},{4,5},{5,6},{6,7},{7,8},{8,9},{9,10},{10,1... | collective-permute-start | bytes 884744 | tf_op jit(solution)/shard_map/ppermute | solution.py:465
  8.0 1.9 %collective-permute-start.1 = (bf16[2,48,1536]{2,1,0:T(8,128)(2,1)}, bf16[2,48,1536]{2,1,0:T(8,128)(2,1)}, u32[]{:S(2)}, u32[]{:S(2)}) collective-permute-start(bf16[2,48,1536]{2,1,0:T(8,128)(2,1)} %get-tuple-element.24), channel_id=1, source_target_pairs={{1,0},{2,1},{3,2},{4,3},{5,4},{6,5},{7,6},{8,7},{9,8},{10,9},{11,1... | collective-permute-start | bytes 884744 | tf_op jit(solution)/shard_map/ppermute | solution.py:466
  9.9 0.0 copy-done.7
  9.9 0.9 %pad_bitcast_fusion.weights = f32[32,1536]{1,0:T(8,128)S(1)} fusion(f32[1536,31]{0,1:T(8,128)} %param.9), kind=kLoop, calls=%fused_computation | loop fusion | bytes 387072 | tf_op jit(solution)/shard_map/transpose | solution.py:467
  10.9 0.0 copy-start.4
  10.9 8.1 %shard_map.93 = (f32[2,12,256,128]{3,2,1,0:T(8,128)S(1)}, f32[448,1536]{1,0:T(8,128)S(1)}, f32[448,1536]{1,0:T(8,128)S(1)}, bf16[1536,1536]{1,0:T(8,128)(2,1)S(1)}) custom-call(s32[2]{0:T(128)S(1)} %copy-done.6, s32[1]{0:T(128)} %bitcast.place, bf16[2,192,3072]{2,1,0:T(8,128)(2,1)S(1)} %copy-done, f32[32,1536]{1,0:T(8,128)S(1)} %pad_bitcast_fusion.weights, ...), custom_call_target="tpu_custom_call" | custom-call | flops 36569088 | bytes 8388608 | tf_op jit(solution)/shard_map/pallas_call | solution.py:471
  19.0 0.0 collective-permute-done.left
  19.0 0.0 collective-permute-done.1.right
  19.1 6.3 %shard_map.95 = (f32[2,12,256,128]{3,2,1,0:T(8,128)S(1)}, f32[448,1536]{1,0:T(8,128)S(1)}, f32[448,1536]{1,0:T(8,128)S(1)}, f32[448,128]{1,0:T(8,128)S(1)}, bf16[384,2304]{1,0:T(8,128)(2,1)S(1)}) custom-call(s32[2]{0:T(128)S(1)} %copy-done.6, s32[1]{0:T(128)} %bitcast.place, ...), custom_call_target="tpu_custom_call", output_to_operand_aliasing={{0}: (2, {}), {1}: (3, {}), {2}: (4, {})} | custom-call | flops 36569088 | bytes 8388608 | tf_op jit(solution)/shard_map/pallas_call | solution.py:479
  25.3 0.1 collective-permute-start.2
  25.4 3.4 %shard_map.96 = (f32[2,12,224,128]{3,2,1,0:T(8,128)S(1)}, f32[1,1536]{1,0:T(1,128)S(1)}) custom-call(s32[2]{0:T(128)S(1)} %copy-done.6, s32[1]{0:T(128)} %bitcast.place, f32[448,1536]{1,0:T(8,128)S(1)} %get-tuple-element.26.grad, f32[448,1536]{1,0:T(8,128)S(1)} %get-tuple-element.27.hat, f32[448,128]{1,0:T(8,128)S(1)} %get-tuple-element.28.inverse, ...), custom_call_target="tpu_custom_call" | custom-call | flops 11796480 | bytes 8388608 | tf_op jit(solution)/shard_map/pallas_call | solution.py:495
  28.8 7.5 %shard_map.98.packed = f32[64,2,8,128]{3,2,1,0:T(8,128)S(1)} custom-call(f32[2,12,224,128]{3,2,1,0:T(8,128)S(1)} %get-tuple-element.29.grad, f32[2,12,256,128]{3,2,1,0:T(8,128)S(1)} %get-tuple-element.31.slab, f32[1,1536]{1,0:T(1,128)S(1)} %get-tuple-element.32.term), custom_call_target="tpu_custom_call" | custom-call | flops 36569088 | bytes 8388608 | tf_op jit(solution)/shard_map/pallas_call | solution.py:503
  36.4 0.0 collective-permute-done.2.far
  36.4 4.1 %shard_map.99 = bf16[64,2,80,128]{3,2,1,0:T(8,128)(2,1)} custom-call(s32[1]{0:T(128)} %bitcast.place, bf16[384,2304]{1,0:T(8,128)(2,1)S(1)} %get-tuple-element.30.near, bf16[384,1536]{1,0:T(8,128)(2,1)S(1)} %bitcast.9, bf16[384,2304]{1,0:T(8,128)(2,1)S(1)} %collective-permute-done.2.far, f32[64,2,8,128]{3,2,1,0:T(8,128)S(1)} %shard_map.98.packed), custom_call_target="tpu_custom_call" | custom-call | flops 1811939328 | bytes 8388608 | tf_op jit(solution)/shard_map/pallas_call | solution.py:517
  40.6 10.7 %all-to-all-start = ((bf16[128,80,128]{2,1,0:T(8,128)(2,1)}), bf16[128,80,128]{2,1,0:T(8,128)(2,1)}, u32[]{:S(2)}, u32[]{:S(2)}) async-start(bf16[128,80,128]{2,1,0:T(8,128)(2,1)} %bitcast.10), calls=%async_computation | async-start | bytes 5242880 | tf_op jit(solution)/shard_map/all_to_all | solution.py:530
  51.3 1.8 %copy-done.3 = f32[2,12,224,128]{3,2,1,0:T(8,128)S(1)} copy-done((f32[2,12,224,128]{3,2,1,0:T(8,128)S(1)}, f32[2,12,224,128]{3,2,1,0:T(8,128)}, u32[]{:S(2)}) %copy-start.3) | copy-done | bytes 2752536
  53.1 8.4 %shard_map.97 = bf16[2,192,3072]{2,1,0:T(8,128)(2,1)} custom-call(s32[2]{0:T(128)S(1)} %copy-done.6, s32[1]{0:T(128)} %bitcast.place, f32[2,12,224,128]{3,2,1,0:T(8,128)S(1)} %copy-done.3, bf16[2,192,3072]{2,1,0:T(8,128)(2,1)S(1)} %copy-done, f32[32,1536]{1,0:T(8,128)S(1)} %copy-done.5), custom_call_target="tpu_custom_call" | custom-call | flops 36569088 | bytes 8388608 | tf_op jit(solution)/shard_map/pallas_call | solution.py:531
  61.5 25.6 %all-to-all-done = bf16[128,80,128]{2,1,0:T(8,128)(2,1)} async-done(((bf16[128,80,128]{2,1,0:T(8,128)(2,1)}), bf16[128,80,128]{2,1,0:T(8,128)(2,1)}, u32[]{:S(2)}, u32[]{:S(2)}) %all-to-all-start) | async-done | bytes 2621472 | tf_op jit(solution)/shard_map/all_to_all | solution.py:530
  87.1 2.5 %shard_map.100 = (f32[12,1536]{1,0:T(8,128)}, f32[12,31]{1,0:T(8,128)}, f32[1,12]{1,0:T(1,128)}) custom-call(bf16[64,2,80,128]{3,2,1,0:T(8,128)(2,1)} %bitcast.4.got), custom_call_target="tpu_custom_call" | custom-call | flops 1048576 | bytes 8388608 | tf_op jit(solution)/shard_map/pallas_call | solution.py:542
  (10 shorter events, 0.0 us)
Async XLA Ops:
  0.6 10.2 %copy-start = (bf16[2,192,3072]{2,1,0:T(8,128)(2,1)S(1)}, bf16[2,192,3072]{2,1,0:T(8,128)(2,1)}, u32[]{:S(2)}) copy-start(bf16[2,192,3072]{2,1,0:T(8,128)(2,1)} %hidden.5) | copy-start | bytes 7077892
  0.6 10.2 %copy-start.1 = (bf16[2,192,1536]{2,1,0:T(8,128)(2,1)S(1)}, bf16[2,192,1536]{2,1,0:T(8,128)(2,1)}, u32[]{:S(2)}) copy-start(bf16[2,192,1536]{2,1,0:T(8,128)(2,1)} %cotangent.1) | copy-start | bytes 3538948
  0.7 9.2 %copy-start.7 = (f32[1536]{0:T(1024)S(1)}, f32[1536]{0:T(1024)}, u32[]{:S(2)}) copy-start(f32[1536]{0:T(1024)} %param.10) | copy-start | bytes 18436
  0.7 10.2 %copy-start.6 = (s32[2]{0:T(128)S(1)}, s32[2]{0:T(128)}, u32[]{:S(2)}) copy-start(s32[2]{0:T(128)} %lengths.7) | copy-start | bytes 28
  3.0 16.0 %collective-permute-start = (bf16[2,48,1536]{2,1,0:T(8,128)(2,1)}, bf16[2,48,1536]{2,1,0:T(8,128)(2,1)}, u32[]{:S(2)}, u32[]{:S(2)}) collective-permute-start(bf16[2,48,1536]{2,1,0:T(8,128)(2,1)} %get-tuple-element.23), channel_id=1, source_target_pairs={{0,1},{1,2},{2,3},{3,4},{4,5},{5,6},{6,7},{7,8},{8,9},{9,10},{10,1... | collective-permute-start | bytes 884744 | tf_op jit(solution)/shard_map/ppermute | solution.py:465
  8.0 11.1 %collective-permute-start.1 = (bf16[2,48,1536]{2,1,0:T(8,128)(2,1)}, bf16[2,48,1536]{2,1,0:T(8,128)(2,1)}, u32[]{:S(2)}, u32[]{:S(2)}) collective-permute-start(bf16[2,48,1536]{2,1,0:T(8,128)(2,1)} %get-tuple-element.24), channel_id=1, source_target_pairs={{1,0},{2,1},{3,2},{4,3},{5,4},{6,5},{7,6},{8,7},{9,8},{10,9},{11,1... | collective-permute-start | bytes 884744 | tf_op jit(solution)/shard_map/ppermute | solution.py:466
  10.9 8.2 %copy-start.4 = (f32[32,1536]{1,0:T(8,128)}, f32[32,1536]{1,0:T(8,128)S(1)}, u32[]{:S(2)}) copy-start(f32[32,1536]{1,0:T(8,128)S(1)} %pad_bitcast_fusion.weights) | copy-start | bytes 589828
  25.3 11.1 %collective-permute-start.2 = (bf16[384,2304]{1,0:T(8,128)(2,1)S(1)}, bf16[384,2304]{1,0:T(8,128)(2,1)S(1)}, u32[]{:S(2)}, u32[]{:S(2)}) collective-permute-start(bf16[384,2304]{1,0:T(8,128)(2,1)S(1)} %get-tuple-element.30.near), channel_id=1, source_target_pairs={{0,1},{1,0},{2,3},{3,2},{4,5},{5,4},{6,7},{7,6},{8,9},{9,8},{10,11... | collective-permute-start | bytes 5308424 | tf_op jit(solution)/shard_map/ppermute | solution.py:494
  28.8 7.6 %copy-start.2 = (f32[2,12,224,128]{3,2,1,0:T(8,128)}, f32[2,12,224,128]{3,2,1,0:T(8,128)S(1)}, u32[]{:S(2)}) copy-start(f32[2,12,224,128]{3,2,1,0:T(8,128)S(1)} %get-tuple-element.29.grad) | copy-start | bytes 8257540
  40.6 10.7 %copy-start.5 = (f32[32,1536]{1,0:T(8,128)S(1)}, f32[32,1536]{1,0:T(8,128)}, u32[]{:S(2)}) copy-start(f32[32,1536]{1,0:T(8,128)} %copy-done.4) | copy-start | bytes 589828
  40.6 46.5 %all-to-all-start = ((bf16[128,80,128]{2,1,0:T(8,128)(2,1)}), bf16[128,80,128]{2,1,0:T(8,128)(2,1)}, u32[]{:S(2)}, u32[]{:S(2)}) async-start(bf16[128,80,128]{2,1,0:T(8,128)(2,1)} %bitcast.10), calls=%async_computation | async-start | bytes 5242880 | tf_op jit(solution)/shard_map/all_to_all | solution.py:530
  51.3 1.8 %copy-start.3 = (f32[2,12,224,128]{3,2,1,0:T(8,128)S(1)}, f32[2,12,224,128]{3,2,1,0:T(8,128)}, u32[]{:S(2)}) copy-start(f32[2,12,224,128]{3,2,1,0:T(8,128)} %copy-done.2) | copy-start | bytes 8257540

commit v6 on v5

--- a/solution.py
+++ b/solution.py
@@ -61,19 +61,24 @@
     return total
 
 
-def edges_kernel(hidden, cotangent, tail, head, cells, upstream, arrived):
+def edges_kernel(
+    place, hidden, cotangent, source, inside, across, weights, cells, upstream, arrived, loaded
+):
     groups, frames, double = hidden.shape
     width = double // 2
+    core = place[0] & 1
     copies = []
-    for side, (start, near) in enumerate(((frames - PAD, frames - HALF_PAD), (0, 0))):
+    for side, last in enumerate((core, 1 - core)):
+        start = pl.multiple_of(last * (frames - PAD), TILE)
+        near = pl.multiple_of(last * (frames - HALF_PAD), TILE)
         for u in range(groups):
             copies.append(
                 (
                     pltpu.make_async_copy(
-                        hidden.at[u, start : start + PAD], cells.at[side, u], arrived.at[0, side, u]
+                        hidden.at[u, pl.ds(start, PAD)], cells.at[side, u], arrived.at[0, side, u]
                     ),
                     pltpu.make_async_copy(
-                        cotangent.at[u, near : near + HALF_PAD],
+                        cotangent.at[u, pl.ds(near, HALF_PAD)],
                         upstream.at[side, u],
                         arrived.at[1, side, u],
                     ),
@@ -82,8 +87,10 @@
     for first, second in copies:
         first.start()
         second.start()
+    taps = pltpu.make_async_copy(source, weights, loaded)
+    taps.start()
     n = 0
-    for side, out in enumerate((tail, head)):
+    for side, out in enumerate((across, inside)):
         for u in range(groups):
             copies[n][0].wait()
             for cb in range(width // LANES):
@@ -95,6 +102,7 @@
             copies[n][1].wait()
             out[u, PAD:, :] = upstream[side, u]
             n += 1
+    taps.wait()
 
 
 CONTRACT_COLUMNS = (((1,), (1,)), ((), ()))
@@ -104,7 +112,7 @@
     lengths, place, hidden, weights, cotangent, source, slab, hat, grad, w_out, arrived
 ):
     groups, frames, double = hidden.shape
-    taps = weights.shape[0] - 1
+    taps = weights.shape[0]
     width = double // 2
     blocks = width // LANES
     span = frames + 2 * HALF_PAD
@@ -156,8 +164,8 @@
     gated,
     inner,
     swish,
-    left,
-    right,
+    inside,
+    across,
     weights,
     gain,
     cotangent,
@@ -171,16 +179,23 @@
     held,
 ):
     groups, blocks, length = slab.shape[:3]
-    taps = weights.shape[0] - 1
+    taps = weights.shape[0]
     width = blocks * LANES
     half = width // 2
     frames = length - 2 * PAD
     span = frames + 2 * HALF_PAD
     theirs = pl.ds(pl.multiple_of((1 - (place[0] & 1)) * half, LANES), half)
     message[:, width:] = cotangent[:, theirs]
+    first = (place[0] & 1) == 0
+
+    def sides(u, rows, lanes):
+        one, two = inside[u, rows, lanes].astype(F32), across[u, rows, lanes].astype(F32)
+        return jnp.where(first, two, one), jnp.where(first, one, two)
+
     for u in range(groups):
-        held[2 * u * HALF_PAD : (2 * u + 1) * HALF_PAD, :] = left[u, PAD:, :]
-        held[(2 * u + 1) * HALF_PAD : (2 * u + 2) * HALF_PAD, :] = right[u, PAD:, :]
+        left, right = sides(u, slice(PAD, PAD + HALF_PAD), slice(0, width))
+        held[2 * u * HALF_PAD : (2 * u + 1) * HALF_PAD, :] = left.astype(BF16)
+        held[(2 * u + 1) * HALF_PAD : (2 * u + 2) * HALF_PAD, :] = right.astype(BF16)
 
     def pair(n, _):
         at = pl.ds(pl.multiple_of(n * 2 * LANES, 2 * LANES), 2 * LANES)
@@ -193,8 +208,7 @@
             base = u * span
             for cb in (2 * n, 2 * n + 1):
                 block = slab.at[u, cb]
-                before = left[u, 0:PAD, lane(cb)].astype(F32)
-                after = right[u, 0:PAD, lane(cb)].astype(F32)
+                before, after = sides(u, slice(0, PAD), lane(cb))
                 block[0:PAD, :] = jnp.where(row - PAD < limit, before, 0.0)
                 block[PAD + frames :, :] = jnp.where(row + frames < limit, after, 0.0)
                 weight = [weights[j : j + 1, lane(cb)] for j in range(taps)]
@@ -236,6 +250,9 @@
             return 0
 
         lax.fori_loop(0, blocks, normalize, 0)
+
+
+CONTRACT_ROWS = (((0,), (0,)), ((), ()))
 
 
 CONTRACT_ROWS = (((0,), (0,)), ((), ()))
@@ -369,7 +386,7 @@
 def input_kernel(lengths, place, grad, hidden, weights, out):
     groups, frames, _ = hidden.shape
     blocks = grad.shape[1]
-    taps = weights.shape[0] - 1
+    taps = weights.shape[0]
     chunk = 64
     for u in range(groups):
         limit = left_of(lengths, place, u, frames)
@@ -450,21 +467,22 @@
 
     spot = place.reshape(1)
     flat = cotangent.reshape(rows, width)
-    tail, head = call(
+    inner_edge, outer_edge, weights = call(
         edges_kernel,
-        [HBM, HBM],
-        [shape((groups, PAD + HALF_PAD, width), BF16)] * 2,
+        [SMEM, HBM, HBM, HBM],
+        [shape((groups, PAD + HALF_PAD, width), BF16)] * 2 + [shape((taps, width), F32)],
         [
             pltpu.VMEM((2, groups, PAD, double), BF16),
             pltpu.VMEM((2, groups, HALF_PAD, width), BF16),
             pltpu.SemaphoreType.DMA((2, 2, groups)),
+            pltpu.SemaphoreType.DMA,
         ],
         1 << 20,
         4,
-    )(far_memory(hidden), far_memory(cotangent))
-    left = lax.ppermute(tail, "seq", [(i, i + 1) for i in range(ends)])
-    right = lax.ppermute(head, "seq", [(i + 1, i) for i in range(ends)])
-    weights = jnp.concatenate([kernel, jnp.zeros((width, 1), F32)], axis=1).T
+    )(spot, far_memory(hidden), far_memory(cotangent), far_memory(kernel.T))
+    bridge = [(i, i + 1) for i in range(1, ends, 2)]
+    across = lax.ppermute(outer_edge, "seq", bridge + [(j, i) for i, j in bridge])
+    inside = lax.ppermute(inner_edge, "seq", swap)
     gain = conv_gain.reshape(1, width)
     slab_shape = shape((groups, blocks, length, LANES), F32)
     wide_shape = shape((groups * span, width), F32)
@@ -490,7 +508,7 @@
         conv_flops,
         4,
         {2: 0, 3: 1, 4: 2},
-    )(lengths, spot, gated, inner, swish, left, right, weights, gain, flat, w_near)
+    )(lengths, spot, gated, inner, swish, inside, across, weights, gain, flat, w_near)
     far = lax.ppermute(message, "seq", swap)
     grad, term_conv = call(
         backward_kernel,

time: 89.9 us -> 85.6 us (0.952)
  starting transfers between devices: 17.6 us -> 15.5 us
  Pallas kernels: 42.8 us -> 41.5 us
  local copies, waits for them, and re-layouts: 2.75 us -> 1.81 us
    ppermute x2, starting transfers between devices: 6.85 us -> 5.02 us  [the longest x1 3.56 us: local(): lax.ppermute(outer_edge, 'seq', bridge + [(j, i) for i, j in bridge])]
    transpose x1 -> x0, local copies, waits for them, and re-layouts: 0.94 us -> none  [local(): weights = jnp.concatenate([kernel, jnp.zeros((width, 1), F32)], axis=1).T]
  transfers between devices with their start and end apart: 4 -> 4, of which waited for: 1 -> 1; matrix products, arithmetic and copies ran while one was open for 1% -> 0% of each run, Pallas kernels for 31% -> 32%
where the time goes in v6:
time: 85.6 us; the launch traced here: 85.3 us
  Pallas kernels  41.5 us (48%)
  waiting for transfers between devices  25.6 us (30%)
  starting transfers between devices  15.5 us (18%)
  local copies, waits for them, and re-layouts  1.81 us (2%)
  between operations  0.86 us (1%)
    all_to_all x1, waiting for transfers between devices, local(): lax.all_to_all(pieces.reshape(devices, deep + 8, LANES), AXES, 0, 0, tile...  25.6 us
    all_to_all x1, starting transfers between devices, local(): lax.all_to_all(pieces.reshape(devices, deep + 8, LANES), AXES, 0, 0, tile...  10.4 us
    pallas_call x1, Pallas kernels, local(): call(input_kernel, [SMEM, SMEM] + [VMEM] * 3, shape((groups, frames, doub...  8.41 us
    pallas_call x1, Pallas kernels, local(): call(gate_kernel, [SMEM, SMEM] + [VMEM] * 3 + [HBM], [slab_shape, wide_sh...  8.1 us
    pallas_call x1, Pallas kernels, local(): call(terms_kernel, [VMEM] * 3, shape((devices // 2, 2, 8, LANES), F32), [...  7.54 us
    pallas_call x1, Pallas kernels, local(): call(forward_kernel, [SMEM, SMEM] + [VMEM] * 9, [slab_shape, wide_shape,...  5.8 us
    pallas_call x1, Pallas kernels, local(): call(product_kernel, [SMEM] + [VMEM] * 4, pltpu.HBM((devices // 2, 2, dee...  4.15 us
    ppermute x1, starting transfers between devices, local(): lax.ppermute(outer_edge, 'seq', bridge + [(j, i) for i, j in bridge])  3.56 us
  transfers between devices with their start and end apart: 4, of which 1 were waited for; matrix products, arithmetic and copies ran while one was open for 0% of the time, Pallas kernels for 32%

profile of v6, /device:TPU:1, one launch (start us, length us, event | category | flops | bytes accessed | tf_op | source)
XLA Modules:
  0.0 85.3 jit_solution(8503595373706371804)
XLA Ops:
  0.6 0.0 copy-start
  0.6 0.0 copy-start.1
  0.7 1.6 %shard_map.93 = (bf16[2,48,1536]{2,1,0:T(8,128)(2,1)S(1)}, bf16[2,48,1536]{2,1,0:T(8,128)(2,1)S(1)}, f32[31,1536]{1,0:T(8,128)S(1)}) custom-call(s32[1]{0:T(128)} %bitcast.place, bf16[2,192,3072]{2,1,0:T(8,128)(2,1)} %hidden.5, bf16[2,192,1536]{2,1,0:T(8,128)(2,1)} %cotangent.1, f32[31,1536]{1,0:T(8,128)} %bitcast.10), custom_call_target="tpu_custom_call" | custom-call | flops 1048576 | bytes 8388608 | tf_op jit(solution)/shard_map/pallas_call | solution.py:470
  2.3 0.0 copy-start.4
  2.3 1.5 %collective-permute-start = (bf16[2,48,1536]{2,1,0:T(8,128)(2,1)S(1)}, bf16[2,48,1536]{2,1,0:T(8,128)(2,1)S(1)}, u32[]{:S(2)}, u32[]{:S(2)}) collective-permute-start(bf16[2,48,1536]{2,1,0:T(8,128)(2,1)S(1)} %get-tuple-element.25), channel_id=1, source_target_pairs={{0,1},{1,0},{2,3},{3,2},{4,5},{5,4},{6,7},{7,6},{8,9},{9,8},{10,11... | collective-permute-start | bytes 884744 | tf_op jit(solution)/shard_map/ppermute | solution.py:485
  3.7 3.6 %collective-permute-start.1 = (bf16[2,48,1536]{2,1,0:T(8,128)(2,1)S(1)}, bf16[2,48,1536]{2,1,0:T(8,128)(2,1)S(1)}, u32[]{:S(2)}, u32[]{:S(2)}) collective-permute-start(bf16[2,48,1536]{2,1,0:T(8,128)(2,1)S(1)} %get-tuple-element.26), channel_id=1, source_target_pairs={{1,2},{3,4},{5,6},{7,8},{9,10},{11,12},{13,14},{15,16},{17,18},{19... | collective-permute-start | bytes 884744 | tf_op jit(solution)/shard_map/ppermute | solution.py:484
  7.4 8.1 %shard_map.94 = (f32[2,12,256,128]{3,2,1,0:T(8,128)S(1)}, f32[448,1536]{1,0:T(8,128)S(1)}, f32[448,1536]{1,0:T(8,128)S(1)}, bf16[1536,1536]{1,0:T(8,128)(2,1)S(1)}) custom-call(s32[2]{0:T(128)S(1)} %copy-done.6, s32[1]{0:T(128)} %bitcast.place, bf16[2,192,3072]{2,1,0:T(8,128)(2,1)S(1)} %copy-done, f32[31,1536]{1,0:T(8,128)S(1)} %get-tuple-element.21.weights, ...), custom_call_target="tpu_custom_call" | custom-call | flops 36569088 | bytes 8388608 | tf_op jit(solution)/shard_map/pallas_call | solution.py:489
  15.5 0.0 collective-permute-done.inside
  15.5 0.0 collective-permute-done.1.across
  15.5 5.8 %shard_map.95 = (f32[2,12,256,128]{3,2,1,0:T(8,128)S(1)}, f32[448,1536]{1,0:T(8,128)S(1)}, f32[448,1536]{1,0:T(8,128)S(1)}, f32[448,128]{1,0:T(8,128)S(1)}, bf16[384,2304]{1,0:T(8,128)(2,1)S(1)}) custom-call(s32[2]{0:T(128)S(1)} %copy-done.6, s32[1]{0:T(128)} %bitcast.place, ...), custom_call_target="tpu_custom_call", output_to_operand_aliasing={{0}: (2, {}), {1}: (3, {}), {2}: (4, {})} | custom-call | flops 36569088 | bytes 8388608 | tf_op jit(solution)/shard_map/pallas_call | solution.py:497
  21.3 0.1 collective-permute-start.2
  21.4 3.4 %shard_map.96 = (f32[2,12,224,128]{3,2,1,0:T(8,128)S(1)}, f32[1,1536]{1,0:T(1,128)S(1)}) custom-call(s32[2]{0:T(128)S(1)} %copy-done.6, s32[1]{0:T(128)} %bitcast.place, f32[448,1536]{1,0:T(8,128)S(1)} %get-tuple-element.28.grad, f32[448,1536]{1,0:T(8,128)S(1)} %get-tuple-element.29.hat, f32[448,128]{1,0:T(8,128)S(1)} %get-tuple-element.30.inverse, ...), custom_call_target="tpu_custom_call" | custom-call | flops 11796480 | bytes 8388608 | tf_op jit(solution)/shard_map/pallas_call | solution.py:513
  24.8 0.0 copy-start.2
  24.8 7.5 %shard_map.98.packed = f32[64,2,8,128]{3,2,1,0:T(8,128)S(1)} custom-call(f32[2,12,224,128]{3,2,1,0:T(8,128)S(1)} %get-tuple-element.31.grad, f32[2,12,256,128]{3,2,1,0:T(8,128)S(1)} %get-tuple-element.33.slab, f32[1,1536]{1,0:T(1,128)S(1)} %get-tuple-element.34.term), custom_call_target="tpu_custom_call" | custom-call | flops 36569088 | bytes 8388608 | tf_op jit(solution)/shard_map/pallas_call | solution.py:521
  32.4 0.0 collective-permute-done.2.far
  32.4 4.1 %shard_map.99 = bf16[64,2,80,128]{3,2,1,0:T(8,128)(2,1)} custom-call(s32[1]{0:T(128)} %bitcast.place, bf16[384,2304]{1,0:T(8,128)(2,1)S(1)} %get-tuple-element.32.near, bf16[384,1536]{1,0:T(8,128)(2,1)S(1)} %bitcast.8, bf16[384,2304]{1,0:T(8,128)(2,1)S(1)} %collective-permute-done.2.far, f32[64,2,8,128]{3,2,1,0:T(8,128)S(1)} %shard_map.98.packed), custom_call_target="tpu_custom_call" | custom-call | flops 1811939328 | bytes 8388608 | tf_op jit(solution)/shard_map/pallas_call | solution.py:535
  36.5 0.0 copy-start.5
  36.5 10.4 %all-to-all-start = ((bf16[128,80,128]{2,1,0:T(8,128)(2,1)}), bf16[128,80,128]{2,1,0:T(8,128)(2,1)}, u32[]{:S(2)}, u32[]{:S(2)}) async-start(bf16[128,80,128]{2,1,0:T(8,128)(2,1)} %bitcast.9), calls=%async_computation | async-start | bytes 5242880 | tf_op jit(solution)/shard_map/all_to_all | solution.py:548
  47.0 0.0 copy-done.5
  47.0 0.0 copy-start.3
  47.0 1.8 %copy-done.3 = f32[2,12,224,128]{3,2,1,0:T(8,128)S(1)} copy-done((f32[2,12,224,128]{3,2,1,0:T(8,128)S(1)}, f32[2,12,224,128]{3,2,1,0:T(8,128)}, u32[]{:S(2)}) %copy-start.3) | copy-done | bytes 2752536
  48.8 8.4 %shard_map.97 = bf16[2,192,3072]{2,1,0:T(8,128)(2,1)} custom-call(s32[2]{0:T(128)S(1)} %copy-done.6, s32[1]{0:T(128)} %bitcast.place, f32[2,12,224,128]{3,2,1,0:T(8,128)S(1)} %copy-done.3, bf16[2,192,3072]{2,1,0:T(8,128)(2,1)S(1)} %copy-done, f32[31,1536]{1,0:T(8,128)S(1)} %copy-done.5), custom_call_target="tpu_custom_call" | custom-call | flops 36569088 | bytes 8388608 | tf_op jit(solution)/shard_map/pallas_call | solution.py:549
  57.2 25.6 %all-to-all-done = bf16[128,80,128]{2,1,0:T(8,128)(2,1)} async-done(((bf16[128,80,128]{2,1,0:T(8,128)(2,1)}), bf16[128,80,128]{2,1,0:T(8,128)(2,1)}, u32[]{:S(2)}, u32[]{:S(2)}) %all-to-all-start) | async-done | bytes 2621472 | tf_op jit(solution)/shard_map/all_to_all | solution.py:548
  82.8 2.5 %shard_map.100 = (f32[12,1536]{1,0:T(8,128)}, f32[12,31]{1,0:T(8,128)}, f32[1,12]{1,0:T(1,128)}) custom-call(bf16[64,2,80,128]{3,2,1,0:T(8,128)(2,1)} %bitcast.4.got), custom_call_target="tpu_custom_call" | custom-call | flops 1048576 | bytes 8388608 | tf_op jit(solution)/shard_map/pallas_call | solution.py:560
  (9 shorter events, 0.0 us)
Async XLA Ops:
  0.6 6.7 %copy-start = (bf16[2,192,3072]{2,1,0:T(8,128)(2,1)S(1)}, bf16[2,192,3072]{2,1,0:T(8,128)(2,1)}, u32[]{:S(2)}) copy-start(bf16[2,192,3072]{2,1,0:T(8,128)(2,1)} %hidden.5) | copy-start | bytes 7077892
  0.6 6.7 %copy-start.1 = (bf16[2,192,1536]{2,1,0:T(8,128)(2,1)S(1)}, bf16[2,192,1536]{2,1,0:T(8,128)(2,1)}, u32[]{:S(2)}) copy-start(bf16[2,192,1536]{2,1,0:T(8,128)(2,1)} %cotangent.1) | copy-start | bytes 3538948
  0.7 6.6 %copy-start.7 = (f32[1536]{0:T(1024)S(1)}, f32[1536]{0:T(1024)}, u32[]{:S(2)}) copy-start(f32[1536]{0:T(1024)} %param.10) | copy-start | bytes 18436
  0.7 6.7 %copy-start.6 = (s32[2]{0:T(128)S(1)}, s32[2]{0:T(128)}, u32[]{:S(2)}) copy-start(s32[2]{0:T(128)} %lengths.7) | copy-start | bytes 28
  2.3 13.2 %copy-start.4 = (f32[31,1536]{1,0:T(8,128)}, f32[31,1536]{1,0:T(8,128)S(1)}, u32[]{:S(2)}) copy-start(f32[31,1536]{1,0:T(8,128)S(1)} %get-tuple-element.21.weights) | copy-start | bytes 571396
  2.3 13.2 %collective-permute-start = (bf16[2,48,1536]{2,1,0:T(8,128)(2,1)S(1)}, bf16[2,48,1536]{2,1,0:T(8,128)(2,1)S(1)}, u32[]{:S(2)}, u32[]{:S(2)}) collective-permute-start(bf16[2,48,1536]{2,1,0:T(8,128)(2,1)S(1)} %get-tuple-element.25), channel_id=1, source_target_pairs={{0,1},{1,0},{2,3},{3,2},{4,5},{5,4},{6,7},{7,6},{8,9},{9,8},{10,11... | collective-permute-start | bytes 884744 | tf_op jit(solution)/shard_map/ppermute | solution.py:485
  3.7 11.7 %collective-permute-start.1 = (bf16[2,48,1536]{2,1,0:T(8,128)(2,1)S(1)}, bf16[2,48,1536]{2,1,0:T(8,128)(2,1)S(1)}, u32[]{:S(2)}, u32[]{:S(2)}) collective-permute-start(bf16[2,48,1536]{2,1,0:T(8,128)(2,1)S(1)} %get-tuple-element.26), channel_id=1, source_target_pairs={{1,2},{3,4},{5,6},{7,8},{9,10},{11,12},{13,14},{15,16},{17,18},{19... | collective-permute-start | bytes 884744 | tf_op jit(solution)/shard_map/ppermute | solution.py:484
  21.3 11.1 %collective-permute-start.2 = (bf16[384,2304]{1,0:T(8,128)(2,1)S(1)}, bf16[384,2304]{1,0:T(8,128)(2,1)S(1)}, u32[]{:S(2)}, u32[]{:S(2)}) collective-permute-start(bf16[384,2304]{1,0:T(8,128)(2,1)S(1)} %get-tuple-element.32.near), channel_id=1, source_target_pairs={{0,1},{1,0},{2,3},{3,2},{4,5},{5,4},{6,7},{7,6},{8,9},{9,8},{10,11... | collective-permute-start | bytes 5308424 | tf_op jit(solution)/shard_map/ppermute | solution.py:512
  24.8 7.6 %copy-start.2 = (f32[2,12,224,128]{3,2,1,0:T(8,128)}, f32[2,12,224,128]{3,2,1,0:T(8,128)S(1)}, u32[]{:S(2)}) copy-start(f32[2,12,224,128]{3,2,1,0:T(8,128)S(1)} %get-tuple-element.31.grad) | copy-start | bytes 8257540
  36.5 10.5 %copy-start.5 = (f32[31,1536]{1,0:T(8,128)S(1)}, f32[31,1536]{1,0:T(8,128)}, u32[]{:S(2)}) copy-start(f32[31,1536]{1,0:T(8,128)} %copy-done.4) | copy-start | bytes 571396
  36.5 46.2 %all-to-all-start = ((bf16[128,80,128]{2,1,0:T(8,128)(2,1)}), bf16[128,80,128]{2,1,0:T(8,128)(2,1)}, u32[]{:S(2)}, u32[]{:S(2)}) async-start(bf16[128,80,128]{2,1,0:T(8,128)(2,1)} %bitcast.9), calls=%async_computation | async-start | bytes 5242880 | tf_op jit(solution)/shard_map/all_to_all | solution.py:548
  47.0 1.8 %copy-start.3 = (f32[2,12,224,128]{3,2,1,0:T(8,128)S(1)}, f32[2,12,224,128]{3,2,1,0:T(8,128)}, u32[]{:S(2)}) copy-start(f32[2,12,224,128]{3,2,1,0:T(8,128)} %copy-done.2) | copy-start | bytes 8257540

commit v7 on v6

--- a/solution.py
+++ b/solution.py
@@ -184,8 +184,11 @@
     half = width // 2
     frames = length - 2 * PAD
     span = frames + 2 * HALF_PAD
-    theirs = pl.ds(pl.multiple_of((1 - (place[0] & 1)) * half, LANES), half)
-    message[:, width:] = cotangent[:, theirs]
+    rows = groups * frames
+    for side in range(half // rows):
+        theirs = (1 - (place[0] & 1)) * half + side * rows
+        part = cotangent[:, pl.ds(pl.multiple_of(theirs, LANES), rows)]
+        message[width + side * rows : width + (side + 1) * rows, :] = part
     first = (place[0] & 1) == 0
 
     def sides(u, rows, lanes):
@@ -226,44 +229,41 @@
 
     lax.fori_loop(0, blocks // 2, pair, 0)
     for u in range(groups):
-        limit = left_of(lengths, place, u, frames)
-        base = u * span
-        rows = slice(base, base + span)
+        rows = slice(u * span, (u + 1) * span)
         total = hat[rows, 0:LANES]
         for cb in range(1, blocks):
             total = total + hat[rows, cb * LANES : (cb + 1) * LANES]
-        mean[...] = row_mean(total, width)
+        mean[rows, :] = row_mean(total, width)
         total = None
         for cb in range(blocks):
-            centered = hat[rows, cb * LANES : (cb + 1) * LANES] - mean[...]
+            centered = hat[rows, cb * LANES : (cb + 1) * LANES] - mean[rows, :]
             total = centered * centered if total is None else total + centered * centered
         inverse[rows, :] = lax.rsqrt(row_mean(total, width) + EPSILON)
 
-        def normalize(cb, _):
-            normed = (hat[rows, lane(cb)] - mean[...]) * inverse[rows, :]
+    def normalize(cb, _):
+        outs = []
+        for u in range(groups):
+            limit = left_of(lengths, place, u, frames)
+            rows = slice(u * span, (u + 1) * span)
+            normed = (hat[rows, lane(cb)] - mean[rows, :]) * inverse[rows, :]
             hat[rows, lane(cb)] = normed
             pre = normed[HALF_PAD : HALF_PAD + frames] * (0.5 * gain[:, lane(cb)])
             out = pre * jnp.tanh(pre) + pre
             row = lax.broadcasted_iota(jnp.int32, (frames, LANES), 0)
-            out = jnp.where(row < limit, out, 0.0).astype(BF16)
-            message[u * frames : (u + 1) * frames, lane(cb)] = out
-            return 0
-
-        lax.fori_loop(0, blocks, normalize, 0)
-
-
-CONTRACT_ROWS = (((0,), (0,)), ((), ()))
-
-
-CONTRACT_ROWS = (((0,), (0,)), ((), ()))
+            outs.append(jnp.where(row < limit, out, 0.0).astype(BF16))
+        message[lane(cb), :] = jnp.concatenate(outs, axis=0).T
+        return 0
+
+    lax.fori_loop(0, blocks, normalize, 0)
 
 
 def product_kernel(place, near, cotangent, far, packed, out, scratch, held, sent):
-    half = cotangent.shape[1] // 2
-    width = 2 * half
+    rows, width = cotangent.shape
+    half = width // 2
     pairs = scratch.shape[0]
     step = 24 * pairs
     deep = scratch.shape[2] - 8
+    wide = 2 * LANES
     first = lax.broadcasted_iota(jnp.int32, (pairs, 8, LANES), 1) < 4
     pick = lambda a, b: jnp.where(first, a, b)
     roll = lambda a: pltpu.roll(a, 4, 1)
@@ -272,19 +272,22 @@
     def copy(s):
         return pltpu.make_async_copy(held.at[s], out.at[pl.ds(s * pairs, pairs)], sent.at[s])
 
-    def rows(s, _):
+    def chunk(s, _):
         at = pl.ds(pl.multiple_of(s * step, step), step)
-        result = lax.dot_general(
-            near[:, at], cotangent[:, mine], CONTRACT_ROWS, preferred_element_type=F32
-        ) + lax.dot_general(far[:, at], far[:, width:], CONTRACT_ROWS, preferred_element_type=F32)
-
-        def parts(k):
-            cut = result[:, k * LANES : (k + 1) * LANES].reshape(pairs, 3, 8, LANES)
-            return cut[:, 0], cut[:, 1], cut[:, 2]
-
-        for q in range(half // LANES // 2):
-            a, b, c = parts(2 * q)
-            d, e, f = parts(2 * q + 1)
+        theirs = [far[width + n * rows : width + (n + 1) * rows, :] for n in range(half // rows)]
+        left = jnp.concatenate([near[at, :], far[at, :]], axis=1)
+        right = jnp.concatenate([cotangent[:, mine], jnp.concatenate(theirs, axis=1)], axis=0)
+        for q in range(half // wide):
+            result = jnp.dot(
+                left, right[:, q * wide : (q + 1) * wide], preferred_element_type=F32
+            )
+
+            def parts(k):
+                cut = result[:, k * LANES : (k + 1) * LANES].reshape(pairs, 3, 8, LANES)
+                return cut[:, 0], cut[:, 1], cut[:, 2]
+
+            a, b, c = parts(0)
+            d, e, f = parts(1)
             rb, rc, rd = roll(b), roll(c), roll(d)
             even = (a, pick(b, rd), pick(rd, roll(e)))
             odd = (pick(rb, rc), pick(rc, e), f)
@@ -296,7 +299,7 @@
         copy(s).start()
         return 0
 
-    lax.fori_loop(0, width // step, rows, 0)
+    lax.fori_loop(0, width // step, chunk, 0)
     for s in range(width // step):
         copy(s).wait()
 
@@ -343,25 +346,43 @@
     term[...] = jnp.sum(sums[...], axis=0, keepdims=True)
 
 
-def terms_kernel(grad, slab, term, packed, square, columns, rounded, rest):
+def terms_kernel(
+    grad, slab, term, packed, square, columns, rounded, rest, values, cells, taken
+):
     groups, blocks, span = grad.shape[:3]
     frames = span - 2 * HALF_PAD
     taps = 31
+    some = frames // 2
+    reach = cells.shape[2]
+    start = PAD - taps // 2
     square[...] = jnp.zeros_like(square)
+    taken[...] = jnp.zeros_like(taken)
 
     def channel(cb, _):
-        for r in range(8):
-            chosen = [j for j in range(r, taps, 8)]
-            totals = [None] * len(chosen)
-            for u in range(groups):
-                for i in range(frames // 8):
-                    value = grad[u, cb, HALF_PAD + 8 * i : HALF_PAD + 8 * i + 8, :]
-                    for n, j in enumerate(chosen):
-                        place = PAD - taps // 2 + 8 * i + j
-                        part = value * slab[u, cb, pl.ds(place, 8), :]
-                        totals[n] = part if totals[n] is None else totals[n] + part
-            for n, j in enumerate(chosen):
-                square[j : j + 1, :] = jnp.sum(totals[n], axis=0, keepdims=True)
+        for u in range(groups):
+            even = grad[u, cb, pl.ds(HALF_PAD, some, stride=2), :]
+            odd = grad[u, cb, pl.ds(HALF_PAD + 1, some, stride=2), :]
+            values[0, u], values[1, u], values[2, u] = even, odd, even + odd
+            here = slab[u, cb, pl.ds(start, reach, stride=2), :]
+            there = slab[u, cb, pl.ds(start + 1, reach, stride=2), :]
+            after = slab[u, cb, pl.ds(start + 2, reach, stride=2), :]
+            cells[0, u], cells[1, u], cells[2, u] = here, there, there + after
+        for kind, lags in enumerate((taps // 2 + 1, taps // 2 + 1, taps // 2)):
+            for r in range(8):
+                chosen = [i for i in range(r, lags, 8)]
+                totals = [None] * len(chosen)
+                for u in range(groups):
+                    for m in range(0, some, 8):
+                        value = values[kind, u, m : m + 8, :]
+                        for n, i in enumerate(chosen):
+                            part = value * cells[kind, u, pl.ds(m + i, 8), :]
+                            totals[n] = part if totals[n] is None else totals[n] + part
+                for n, i in enumerate(chosen):
+                    taken[kind, i : i + 1, :] = jnp.sum(totals[n], axis=0, keepdims=True)
+        evens = taken[0] + taken[1]
+        odds = taken[2] - pltpu.roll(taken[0], 15, 0) - taken[1]
+        square[pl.ds(0, 16, stride=2), :] = evens
+        square[pl.ds(1, 16, stride=2), :] = odds
         square[taps : taps + 1, :] = term[:, lane(cb)]
         columns[lane(cb), :] = square[...].T
         return 0
@@ -502,9 +523,9 @@
             wide_shape,
             wide_shape,
             shape((groups * span, LANES), F32),
-            shape((rows, width + half), BF16),
+            shape((width + half, rows), BF16),
         ],
-        [pltpu.VMEM((span, LANES), F32), pltpu.VMEM((2 * groups * HALF_PAD, width), BF16)],
+        [pltpu.VMEM((groups * span, LANES), F32), pltpu.VMEM((2 * groups * HALF_PAD, width), BF16)],
         conv_flops,
         4,
         {2: 0, 3: 1, 4: 2},
@@ -527,18 +548,22 @@
             pltpu.VMEM((width, LANES), F32),
             pltpu.VMEM((width // 4 + 8, LANES), F32),
             pltpu.VMEM((width // 4 + 16, LANES), F32),
+            pltpu.VMEM((3, groups, frames // 2, LANES), F32),
+            pltpu.VMEM((3, groups, frames // 2 + 16, LANES), F32),
+            pltpu.VMEM((3, 16, LANES), F32),
         ],
         conv_flops,
         6,
     )(grad, slab, term_conv)
-    steps = devices // 32
+    pairs = 32
+    steps = devices // (2 * pairs)
     pieces = call(
         product_kernel,
         [SMEM] + [VMEM] * 4,
         pltpu.HBM((devices // 2, 2, deep + 8, LANES), BF16),
         [
-            pltpu.VMEM((16, 2, deep + 8, LANES), F32),
-            pltpu.VMEM((steps, 16, 2, deep + 8, LANES), BF16),
+            pltpu.VMEM((pairs, 2, deep + 8, LANES), F32),
+            pltpu.VMEM((steps, pairs, 2, deep + 8, LANES), BF16),
             pltpu.SemaphoreType.DMA((steps,)),
         ],
         4 * rows * width * half,

time: 85.6 us -> 83.6 us (0.977)
  Pallas kernels: 41.5 us -> 39.5 us
    pallas_call x1, Pallas kernels: 7.54 us -> 6.12 us  [local(): call(terms_kernel, [VMEM] * 3, shape((devices // 2, 2, 8, LANES), F32), [...]
    pallas_call x1, Pallas kernels: 4.15 us -> 3.27 us  [local(): call(product_kernel, [SMEM] + [VMEM] * 4, pltpu.HBM((devices // 2, 2, dee...]
  transfers between devices with their start and end apart: 4 -> 4, of which waited for: 1 -> 1; matrix products, arithmetic and copies ran while one was open for 0% -> 0% of each run, Pallas kernels for 32% -> 31%
where the time goes in v7:
time: 83.6 us; the launch traced here: 83.3 us
  Pallas kernels  39.5 us (47%)
  waiting for transfers between devices  25.6 us (31%)
  starting transfers between devices  15.5 us (19%)
  local copies, waits for them, and re-layouts  1.81 us (2%)
  between operations  0.86 us (1%)
    all_to_all x1, waiting for transfers between devices, local(): lax.all_to_all(pieces.reshape(devices, deep + 8, LANES), AXES, 0, 0, tile...  25.6 us
    all_to_all x1, starting transfers between devices, local(): lax.all_to_all(pieces.reshape(devices, deep + 8, LANES), AXES, 0, 0, tile...  10.4 us
    pallas_call x1, Pallas kernels, local(): call(input_kernel, [SMEM, SMEM] + [VMEM] * 3, shape((groups, frames, doub...  8.41 us
    pallas_call x1, Pallas kernels, local(): call(gate_kernel, [SMEM, SMEM] + [VMEM] * 3 + [HBM], [slab_shape, wide_sh...  8.1 us
    pallas_call x1, Pallas kernels, local(): call(terms_kernel, [VMEM] * 3, shape((devices // 2, 2, 8, LANES), F32), [...  6.12 us
    pallas_call x1, Pallas kernels, local(): call(forward_kernel, [SMEM, SMEM] + [VMEM] * 9, [slab_shape, wide_shape,...  6.09 us
    ppermute x1, starting transfers between devices, local(): lax.ppermute(outer_edge, 'seq', bridge + [(j, i) for i, j in bridge])  3.56 us
    pallas_call x1, Pallas kernels, local(): call(backward_kernel, [SMEM, SMEM] + [VMEM] * 4, [shape((groups, blocks,...  3.39 us
  transfers between devices with their start and end apart: 4, of which 1 were waited for; matrix products, arithmetic and copies ran while one was open for 0% of the time, Pallas kernels for 31%

profile of v7, /device:TPU:1, one launch (start us, length us, event | category | flops | bytes accessed | tf_op | source)
XLA Modules:
  0.0 83.3 jit_solution(108112392343959972)
XLA Ops:
  0.6 0.0 copy-start
  0.6 0.0 copy-start.1
  0.7 0.0 copy-start.7
  0.7 0.0 copy-start.6
  0.7 1.6 %shard_map.93 = (bf16[2,48,1536]{2,1,0:T(8,128)(2,1)S(1)}, bf16[2,48,1536]{2,1,0:T(8,128)(2,1)S(1)}, f32[31,1536]{1,0:T(8,128)S(1)}) custom-call(s32[1]{0:T(128)} %bitcast.place, bf16[2,192,3072]{2,1,0:T(8,128)(2,1)} %hidden.5, bf16[2,192,1536]{2,1,0:T(8,128)(2,1)} %cotangent.1, f32[31,1536]{1,0:T(8,128)} %bitcast.10), custom_call_target="tpu_custom_call" | custom-call | flops 1048576 | bytes 8388608 | tf_op jit(solution)/shard_map/pallas_call | solution.py:491
  2.3 0.0 copy-start.4
  2.3 1.5 %collective-permute-start = (bf16[2,48,1536]{2,1,0:T(8,128)(2,1)S(1)}, bf16[2,48,1536]{2,1,0:T(8,128)(2,1)S(1)}, u32[]{:S(2)}, u32[]{:S(2)}) collective-permute-start(bf16[2,48,1536]{2,1,0:T(8,128)(2,1)S(1)} %get-tuple-element.25), channel_id=1, source_target_pairs={{0,1},{1,0},{2,3},{3,2},{4,5},{5,4},{6,7},{7,6},{8,9},{9,8},{10,11... | collective-permute-start | bytes 884744 | tf_op jit(solution)/shard_map/ppermute | solution.py:506
  3.7 3.6 %collective-permute-start.1 = (bf16[2,48,1536]{2,1,0:T(8,128)(2,1)S(1)}, bf16[2,48,1536]{2,1,0:T(8,128)(2,1)S(1)}, u32[]{:S(2)}, u32[]{:S(2)}) collective-permute-start(bf16[2,48,1536]{2,1,0:T(8,128)(2,1)S(1)} %get-tuple-element.26), channel_id=1, source_target_pairs={{1,2},{3,4},{5,6},{7,8},{9,10},{11,12},{13,14},{15,16},{17,18},{19... | collective-permute-start | bytes 884744 | tf_op jit(solution)/shard_map/ppermute | solution.py:505
  7.4 8.1 %shard_map.94 = (f32[2,12,256,128]{3,2,1,0:T(8,128)S(1)}, f32[448,1536]{1,0:T(8,128)S(1)}, f32[448,1536]{1,0:T(8,128)S(1)}, bf16[1536,1536]{1,0:T(8,128)(2,1)S(1)}) custom-call(s32[2]{0:T(128)S(1)} %copy-done.6, s32[1]{0:T(128)} %bitcast.place, bf16[2,192,3072]{2,1,0:T(8,128)(2,1)S(1)} %copy-done, f32[31,1536]{1,0:T(8,128)S(1)} %get-tuple-element.21.weights, ...), custom_call_target="tpu_custom_call" | custom-call | flops 36569088 | bytes 8388608 | tf_op jit(solution)/shard_map/pallas_call | solution.py:510
  15.5 0.0 collective-permute-done.inside
  15.5 0.0 collective-permute-done.1.across
  15.5 6.1 %shard_map.95 = (f32[2,12,256,128]{3,2,1,0:T(8,128)S(1)}, f32[448,1536]{1,0:T(8,128)S(1)}, f32[448,1536]{1,0:T(8,128)S(1)}, f32[448,128]{1,0:T(8,128)S(1)}, bf16[2304,384]{1,0:T(8,128)(2,1)S(1)}) custom-call(s32[2]{0:T(128)S(1)} %copy-done.6, s32[1]{0:T(128)} %bitcast.place, ...), custom_call_target="tpu_custom_call", output_to_operand_aliasing={{0}: (2, {}), {1}: (3, {}), {2}: (4, {})} | custom-call | flops 36569088 | bytes 8388608 | tf_op jit(solution)/shard_map/pallas_call | solution.py:518
  21.6 0.1 collective-permute-start.2
  21.7 3.4 %shard_map.96 = (f32[2,12,224,128]{3,2,1,0:T(8,128)S(1)}, f32[1,1536]{1,0:T(1,128)S(1)}) custom-call(s32[2]{0:T(128)S(1)} %copy-done.6, s32[1]{0:T(128)} %bitcast.place, f32[448,1536]{1,0:T(8,128)S(1)} %get-tuple-element.28.grad, f32[448,1536]{1,0:T(8,128)S(1)} %get-tuple-element.29.hat, f32[448,128]{1,0:T(8,128)S(1)} %get-tuple-element.30.inverse, ...), custom_call_target="tpu_custom_call" | custom-call | flops 11796480 | bytes 8388608 | tf_op jit(solution)/shard_map/pallas_call | solution.py:534
  25.1 0.0 copy-start.2
  25.1 6.1 %shard_map.98.packed = f32[64,2,8,128]{3,2,1,0:T(8,128)S(1)} custom-call(f32[2,12,224,128]{3,2,1,0:T(8,128)S(1)} %get-tuple-element.31.grad, f32[2,12,256,128]{3,2,1,0:T(8,128)S(1)} %get-tuple-element.33.slab, f32[1,1536]{1,0:T(1,128)S(1)} %get-tuple-element.34.term), custom_call_target="tpu_custom_call" | custom-call | flops 36569088 | bytes 8388608 | tf_op jit(solution)/shard_map/pallas_call | solution.py:542
  31.2 0.0 collective-permute-done.2.far
  31.2 3.3 %shard_map.99 = bf16[64,2,80,128]{3,2,1,0:T(8,128)(2,1)} custom-call(s32[1]{0:T(128)} %bitcast.place, bf16[2304,384]{1,0:T(8,128)(2,1)S(1)} %get-tuple-element.32.near, bf16[384,1536]{1,0:T(8,128)(2,1)S(1)} %bitcast.8, bf16[2304,384]{1,0:T(8,128)(2,1)S(1)} %collective-permute-done.2.far, f32[64,2,8,128]{3,2,1,0:T(8,128)S(1)} %shard_map.98.packed), custom_call_target="tpu_custom_call" | custom-call | flops 1811939328 | bytes 8388608 | tf_op jit(solution)/shard_map/pallas_call | solution.py:560
  34.5 0.0 copy-start.5
  34.5 10.4 %all-to-all-start = ((bf16[128,80,128]{2,1,0:T(8,128)(2,1)}), bf16[128,80,128]{2,1,0:T(8,128)(2,1)}, u32[]{:S(2)}, u32[]{:S(2)}) async-start(bf16[128,80,128]{2,1,0:T(8,128)(2,1)} %bitcast.9), calls=%async_computation | async-start | bytes 5242880 | tf_op jit(solution)/shard_map/all_to_all | solution.py:573
  45.0 1.8 %copy-done.3 = f32[2,12,224,128]{3,2,1,0:T(8,128)S(1)} copy-done((f32[2,12,224,128]{3,2,1,0:T(8,128)S(1)}, f32[2,12,224,128]{3,2,1,0:T(8,128)}, u32[]{:S(2)}) %copy-start.3) | copy-done | bytes 2752536
  46.8 8.4 %shard_map.97 = bf16[2,192,3072]{2,1,0:T(8,128)(2,1)} custom-call(s32[2]{0:T(128)S(1)} %copy-done.6, s32[1]{0:T(128)} %bitcast.place, f32[2,12,224,128]{3,2,1,0:T(8,128)S(1)} %copy-done.3, bf16[2,192,3072]{2,1,0:T(8,128)(2,1)S(1)} %copy-done, f32[31,1536]{1,0:T(8,128)S(1)} %copy-done.5), custom_call_target="tpu_custom_call" | custom-call | flops 36569088 | bytes 8388608 | tf_op jit(solution)/shard_map/pallas_call | solution.py:574
  55.2 25.6 %all-to-all-done = bf16[128,80,128]{2,1,0:T(8,128)(2,1)} async-done(((bf16[128,80,128]{2,1,0:T(8,128)(2,1)}), bf16[128,80,128]{2,1,0:T(8,128)(2,1)}, u32[]{:S(2)}, u32[]{:S(2)}) %all-to-all-start) | async-done | bytes 2621472 | tf_op jit(solution)/shard_map/all_to_all | solution.py:573
  80.8 2.5 %shard_map.100 = (f32[12,1536]{1,0:T(8,128)}, f32[12,31]{1,0:T(8,128)}, f32[1,12]{1,0:T(1,128)}) custom-call(bf16[64,2,80,128]{3,2,1,0:T(8,128)(2,1)} %bitcast.4.got), custom_call_target="tpu_custom_call" | custom-call | flops 1048576 | bytes 8388608 | tf_op jit(solution)/shard_map/pallas_call | solution.py:585
  (9 shorter events, 0.0 us)
Async XLA Ops:
  0.6 6.7 %copy-start = (bf16[2,192,3072]{2,1,0:T(8,128)(2,1)S(1)}, bf16[2,192,3072]{2,1,0:T(8,128)(2,1)}, u32[]{:S(2)}) copy-start(bf16[2,192,3072]{2,1,0:T(8,128)(2,1)} %hidden.5) | copy-start | bytes 7077892
  0.6 6.7 %copy-start.1 = (bf16[2,192,1536]{2,1,0:T(8,128)(2,1)S(1)}, bf16[2,192,1536]{2,1,0:T(8,128)(2,1)}, u32[]{:S(2)}) copy-start(bf16[2,192,1536]{2,1,0:T(8,128)(2,1)} %cotangent.1) | copy-start | bytes 3538948
  0.7 6.6 %copy-start.7 = (f32[1536]{0:T(1024)S(1)}, f32[1536]{0:T(1024)}, u32[]{:S(2)}) copy-start(f32[1536]{0:T(1024)} %param.10) | copy-start | bytes 18436
  0.7 6.7 %copy-start.6 = (s32[2]{0:T(128)S(1)}, s32[2]{0:T(128)}, u32[]{:S(2)}) copy-start(s32[2]{0:T(128)} %lengths.7) | copy-start | bytes 28
  2.3 13.2 %copy-start.4 = (f32[31,1536]{1,0:T(8,128)}, f32[31,1536]{1,0:T(8,128)S(1)}, u32[]{:S(2)}) copy-start(f32[31,1536]{1,0:T(8,128)S(1)} %get-tuple-element.21.weights) | copy-start | bytes 571396
  2.3 13.2 %collective-permute-start = (bf16[2,48,1536]{2,1,0:T(8,128)(2,1)S(1)}, bf16[2,48,1536]{2,1,0:T(8,128)(2,1)S(1)}, u32[]{:S(2)}, u32[]{:S(2)}) collective-permute-start(bf16[2,48,1536]{2,1,0:T(8,128)(2,1)S(1)} %get-tuple-element.25), channel_id=1, source_target_pairs={{0,1},{1,0},{2,3},{3,2},{4,5},{5,4},{6,7},{7,6},{8,9},{9,8},{10,11... | collective-permute-start | bytes 884744 | tf_op jit(solution)/shard_map/ppermute | solution.py:506
  3.7 11.7 %collective-permute-start.1 = (bf16[2,48,1536]{2,1,0:T(8,128)(2,1)S(1)}, bf16[2,48,1536]{2,1,0:T(8,128)(2,1)S(1)}, u32[]{:S(2)}, u32[]{:S(2)}) collective-permute-start(bf16[2,48,1536]{2,1,0:T(8,128)(2,1)S(1)} %get-tuple-element.26), channel_id=1, source_target_pairs={{1,2},{3,4},{5,6},{7,8},{9,10},{11,12},{13,14},{15,16},{17,18},{19... | collective-permute-start | bytes 884744 | tf_op jit(solution)/shard_map/ppermute | solution.py:505
  21.6 9.6 %collective-permute-start.2 = (bf16[2304,384]{1,0:T(8,128)(2,1)S(1)}, bf16[2304,384]{1,0:T(8,128)(2,1)S(1)}, u32[]{:S(2)}, u32[]{:S(2)}) collective-permute-start(bf16[2304,384]{1,0:T(8,128)(2,1)S(1)} %get-tuple-element.32.near), channel_id=1, source_target_pairs={{0,1},{1,0},{2,3},{3,2},{4,5},{5,4},{6,7},{7,6},{8,9},{9,8},{10,11... | collective-permute-start | bytes 5308424 | tf_op jit(solution)/shard_map/ppermute | solution.py:533
  25.1 6.1 %copy-start.2 = (f32[2,12,224,128]{3,2,1,0:T(8,128)}, f32[2,12,224,128]{3,2,1,0:T(8,128)S(1)}, u32[]{:S(2)}) copy-start(f32[2,12,224,128]{3,2,1,0:T(8,128)S(1)} %get-tuple-element.31.grad) | copy-start | bytes 8257540
  34.5 10.5 %copy-start.5 = (f32[31,1536]{1,0:T(8,128)S(1)}, f32[31,1536]{1,0:T(8,128)}, u32[]{:S(2)}) copy-start(f32[31,1536]{1,0:T(8,128)} %copy-done.4) | copy-start | bytes 571396
  34.5 46.2 %all-to-all-start = ((bf16[128,80,128]{2,1,0:T(8,128)(2,1)}), bf16[128,80,128]{2,1,0:T(8,128)(2,1)}, u32[]{:S(2)}, u32[]{:S(2)}) async-start(bf16[128,80,128]{2,1,0:T(8,128)(2,1)} %bitcast.9), calls=%async_computation | async-start | bytes 5242880 | tf_op jit(solution)/shard_map/all_to_all | solution.py:573
  45.0 1.8 %copy-start.3 = (f32[2,12,224,128]{3,2,1,0:T(8,128)S(1)}, f32[2,12,224,128]{3,2,1,0:T(8,128)}, u32[]{:S(2)}) copy-start(f32[2,12,224,128]{3,2,1,0:T(8,128)} %copy-done.2) | copy-start | bytes 8257540

commit v8 on v7

--- a/solution.py
+++ b/solution.py
@@ -108,15 +108,38 @@
 CONTRACT_COLUMNS = (((1,), (1,)), ((), ()))
 
 
+def inner_rows(block, weights, cb, cells, evens, mixed, some, taps):
+    reach = cells.shape[1]
+    here = block[pl.ds(PAD + 1, reach, stride=2), :]
+    there = block[pl.ds(PAD + 2, reach, stride=2), :]
+    after = block[pl.ds(PAD + 3, reach, stride=2), :]
+    cells[0], cells[1], cells[2] = here, there, there + after
+    weight = [weights[j : j + 1, lane(cb)] for j in range(taps)]
+    paired = [weight[j] + weight[j + 1] for j in range(0, taps - 1, 2)] + [weight[taps - 1]]
+
+    def run(kind, rows, chosen):
+        total = None
+        for i, factor in enumerate(chosen):
+            part = cells[kind, pl.ds(i, rows), :] * factor
+            total = part if total is None else total + part
+        return total
+
+    evens[...] = run(0, some + 8, weight[0::2])
+    odd = run(1, some, weight[1::2])
+    mixed[pl.ds(0, some, stride=2), :] = evens[0:some, :] + odd
+    both = run(2, some, paired)
+    mixed[pl.ds(1, some, stride=2), :] = both - evens[1 : some + 1, :] - odd
+
+
 def gate_kernel(
-    lengths, place, hidden, weights, cotangent, source, slab, hat, grad, w_out, arrived
+    lengths, place, hidden, weights, cotangent, source, slab, hat, grad, w_out, arrived, cells, evens, mixed
 ):
     groups, frames, double = hidden.shape
     taps = weights.shape[0]
     width = double // 2
     blocks = width // LANES
     span = frames + 2 * HALF_PAD
-    chunk = (span - 2 * PAD) // 2
+    some = (span - 2 * PAD) // 2
 
     def copy(n):
         at = pl.ds(pl.multiple_of(n * 2 * LANES, 2 * LANES), 2 * LANES)
@@ -141,10 +164,11 @@
                 glu = jnp.where(row < limit, linear * gate, 0.0)
                 block = slab.at[u, cb]
                 block[PAD : PAD + frames, :] = glu.astype(BF16).astype(F32)
-                weight = [weights[j : j + 1, lane(cb)] for j in range(taps)]
-                for start in range(PAD, span - PAD, chunk):
-                    to = slice(base + start, base + start + chunk)
-                    hat[to, lane(cb)] = depthwise(block, weight, start, chunk, range(taps))
+                inner_rows(
+                    block, weights, cb, cells.at[u], evens.at[u], mixed.at[u], some, taps
+                )
+                to = slice(base + PAD, base + span - PAD)
+                hat[to, lane(cb)] = mixed[u]
         for u in range(groups):
             to = u * span + HALF_PAD
             grad[to : to + frames, at] = swish[u * frames : (u + 1) * frames]
@@ -355,7 +379,6 @@
     some = frames // 2
     reach = cells.shape[2]
     start = PAD - taps // 2
-    square[...] = jnp.zeros_like(square)
     taken[...] = jnp.zeros_like(taken)
 
     def channel(cb, _):
@@ -378,20 +401,33 @@
                             part = value * cells[kind, u, pl.ds(m + i, 8), :]
                             totals[n] = part if totals[n] is None else totals[n] + part
                 for n, i in enumerate(chosen):
-                    taken[kind, i : i + 1, :] = jnp.sum(totals[n], axis=0, keepdims=True)
-        evens = taken[0] + taken[1]
-        odds = taken[2] - pltpu.roll(taken[0], 15, 0) - taken[1]
-        square[pl.ds(0, 16, stride=2), :] = evens
-        square[pl.ds(1, 16, stride=2), :] = odds
-        square[taps : taps + 1, :] = term[:, lane(cb)]
-        columns[lane(cb), :] = square[...].T
+                    taken[kind, 8 * i : 8 * i + 8, :] = totals[n]
+        sums = []
+        for kind in range(3):
+            line = taken[kind, pl.ds(0, 16, stride=8), :]
+            for k in range(1, 8):
+                line = line + taken[kind, pl.ds(k, 16, stride=8), :]
+            sums.append(line)
+        evens = sums[0] + sums[1]
+        odds = sums[2] - pltpu.roll(sums[0], 15, 0) - sums[1]
+        square[cb, pl.ds(0, 16, stride=2), :] = evens
+        square[cb, pl.ds(1, 16, stride=2), :] = odds
+        square[cb, taps : taps + 1, :] = term[:, lane(cb)]
         return 0
 
     lax.fori_loop(0, blocks, channel, 0)
-    quarter = columns.shape[0] // 4
-    total = columns[pl.ds(0, quarter, stride=4), :]
-    for m in range(1, 4):
-        total = total + pltpu.roll(columns[pl.ds(m, quarter, stride=4), :], 32 * m, 1)
+    quarter = blocks * LANES // 4
+    spot = lax.broadcasted_iota(jnp.int32, (32, LANES), 1) // 32
+    lines = []
+    for g in range(blocks // 4):
+        columns[g] = square[4 * g : 4 * g + 4].reshape(LANES, LANES).T
+        for b in range(4):
+            line = jnp.zeros((32, LANES), F32)
+            for m in range(4):
+                taken_rows = columns[g, pl.ds(m, 32, stride=4), :]
+                line = jnp.where(spot == m, pltpu.roll(taken_rows, 32 * ((m - b) % 4), 1), line)
+            lines.append(line)
+    total = jnp.concatenate(lines, axis=0)
     high = total.astype(BF16).astype(F32)
     rounded[0:quarter, :] = high
     rest[8 : 8 + quarter, :] = total - high
@@ -511,7 +547,12 @@
         gate_kernel,
         [SMEM, SMEM] + [VMEM] * 3 + [HBM],
         [slab_shape, wide_shape, wide_shape, shape((width, width), BF16)],
-        [pltpu.SemaphoreType.DMA((blocks // 2,))],
+        [
+            pltpu.SemaphoreType.DMA((blocks // 2,)),
+            pltpu.VMEM((groups, 3, 104, LANES), F32),
+            pltpu.VMEM((groups, 88, LANES), F32),
+            pltpu.VMEM((groups, 160, LANES), F32),
+        ],
         conv_flops,
         4,
     )(lengths, spot, hidden, weights, flat, far_memory(w_out))
@@ -544,13 +585,13 @@
         [VMEM] * 3,
         shape((devices // 2, 2, 8, LANES), F32),
         [
-            pltpu.VMEM((LANES, LANES), F32),
-            pltpu.VMEM((width, LANES), F32),
+            pltpu.VMEM((blocks, 32, LANES), F32),
+            pltpu.VMEM((blocks // 4, LANES, LANES), F32),
             pltpu.VMEM((width // 4 + 8, LANES), F32),
             pltpu.VMEM((width // 4 + 16, LANES), F32),
             pltpu.VMEM((3, groups, frames // 2, LANES), F32),
             pltpu.VMEM((3, groups, frames // 2 + 16, LANES), F32),
-            pltpu.VMEM((3, 16, LANES), F32),
+            pltpu.VMEM((3, 128, LANES), F32),
         ],
         conv_flops,
         6,

time: 83.6 us -> 81.7 us (0.977)
  Pallas kernels: 39.5 us -> 37.6 us
    pallas_call x1, Pallas kernels: 6.12 us -> 4.64 us  [local(): call(terms_kernel, [VMEM] * 3, shape((devices // 2, 2, 8, LANES), F32), [...]
  transfers between devices with their start and end apart: 4 -> 4, of which waited for: 1 -> 1; matrix products, arithmetic and copies ran while one was open for 0% -> 0% of each run, Pallas kernels for 31% -> 30%
where the time goes in v8:
time: 81.7 us; the launch traced here: 81.4 us
  Pallas kernels  37.6 us (46%)
  waiting for transfers between devices  25.6 us (31%)
  starting transfers between devices  15.5 us (19%)
  local copies, waits for them, and re-layouts  1.81 us (2%)
  between operations  0.86 us (1%)
    all_to_all x1, waiting for transfers between devices, local(): lax.all_to_all(pieces.reshape(devices, deep + 8, LANES), AXES, 0, 0, tile...  25.6 us
    all_to_all x1, starting transfers between devices, local(): lax.all_to_all(pieces.reshape(devices, deep + 8, LANES), AXES, 0, 0, tile...  10.4 us
    pallas_call x1, Pallas kernels, local(): call(input_kernel, [SMEM, SMEM] + [VMEM] * 3, shape((groups, frames, doub...  8.41 us
    pallas_call x1, Pallas kernels, local(): call(gate_kernel, [SMEM, SMEM] + [VMEM] * 3 + [HBM], [slab_shape, wide_sh...  7.72 us
    pallas_call x1, Pallas kernels, local(): call(forward_kernel, [SMEM, SMEM] + [VMEM] * 9, [slab_shape, wide_shape,...  6.09 us
    pallas_call x1, Pallas kernels, local(): call(terms_kernel, [VMEM] * 3, shape((devices // 2, 2, 8, LANES), F32), [...  4.64 us
    ppermute x1, starting transfers between devices, local(): lax.ppermute(outer_edge, 'seq', bridge + [(j, i) for i, j in bridge])  3.56 us
    pallas_call x1, Pallas kernels, local(): call(backward_kernel, [SMEM, SMEM] + [VMEM] * 4, [shape((groups, blocks,...  3.39 us
  transfers between devices with their start and end apart: 4, of which 1 were waited for; matrix products, arithmetic and copies ran while one was open for 0% of the time, Pallas kernels for 30%

profile of v8, /device:TPU:1, one launch (start us, length us, event | category | flops | bytes accessed | tf_op | source)
XLA Modules:
  0.0 81.4 jit_solution(4919134922933633884)
XLA Ops:
  0.6 0.0 copy-start
  0.6 0.0 copy-start.1
  0.7 1.6 %shard_map.93 = (bf16[2,48,1536]{2,1,0:T(8,128)(2,1)S(1)}, bf16[2,48,1536]{2,1,0:T(8,128)(2,1)S(1)}, f32[31,1536]{1,0:T(8,128)S(1)}) custom-call(s32[1]{0:T(128)} %bitcast.place, bf16[2,192,3072]{2,1,0:T(8,128)(2,1)} %hidden.5, bf16[2,192,1536]{2,1,0:T(8,128)(2,1)} %cotangent.1, f32[31,1536]{1,0:T(8,128)} %bitcast.10), custom_call_target="tpu_custom_call" | custom-call | flops 1048576 | bytes 8388608 | tf_op jit(solution)/shard_map/pallas_call | solution.py:527
  2.3 0.0 copy-start.4
  2.3 1.5 %collective-permute-start = (bf16[2,48,1536]{2,1,0:T(8,128)(2,1)S(1)}, bf16[2,48,1536]{2,1,0:T(8,128)(2,1)S(1)}, u32[]{:S(2)}, u32[]{:S(2)}) collective-permute-start(bf16[2,48,1536]{2,1,0:T(8,128)(2,1)S(1)} %get-tuple-element.25), channel_id=1, source_target_pairs={{0,1},{1,0},{2,3},{3,2},{4,5},{5,4},{6,7},{7,6},{8,9},{9,8},{10,11... | collective-permute-start | bytes 884744 | tf_op jit(solution)/shard_map/ppermute | solution.py:542
  3.7 3.6 %collective-permute-start.1 = (bf16[2,48,1536]{2,1,0:T(8,128)(2,1)S(1)}, bf16[2,48,1536]{2,1,0:T(8,128)(2,1)S(1)}, u32[]{:S(2)}, u32[]{:S(2)}) collective-permute-start(bf16[2,48,1536]{2,1,0:T(8,128)(2,1)S(1)} %get-tuple-element.26), channel_id=1, source_target_pairs={{1,2},{3,4},{5,6},{7,8},{9,10},{11,12},{13,14},{15,16},{17,18},{19... | collective-permute-start | bytes 884744 | tf_op jit(solution)/shard_map/ppermute | solution.py:541
  7.4 7.7 %shard_map.94 = (f32[2,12,256,128]{3,2,1,0:T(8,128)S(1)}, f32[448,1536]{1,0:T(8,128)S(1)}, f32[448,1536]{1,0:T(8,128)S(1)}, bf16[1536,1536]{1,0:T(8,128)(2,1)S(1)}) custom-call(s32[2]{0:T(128)S(1)} %copy-done.6, s32[1]{0:T(128)} %bitcast.place, bf16[2,192,3072]{2,1,0:T(8,128)(2,1)S(1)} %copy-done, f32[31,1536]{1,0:T(8,128)S(1)} %get-tuple-element.21.weights, ...), custom_call_target="tpu_custom_call" | custom-call | flops 36569088 | bytes 8388608 | tf_op jit(solution)/shard_map/pallas_call | solution.py:546
  15.1 0.0 collective-permute-done.inside
  15.1 0.0 collective-permute-done.1.across
  15.1 6.1 %shard_map.95 = (f32[2,12,256,128]{3,2,1,0:T(8,128)S(1)}, f32[448,1536]{1,0:T(8,128)S(1)}, f32[448,1536]{1,0:T(8,128)S(1)}, f32[448,128]{1,0:T(8,128)S(1)}, bf16[2304,384]{1,0:T(8,128)(2,1)S(1)}) custom-call(s32[2]{0:T(128)S(1)} %copy-done.6, s32[1]{0:T(128)} %bitcast.place, ...), custom_call_target="tpu_custom_call", output_to_operand_aliasing={{0}: (2, {}), {1}: (3, {}), {2}: (4, {})} | custom-call | flops 36569088 | bytes 8388608 | tf_op jit(solution)/shard_map/pallas_call | solution.py:559
  21.2 0.1 collective-permute-start.2
  21.3 3.4 %shard_map.96 = (f32[2,12,224,128]{3,2,1,0:T(8,128)S(1)}, f32[1,1536]{1,0:T(1,128)S(1)}) custom-call(s32[2]{0:T(128)S(1)} %copy-done.6, s32[1]{0:T(128)} %bitcast.place, f32[448,1536]{1,0:T(8,128)S(1)} %get-tuple-element.28.grad, f32[448,1536]{1,0:T(8,128)S(1)} %get-tuple-element.29.hat, f32[448,128]{1,0:T(8,128)S(1)} %get-tuple-element.30.inverse, ...), custom_call_target="tpu_custom_call" | custom-call | flops 11796480 | bytes 8388608 | tf_op jit(solution)/shard_map/pallas_call | solution.py:575
  24.7 0.0 copy-start.2
  24.7 4.6 %shard_map.98.packed = f32[64,2,8,128]{3,2,1,0:T(8,128)S(1)} custom-call(f32[2,12,224,128]{3,2,1,0:T(8,128)S(1)} %get-tuple-element.31.grad, f32[2,12,256,128]{3,2,1,0:T(8,128)S(1)} %get-tuple-element.33.slab, f32[1,1536]{1,0:T(1,128)S(1)} %get-tuple-element.34.term), custom_call_target="tpu_custom_call" | custom-call | flops 36569088 | bytes 8388608 | tf_op jit(solution)/shard_map/pallas_call | solution.py:583
  29.4 0.0 collective-permute-done.2.far
  29.4 3.3 %shard_map.99 = bf16[64,2,80,128]{3,2,1,0:T(8,128)(2,1)} custom-call(s32[1]{0:T(128)} %bitcast.place, bf16[2304,384]{1,0:T(8,128)(2,1)S(1)} %get-tuple-element.32.near, bf16[384,1536]{1,0:T(8,128)(2,1)S(1)} %bitcast.8, bf16[2304,384]{1,0:T(8,128)(2,1)S(1)} %collective-permute-done.2.far, f32[64,2,8,128]{3,2,1,0:T(8,128)S(1)} %shard_map.98.packed), custom_call_target="tpu_custom_call" | custom-call | flops 1811939328 | bytes 8388608 | tf_op jit(solution)/shard_map/pallas_call | solution.py:601
  32.7 0.0 copy-start.5
  32.7 10.4 %all-to-all-start = ((bf16[128,80,128]{2,1,0:T(8,128)(2,1)}), bf16[128,80,128]{2,1,0:T(8,128)(2,1)}, u32[]{:S(2)}, u32[]{:S(2)}) async-start(bf16[128,80,128]{2,1,0:T(8,128)(2,1)} %bitcast.9), calls=%async_computation | async-start | bytes 5242880 | tf_op jit(solution)/shard_map/all_to_all | solution.py:614
  43.1 0.0 copy-done.5
  43.1 0.0 copy-start.3
  43.1 1.8 %copy-done.3 = f32[2,12,224,128]{3,2,1,0:T(8,128)S(1)} copy-done((f32[2,12,224,128]{3,2,1,0:T(8,128)S(1)}, f32[2,12,224,128]{3,2,1,0:T(8,128)}, u32[]{:S(2)}) %copy-start.3) | copy-done | bytes 2752536
  44.9 8.4 %shard_map.97 = bf16[2,192,3072]{2,1,0:T(8,128)(2,1)} custom-call(s32[2]{0:T(128)S(1)} %copy-done.6, s32[1]{0:T(128)} %bitcast.place, f32[2,12,224,128]{3,2,1,0:T(8,128)S(1)} %copy-done.3, bf16[2,192,3072]{2,1,0:T(8,128)(2,1)S(1)} %copy-done, f32[31,1536]{1,0:T(8,128)S(1)} %copy-done.5), custom_call_target="tpu_custom_call" | custom-call | flops 36569088 | bytes 8388608 | tf_op jit(solution)/shard_map/pallas_call | solution.py:615
  53.3 25.6 %all-to-all-done = bf16[128,80,128]{2,1,0:T(8,128)(2,1)} async-done(((bf16[128,80,128]{2,1,0:T(8,128)(2,1)}), bf16[128,80,128]{2,1,0:T(8,128)(2,1)}, u32[]{:S(2)}, u32[]{:S(2)}) %all-to-all-start) | async-done | bytes 2621472 | tf_op jit(solution)/shard_map/all_to_all | solution.py:614
  78.9 2.5 %shard_map.100 = (f32[12,1536]{1,0:T(8,128)}, f32[12,31]{1,0:T(8,128)}, f32[1,12]{1,0:T(1,128)}) custom-call(bf16[64,2,80,128]{3,2,1,0:T(8,128)(2,1)} %bitcast.4.got), custom_call_target="tpu_custom_call" | custom-call | flops 1048576 | bytes 8388608 | tf_op jit(solution)/shard_map/pallas_call | solution.py:626
  (9 shorter events, 0.0 us)
Async XLA Ops:
  0.6 6.7 %copy-start = (bf16[2,192,3072]{2,1,0:T(8,128)(2,1)S(1)}, bf16[2,192,3072]{2,1,0:T(8,128)(2,1)}, u32[]{:S(2)}) copy-start(bf16[2,192,3072]{2,1,0:T(8,128)(2,1)} %hidden.5) | copy-start | bytes 7077892
  0.6 6.7 %copy-start.1 = (bf16[2,192,1536]{2,1,0:T(8,128)(2,1)S(1)}, bf16[2,192,1536]{2,1,0:T(8,128)(2,1)}, u32[]{:S(2)}) copy-start(bf16[2,192,1536]{2,1,0:T(8,128)(2,1)} %cotangent.1) | copy-start | bytes 3538948
  0.7 6.6 %copy-start.7 = (f32[1536]{0:T(1024)S(1)}, f32[1536]{0:T(1024)}, u32[]{:S(2)}) copy-start(f32[1536]{0:T(1024)} %param.10) | copy-start | bytes 18436
  0.7 6.7 %copy-start.6 = (s32[2]{0:T(128)S(1)}, s32[2]{0:T(128)}, u32[]{:S(2)}) copy-start(s32[2]{0:T(128)} %lengths.7) | copy-start | bytes 28
  2.3 12.8 %copy-start.4 = (f32[31,1536]{1,0:T(8,128)}, f32[31,1536]{1,0:T(8,128)S(1)}, u32[]{:S(2)}) copy-start(f32[31,1536]{1,0:T(8,128)S(1)} %get-tuple-element.21.weights) | copy-start | bytes 571396
  2.3 12.8 %collective-permute-start = (bf16[2,48,1536]{2,1,0:T(8,128)(2,1)S(1)}, bf16[2,48,1536]{2,1,0:T(8,128)(2,1)S(1)}, u32[]{:S(2)}, u32[]{:S(2)}) collective-permute-start(bf16[2,48,1536]{2,1,0:T(8,128)(2,1)S(1)} %get-tuple-element.25), channel_id=1, source_target_pairs={{0,1},{1,0},{2,3},{3,2},{4,5},{5,4},{6,7},{7,6},{8,9},{9,8},{10,11... | collective-permute-start | bytes 884744 | tf_op jit(solution)/shard_map/ppermute | solution.py:542
  3.7 11.4 %collective-permute-start.1 = (bf16[2,48,1536]{2,1,0:T(8,128)(2,1)S(1)}, bf16[2,48,1536]{2,1,0:T(8,128)(2,1)S(1)}, u32[]{:S(2)}, u32[]{:S(2)}) collective-permute-start(bf16[2,48,1536]{2,1,0:T(8,128)(2,1)S(1)} %get-tuple-element.26), channel_id=1, source_target_pairs={{1,2},{3,4},{5,6},{7,8},{9,10},{11,12},{13,14},{15,16},{17,18},{19... | collective-permute-start | bytes 884744 | tf_op jit(solution)/shard_map/ppermute | solution.py:541
  21.2 8.2 %collective-permute-start.2 = (bf16[2304,384]{1,0:T(8,128)(2,1)S(1)}, bf16[2304,384]{1,0:T(8,128)(2,1)S(1)}, u32[]{:S(2)}, u32[]{:S(2)}) collective-permute-start(bf16[2304,384]{1,0:T(8,128)(2,1)S(1)} %get-tuple-element.32.near), channel_id=1, source_target_pairs={{0,1},{1,0},{2,3},{3,2},{4,5},{5,4},{6,7},{7,6},{8,9},{9,8},{10,11... | collective-permute-start | bytes 5308424 | tf_op jit(solution)/shard_map/ppermute | solution.py:574
  24.7 4.7 %copy-start.2 = (f32[2,12,224,128]{3,2,1,0:T(8,128)}, f32[2,12,224,128]{3,2,1,0:T(8,128)S(1)}, u32[]{:S(2)}) copy-start(f32[2,12,224,128]{3,2,1,0:T(8,128)S(1)} %get-tuple-element.31.grad) | copy-start | bytes 8257540
  32.7 10.5 %copy-start.5 = (f32[31,1536]{1,0:T(8,128)S(1)}, f32[31,1536]{1,0:T(8,128)}, u32[]{:S(2)}) copy-start(f32[31,1536]{1,0:T(8,128)} %copy-done.4) | copy-start | bytes 571396
  32.7 46.2 %all-to-all-start = ((bf16[128,80,128]{2,1,0:T(8,128)(2,1)}), bf16[128,80,128]{2,1,0:T(8,128)(2,1)}, u32[]{:S(2)}, u32[]{:S(2)}) async-start(bf16[128,80,128]{2,1,0:T(8,128)(2,1)} %bitcast.9), calls=%async_computation | async-start | bytes 5242880 | tf_op jit(solution)/shard_map/all_to_all | solution.py:614
  43.1 1.8 %copy-start.3 = (f32[2,12,224,128]{3,2,1,0:T(8,128)S(1)}, f32[2,12,224,128]{3,2,1,0:T(8,128)}, u32[]{:S(2)}) copy-start(f32[2,12,224,128]{3,2,1,0:T(8,128)} %copy-done.2) | copy-start | bytes 8257540

commit v9 on v8

--- a/solution.py
+++ b/solution.py
@@ -286,7 +286,6 @@
     half = width // 2
     pairs = scratch.shape[0]
     step = 24 * pairs
-    deep = scratch.shape[2] - 8
     wide = 2 * LANES
     first = lax.broadcasted_iota(jnp.int32, (pairs, 8, LANES), 1) < 4
     pick = lambda a, b: jnp.where(first, a, b)
@@ -301,6 +300,9 @@
         theirs = [far[width + n * rows : width + (n + 1) * rows, :] for n in range(half // rows)]
         left = jnp.concatenate([near[at, :], far[at, :]], axis=1)
         right = jnp.concatenate([cotangent[:, mine], jnp.concatenate(theirs, axis=1)], axis=0)
+        small = packed[pl.ds(s * pairs, pairs)]
+        before = small
+        split = 12 * half // LANES
         for q in range(half // wide):
             result = jnp.dot(
                 left, right[:, q * wide : (q + 1) * wide], preferred_element_type=F32
@@ -312,13 +314,14 @@
 
             a, b, c = parts(0)
             d, e, f = parts(1)
-            rb, rc, rd = roll(b), roll(c), roll(d)
-            even = (a, pick(b, rd), pick(rd, roll(e)))
-            odd = (pick(rb, rc), pick(rc, e), f)
-            for side, tiles in enumerate((even, odd)):
-                for i, tile in enumerate(tiles):
-                    scratch[:, side, 24 * q + 8 * i : 24 * q + 8 * i + 8, :] = tile
-        scratch[:, :, deep:, :] = packed[pl.ds(s * pairs, pairs)]
+            rd, re, rf = roll(d), roll(e), roll(f)
+            for i, tile in enumerate((a, pick(b, rd), pick(rd, re))):
+                scratch[:, 24 * q + 8 * i : 24 * q + 8 * i + 8, :] = tile
+            for i, tile in enumerate((pick(before, b), c, pick(re, rf))):
+                spot = split + 24 * q + 8 * i
+                scratch[:, spot : spot + 8, :] = tile
+            before = rf
+        scratch[:, 2 * split : 2 * split + 8, :] = pick(before, small)
         held[s] = scratch[...].astype(BF16)
         copy(s).start()
         return 0
@@ -371,7 +374,7 @@
 
 
 def terms_kernel(
-    grad, slab, term, packed, square, columns, rounded, rest, values, cells, taken
+    grad, slab, term, packed, square, columns, rest, values, cells, taken
 ):
     groups, blocks, span = grad.shape[:3]
     frames = span - 2 * HALF_PAD
@@ -428,16 +431,12 @@
                 line = jnp.where(spot == m, pltpu.roll(taken_rows, 32 * ((m - b) % 4), 1), line)
             lines.append(line)
     total = jnp.concatenate(lines, axis=0)
-    high = total.astype(BF16).astype(F32)
-    rounded[0:quarter, :] = high
-    rest[8 : 8 + quarter, :] = total - high
+    rest[8 : 8 + quarter, :] = total
     row = lax.broadcasted_iota(jnp.int32, (8, LANES), 0)
-    pairs, sides = packed.shape[:2]
-    for d in range(pairs * sides):
-        upper = rounded[3 * d : 3 * d + 8, :]
-        lower = rest[3 * d + 5 : 3 * d + 13, :]
-        tile = jnp.where(row < 3, upper, jnp.where(row < 6, lower, 0.0))
-        packed[d // 2, d % 2] = tile
+    for p in range(packed.shape[0]):
+        upper = rest[6 * p + 8 : 6 * p + 16, :]
+        lower = rest[6 * p + 7 : 6 * p + 15, :]
+        packed[p] = jnp.where(row < 3, upper, jnp.where((row > 3) & (row < 7), lower, 0.0))
 
 
 def input_kernel(lengths, place, grad, hidden, weights, out):
@@ -468,7 +467,7 @@
 
 def sum_kernel(factor, got, out, taps_out, gain_out, total, held, arrived):
     own = out.shape[0]
-    slots, step, _, tall, _ = held.shape
+    slots, step = held.shape[:2]
 
     def copy(i):
         return pltpu.make_async_copy(got.at[pl.ds(i * step, step)], held.at[i], arrived.at[i])
@@ -484,14 +483,14 @@
         return 0
 
     lax.fori_loop(0, slots, add, 0)
-    deep = tall - 8
-    blocks = deep // own
+    tall = total.shape[0] // 2
+    blocks = (tall - 4) // own
     for side in range(2):
         for k in range(blocks):
             at = (side * blocks + k) * LANES
-            out[:, at : at + LANES] = total[side, own * k : own * (k + 1), :] * factor
-    both = total[0, deep:, :] + total[1, deep:, :]
-    small = (both[0:3] + both[3:6]) * factor
+            start = tall * side + own * k
+            out[:, at : at + LANES] = total[start : start + own, :] * factor
+    small = (total[tall - 4 : tall - 1, :] + total[2 * tall - 4 : 2 * tall - 1, :]) * factor
     taps = taps_out.shape[1]
     spot = lax.broadcasted_iota(jnp.int32, (1, LANES), 1)
     gains = jnp.zeros((1, LANES), F32)
@@ -516,7 +515,7 @@
     rows = groups * frames
     span = frames + 2 * HALF_PAD
     length = frames + 2 * PAD
-    deep = own * half // LANES
+    tall = own * half // LANES + 4
     ends = seq_count - 1
     swap = [(i, i ^ 1) for i in range(seq_count)]
     place = lax.axis_index("seq")
@@ -583,11 +582,10 @@
     packed = call(
         terms_kernel,
         [VMEM] * 3,
-        shape((devices // 2, 2, 8, LANES), F32),
+        shape((devices // 2, 8, LANES), F32),
         [
             pltpu.VMEM((blocks, 32, LANES), F32),
             pltpu.VMEM((blocks // 4, LANES, LANES), F32),
-            pltpu.VMEM((width // 4 + 8, LANES), F32),
             pltpu.VMEM((width // 4 + 16, LANES), F32),
             pltpu.VMEM((3, groups, frames // 2, LANES), F32),
             pltpu.VMEM((3, groups, frames // 2 + 16, LANES), F32),
@@ -601,17 +599,18 @@
     pieces = call(
         product_kernel,
         [SMEM] + [VMEM] * 4,
-        pltpu.HBM((devices // 2, 2, deep + 8, LANES), BF16),
+        pltpu.HBM((devices // 2, 2 * tall, LANES), BF16),
         [
-            pltpu.VMEM((pairs, 2, deep + 8, LANES), F32),
-            pltpu.VMEM((steps, pairs, 2, deep + 8, LANES), BF16),
+            pltpu.VMEM((pairs, 2 * tall, LANES), F32),
+            pltpu.VMEM((steps, pairs, 2 * tall, LANES), BF16),
             pltpu.SemaphoreType.DMA((steps,)),
         ],
         4 * rows * width * half,
         10,
         out_specs=HBM,
     )(spot, message, flat, far, packed)
-    got = lax.all_to_all(pieces.reshape(devices, deep + 8, LANES), AXES, 0, 0, tiled=True)
+    blocked = pieces.reshape(devices, tall // 4, 4, LANES)
+    got = lax.all_to_all(blocked, AXES, 0, 0, tiled=True)
     grad_hidden = call(
         input_kernel,
         [SMEM, SMEM] + [VMEM] * 3,
@@ -628,13 +627,13 @@
         [HBM],
         [shape((own, width), F32), shape((own, taps), F32), shape((1, own), F32)],
         [
-            pltpu.VMEM((2, deep + 8, LANES), F32),
-            pltpu.VMEM((slots, devices // 2 // slots, 2, deep + 8, LANES), BF16),
+            pltpu.VMEM((2 * tall, LANES), F32),
+            pltpu.VMEM((slots, devices // 2 // slots, 2 * tall, LANES), BF16),
             pltpu.SemaphoreType.DMA((slots,)),
         ],
         1 << 20,
         6,
-    )(far_memory(got.reshape(devices // 2, 2, deep + 8, LANES)))
+    )(far_memory(got.reshape(devices // 2, 2 * tall, LANES)))
     return grad_hidden, grad_w, grad_kernel, grad_gain.reshape(own)
 
 

time: 81.7 us -> 80.2 us (0.982)
  waiting for transfers between devices: 25.6 us -> 24.2 us
    all_to_all x1, waiting for transfers between devices: 25.6 us -> 24.2 us  [local(): got = lax.all_to_all(blocked, AXES, 0, 0, tiled=True)]
where the time goes in v9:
time: 80.2 us; the launch traced here: 79.9 us
  Pallas kernels  37.6 us (47%)
  waiting for transfers between devices  24.2 us (30%)
  starting transfers between devices  15.6 us (19%)
  local copies, waits for them, and re-layouts  1.81 us (2%)
  between operations  0.86 us (1%)
    all_to_all x1, waiting for transfers between devices, local(): got = lax.all_to_all(blocked, AXES, 0, 0, tiled=True)  24.2 us
    all_to_all x1, starting transfers between devices, local(): got = lax.all_to_all(blocked, AXES, 0, 0, tiled=True)  10.4 us
    pallas_call x1, Pallas kernels, local(): call(input_kernel, [SMEM, SMEM] + [VMEM] * 3, shape((groups, frames, doub...  8.41 us
    pallas_call x1, Pallas kernels, local(): call(gate_kernel, [SMEM, SMEM] + [VMEM] * 3 + [HBM], [slab_shape, wide_sh...  7.72 us
    pallas_call x1, Pallas kernels, local(): call(forward_kernel, [SMEM, SMEM] + [VMEM] * 9, [slab_shape, wide_shape,...  6.09 us
    pallas_call x1, Pallas kernels, local(): call(terms_kernel, [VMEM] * 3, shape((devices // 2, 8, LANES), F32), [plt...  4.63 us
    ppermute x1, starting transfers between devices, local(): lax.ppermute(outer_edge, 'seq', bridge + [(j, i) for i, j in bridge])  3.56 us
    pallas_call x1, Pallas kernels, local(): call(backward_kernel, [SMEM, SMEM] + [VMEM] * 4, [shape((groups, blocks,...  3.39 us
  transfers between devices with their start and end apart: 4, of which 1 were waited for; matrix products, arithmetic and copies ran while one was open for 0% of the time, Pallas kernels for 30%

profile of v9, /device:TPU:1, one launch (start us, length us, event | category | flops | bytes accessed | tf_op | source)
XLA Modules:
  0.0 79.9 jit_solution(13815639880368652842)
XLA Ops:
  0.6 0.0 copy-start
  0.6 0.0 copy-start.1
  0.7 0.0 copy-start.7
  0.7 1.6 %shard_map.93 = (bf16[2,48,1536]{2,1,0:T(8,128)(2,1)S(1)}, bf16[2,48,1536]{2,1,0:T(8,128)(2,1)S(1)}, f32[31,1536]{1,0:T(8,128)S(1)}) custom-call(s32[1]{0:T(128)} %bitcast.place, bf16[2,192,3072]{2,1,0:T(8,128)(2,1)} %hidden.5, bf16[2,192,1536]{2,1,0:T(8,128)(2,1)} %cotangent.1, f32[31,1536]{1,0:T(8,128)} %bitcast.10), custom_call_target="tpu_custom_call" | custom-call | flops 1048576 | bytes 8388608 | tf_op jit(solution)/shard_map/pallas_call | solution.py:526
  2.3 0.0 copy-start.4
  2.3 1.5 %collective-permute-start = (bf16[2,48,1536]{2,1,0:T(8,128)(2,1)S(1)}, bf16[2,48,1536]{2,1,0:T(8,128)(2,1)S(1)}, u32[]{:S(2)}, u32[]{:S(2)}) collective-permute-start(bf16[2,48,1536]{2,1,0:T(8,128)(2,1)S(1)} %get-tuple-element.25), channel_id=1, source_target_pairs={{0,1},{1,0},{2,3},{3,2},{4,5},{5,4},{6,7},{7,6},{8,9},{9,8},{10,11... | collective-permute-start | bytes 884744 | tf_op jit(solution)/shard_map/ppermute | solution.py:541
  3.7 3.6 %collective-permute-start.1 = (bf16[2,48,1536]{2,1,0:T(8,128)(2,1)S(1)}, bf16[2,48,1536]{2,1,0:T(8,128)(2,1)S(1)}, u32[]{:S(2)}, u32[]{:S(2)}) collective-permute-start(bf16[2,48,1536]{2,1,0:T(8,128)(2,1)S(1)} %get-tuple-element.26), channel_id=1, source_target_pairs={{1,2},{3,4},{5,6},{7,8},{9,10},{11,12},{13,14},{15,16},{17,18},{19... | collective-permute-start | bytes 884744 | tf_op jit(solution)/shard_map/ppermute | solution.py:540
  7.4 7.7 %shard_map.94 = (f32[2,12,256,128]{3,2,1,0:T(8,128)S(1)}, f32[448,1536]{1,0:T(8,128)S(1)}, f32[448,1536]{1,0:T(8,128)S(1)}, bf16[1536,1536]{1,0:T(8,128)(2,1)S(1)}) custom-call(s32[2]{0:T(128)S(1)} %copy-done.6, s32[1]{0:T(128)} %bitcast.place, bf16[2,192,3072]{2,1,0:T(8,128)(2,1)S(1)} %copy-done, f32[31,1536]{1,0:T(8,128)S(1)} %get-tuple-element.21.weights, ...), custom_call_target="tpu_custom_call" | custom-call | flops 36569088 | bytes 8388608 | tf_op jit(solution)/shard_map/pallas_call | solution.py:545
  15.1 0.0 collective-permute-done.inside
  15.1 0.0 collective-permute-done.1.across
  15.1 6.1 %shard_map.95 = (f32[2,12,256,128]{3,2,1,0:T(8,128)S(1)}, f32[448,1536]{1,0:T(8,128)S(1)}, f32[448,1536]{1,0:T(8,128)S(1)}, f32[448,128]{1,0:T(8,128)S(1)}, bf16[2304,384]{1,0:T(8,128)(2,1)S(1)}) custom-call(s32[2]{0:T(128)S(1)} %copy-done.6, s32[1]{0:T(128)} %bitcast.place, ...), custom_call_target="tpu_custom_call", output_to_operand_aliasing={{0}: (2, {}), {1}: (3, {}), {2}: (4, {})} | custom-call | flops 36569088 | bytes 8388608 | tf_op jit(solution)/shard_map/pallas_call | solution.py:558
  21.2 0.1 collective-permute-start.2
  21.3 3.4 %shard_map.96 = (f32[2,12,224,128]{3,2,1,0:T(8,128)S(1)}, f32[1,1536]{1,0:T(1,128)S(1)}) custom-call(s32[2]{0:T(128)S(1)} %copy-done.6, s32[1]{0:T(128)} %bitcast.place, f32[448,1536]{1,0:T(8,128)S(1)} %get-tuple-element.28.grad, f32[448,1536]{1,0:T(8,128)S(1)} %get-tuple-element.29.hat, f32[448,128]{1,0:T(8,128)S(1)} %get-tuple-element.30.inverse, ...), custom_call_target="tpu_custom_call" | custom-call | flops 11796480 | bytes 8388608 | tf_op jit(solution)/shard_map/pallas_call | solution.py:574
  24.7 0.0 copy-start.2
  24.7 4.6 %shard_map.98.packed = f32[64,8,128]{2,1,0:T(8,128)S(1)} custom-call(f32[2,12,224,128]{3,2,1,0:T(8,128)S(1)} %get-tuple-element.31.grad, f32[2,12,256,128]{3,2,1,0:T(8,128)S(1)} %get-tuple-element.33.slab, f32[1,1536]{1,0:T(1,128)S(1)} %get-tuple-element.34.term), custom_call_target="tpu_custom_call" | custom-call | flops 36569088 | bytes 8388608 | tf_op jit(solution)/shard_map/pallas_call | solution.py:582
  29.4 0.0 copy-done.2
  29.4 0.0 collective-permute-done.2.far
  29.4 3.2 %shard_map.99 = bf16[64,152,128]{2,1,0:T(8,128)(2,1)} custom-call(s32[1]{0:T(128)} %bitcast.place, bf16[2304,384]{1,0:T(8,128)(2,1)S(1)} %get-tuple-element.32.near, bf16[384,1536]{1,0:T(8,128)(2,1)S(1)} %bitcast.8, bf16[2304,384]{1,0:T(8,128)(2,1)S(1)} %collective-permute-done.2.far, f32[64,8,128]{2,1,0:T(8,128)S(1)} %shard_map.98.packed), custom_call_target="tpu_custom_call" | custom-call | flops 1811939328 | bytes 8388608 | tf_op jit(solution)/shard_map/pallas_call | solution.py:599
  32.6 0.0 copy-start.5
  32.6 10.4 %all-to-all-start = ((bf16[128,19,4,128]{3,2,1,0:T(4,128)(2,1)}), bf16[128,19,4,128]{3,2,1,0:T(4,128)(2,1)}, u32[]{:S(2)}, u32[]{:S(2)}) async-start(bf16[128,19,4,128]{3,2,1,0:T(4,128)(2,1)} %bitcast.9), calls=%async_computation | async-start | bytes 4980736 | tf_op jit(solution)/shard_map/all_to_all | solution.py:613
  43.1 1.8 %copy-done.3 = f32[2,12,224,128]{3,2,1,0:T(8,128)S(1)} copy-done((f32[2,12,224,128]{3,2,1,0:T(8,128)S(1)}, f32[2,12,224,128]{3,2,1,0:T(8,128)}, u32[]{:S(2)}) %copy-start.3) | copy-done | bytes 2752536
  44.9 8.4 %shard_map.97 = bf16[2,192,3072]{2,1,0:T(8,128)(2,1)} custom-call(s32[2]{0:T(128)S(1)} %copy-done.6, s32[1]{0:T(128)} %bitcast.place, f32[2,12,224,128]{3,2,1,0:T(8,128)S(1)} %copy-done.3, bf16[2,192,3072]{2,1,0:T(8,128)(2,1)S(1)} %copy-done, f32[31,1536]{1,0:T(8,128)S(1)} %copy-done.5), custom_call_target="tpu_custom_call" | custom-call | flops 36569088 | bytes 8388608 | tf_op jit(solution)/shard_map/pallas_call | solution.py:614
  53.3 24.2 %all-to-all-done = bf16[128,19,4,128]{3,2,1,0:T(4,128)(2,1)} async-done(((bf16[128,19,4,128]{3,2,1,0:T(4,128)(2,1)}), bf16[128,19,4,128]{3,2,1,0:T(4,128)(2,1)}, u32[]{:S(2)}, u32[]{:S(2)}) %all-to-all-start) | async-done | bytes 2490400 | tf_op jit(solution)/shard_map/all_to_all | solution.py:613
  77.4 2.5 %shard_map.100 = (f32[12,1536]{1,0:T(8,128)}, f32[12,31]{1,0:T(8,128)}, f32[1,12]{1,0:T(1,128)}) custom-call(bf16[64,152,128]{2,1,0:T(8,128)(2,1)} %bitcast.4.got), custom_call_target="tpu_custom_call" | custom-call | flops 1048576 | bytes 8388608 | tf_op jit(solution)/shard_map/pallas_call | solution.py:625
  (9 shorter events, 0.0 us)
Async XLA Ops:
  0.6 6.7 %copy-start = (bf16[2,192,3072]{2,1,0:T(8,128)(2,1)S(1)}, bf16[2,192,3072]{2,1,0:T(8,128)(2,1)}, u32[]{:S(2)}) copy-start(bf16[2,192,3072]{2,1,0:T(8,128)(2,1)} %hidden.5) | copy-start | bytes 7077892
  0.6 6.7 %copy-start.1 = (bf16[2,192,1536]{2,1,0:T(8,128)(2,1)S(1)}, bf16[2,192,1536]{2,1,0:T(8,128)(2,1)}, u32[]{:S(2)}) copy-start(bf16[2,192,1536]{2,1,0:T(8,128)(2,1)} %cotangent.1) | copy-start | bytes 3538948
  0.7 6.6 %copy-start.7 = (f32[1536]{0:T(1024)S(1)}, f32[1536]{0:T(1024)}, u32[]{:S(2)}) copy-start(f32[1536]{0:T(1024)} %param.10) | copy-start | bytes 18436
  0.7 6.7 %copy-start.6 = (s32[2]{0:T(128)S(1)}, s32[2]{0:T(128)}, u32[]{:S(2)}) copy-start(s32[2]{0:T(128)} %lengths.7) | copy-start | bytes 28
  2.3 12.8 %copy-start.4 = (f32[31,1536]{1,0:T(8,128)}, f32[31,1536]{1,0:T(8,128)S(1)}, u32[]{:S(2)}) copy-start(f32[31,1536]{1,0:T(8,128)S(1)} %get-tuple-element.21.weights) | copy-start | bytes 571396
  2.3 12.8 %collective-permute-start = (bf16[2,48,1536]{2,1,0:T(8,128)(2,1)S(1)}, bf16[2,48,1536]{2,1,0:T(8,128)(2,1)S(1)}, u32[]{:S(2)}, u32[]{:S(2)}) collective-permute-start(bf16[2,48,1536]{2,1,0:T(8,128)(2,1)S(1)} %get-tuple-element.25), channel_id=1, source_target_pairs={{0,1},{1,0},{2,3},{3,2},{4,5},{5,4},{6,7},{7,6},{8,9},{9,8},{10,11... | collective-permute-start | bytes 884744 | tf_op jit(solution)/shard_map/ppermute | solution.py:541
  3.7 11.4 %collective-permute-start.1 = (bf16[2,48,1536]{2,1,0:T(8,128)(2,1)S(1)}, bf16[2,48,1536]{2,1,0:T(8,128)(2,1)S(1)}, u32[]{:S(2)}, u32[]{:S(2)}) collective-permute-start(bf16[2,48,1536]{2,1,0:T(8,128)(2,1)S(1)} %get-tuple-element.26), channel_id=1, source_target_pairs={{1,2},{3,4},{5,6},{7,8},{9,10},{11,12},{13,14},{15,16},{17,18},{19... | collective-permute-start | bytes 884744 | tf_op jit(solution)/shard_map/ppermute | solution.py:540
  21.2 8.2 %collective-permute-start.2 = (bf16[2304,384]{1,0:T(8,128)(2,1)S(1)}, bf16[2304,384]{1,0:T(8,128)(2,1)S(1)}, u32[]{:S(2)}, u32[]{:S(2)}) collective-permute-start(bf16[2304,384]{1,0:T(8,128)(2,1)S(1)} %get-tuple-element.32.near), channel_id=1, source_target_pairs={{0,1},{1,0},{2,3},{3,2},{4,5},{5,4},{6,7},{7,6},{8,9},{9,8},{10,11... | collective-permute-start | bytes 5308424 | tf_op jit(solution)/shard_map/ppermute | solution.py:573
  24.7 4.7 %copy-start.2 = (f32[2,12,224,128]{3,2,1,0:T(8,128)}, f32[2,12,224,128]{3,2,1,0:T(8,128)S(1)}, u32[]{:S(2)}) copy-start(f32[2,12,224,128]{3,2,1,0:T(8,128)S(1)} %get-tuple-element.31.grad) | copy-start | bytes 8257540
  32.6 10.5 %copy-start.5 = (f32[31,1536]{1,0:T(8,128)S(1)}, f32[31,1536]{1,0:T(8,128)}, u32[]{:S(2)}) copy-start(f32[31,1536]{1,0:T(8,128)} %copy-done.4) | copy-start | bytes 571396
  32.6 44.8 %all-to-all-start = ((bf16[128,19,4,128]{3,2,1,0:T(4,128)(2,1)}), bf16[128,19,4,128]{3,2,1,0:T(4,128)(2,1)}, u32[]{:S(2)}, u32[]{:S(2)}) async-start(bf16[128,19,4,128]{3,2,1,0:T(4,128)(2,1)} %bitcast.9), calls=%async_computation | async-start | bytes 4980736 | tf_op jit(solution)/shard_map/all_to_all | solution.py:613
  43.1 1.8 %copy-start.3 = (f32[2,12,224,128]{3,2,1,0:T(8,128)S(1)}, f32[2,12,224,128]{3,2,1,0:T(8,128)}, u32[]{:S(2)}) copy-start(f32[2,12,224,128]{3,2,1,0:T(8,128)} %copy-done.2) | copy-start | bytes 8257540

commit v10 on v9

--- a/solution.py
+++ b/solution.py
@@ -138,8 +138,7 @@
     taps = weights.shape[0]
     width = double // 2
     blocks = width // LANES
-    span = frames + 2 * HALF_PAD
-    some = (span - 2 * PAD) // 2
+    some = frames // 2 - HALF_PAD
 
     def copy(n):
         at = pl.ds(pl.multiple_of(n * 2 * LANES, 2 * LANES), 2 * LANES)
@@ -156,7 +155,7 @@
         )
         for u in range(groups):
             limit = left_of(lengths, place, u, frames)
-            base = u * span
+            base = u * frames
             for cb in (2 * n, 2 * n + 1):
                 row = lax.broadcasted_iota(jnp.int32, (frames, LANES), 0)
                 linear = hidden[u, :, lane(cb)].astype(F32)
@@ -167,11 +166,9 @@
                 inner_rows(
                     block, weights, cb, cells.at[u], evens.at[u], mixed.at[u], some, taps
                 )
-                to = slice(base + PAD, base + span - PAD)
+                to = slice(base + HALF_PAD, base + frames - HALF_PAD)
                 hat[to, lane(cb)] = mixed[u]
-        for u in range(groups):
-            to = u * span + HALF_PAD
-            grad[to : to + frames, at] = swish[u * frames : (u + 1) * frames]
+        grad[:, at] = swish
         return 0
 
     lax.fori_loop(0, blocks // 2, pair, 0)
@@ -180,6 +177,12 @@
 def row_mean(values, width):
     mean = jnp.sum(values, axis=-1, keepdims=True) * (1.0 / width)
     return jnp.broadcast_to(mean, values.shape)
+
+
+def sides(place, inside, across, u, rows, lanes):
+    first = (place[0] & 1) == 0
+    one, two = inside[u, rows, lanes].astype(F32), across[u, rows, lanes].astype(F32)
+    return jnp.where(first, two, one), jnp.where(first, one, two)
 
 
 def forward_kernel(
@@ -187,73 +190,49 @@
     place,
     gated,
     inner,
-    swish,
     inside,
     across,
     weights,
     gain,
     cotangent,
-    w_out,
     slab,
     hat,
-    grad,
     inverse,
     message,
     mean,
-    held,
 ):
     groups, blocks, length = slab.shape[:3]
     taps = weights.shape[0]
     width = blocks * LANES
     half = width // 2
     frames = length - 2 * PAD
-    span = frames + 2 * HALF_PAD
     rows = groups * frames
     for side in range(half // rows):
         theirs = (1 - (place[0] & 1)) * half + side * rows
         part = cotangent[:, pl.ds(pl.multiple_of(theirs, LANES), rows)]
         message[width + side * rows : width + (side + 1) * rows, :] = part
-    first = (place[0] & 1) == 0
-
-    def sides(u, rows, lanes):
-        one, two = inside[u, rows, lanes].astype(F32), across[u, rows, lanes].astype(F32)
-        return jnp.where(first, two, one), jnp.where(first, one, two)
-
-    for u in range(groups):
-        left, right = sides(u, slice(PAD, PAD + HALF_PAD), slice(0, width))
-        held[2 * u * HALF_PAD : (2 * u + 1) * HALF_PAD, :] = left.astype(BF16)
-        held[(2 * u + 1) * HALF_PAD : (2 * u + 2) * HALF_PAD, :] = right.astype(BF16)
 
     def pair(n, _):
-        at = pl.ds(pl.multiple_of(n * 2 * LANES, 2 * LANES), 2 * LANES)
-        result = lax.dot_general(
-            held[...], w_out[at, :], CONTRACT_COLUMNS, preferred_element_type=F32
-        )
         row = lax.broadcasted_iota(jnp.int32, (PAD, LANES), 0)
-        for u in range(groups):
-            limit = left_of(lengths, place, u, frames)
-            base = u * span
-            for cb in (2 * n, 2 * n + 1):
+        for cb in (2 * n, 2 * n + 1):
+            weight = [weights[j : j + 1, lane(cb)] for j in range(taps)]
+            for u in range(groups):
+                limit = left_of(lengths, place, u, frames)
+                base = u * frames
                 block = slab.at[u, cb]
-                before, after = sides(u, slice(0, PAD), lane(cb))
+                before, after = sides(place, inside, across, u, slice(0, PAD), lane(cb))
                 block[0:PAD, :] = jnp.where(row - PAD < limit, before, 0.0)
                 block[PAD + frames :, :] = jnp.where(row + frames < limit, after, 0.0)
-                weight = [weights[j : j + 1, lane(cb)] for j in range(taps)]
-                for start in (0, span - PAD):
-                    to = slice(base + start, base + start + PAD)
-                    hat[to, lane(cb)] = depthwise(block, weight, start, PAD, range(taps))
-        for u in range(groups):
-            base = u * span
-            near = 2 * u * HALF_PAD
-            grad[base : base + HALF_PAD, at] = result[near : near + HALF_PAD]
-            grad[base + span - HALF_PAD : base + span, at] = result[
-                near + HALF_PAD : near + 2 * HALF_PAD
-            ]
+                for start in (0, frames - HALF_PAD):
+                    to = slice(base + start, base + start + HALF_PAD)
+                    hat[to, lane(cb)] = depthwise(
+                        block, weight, HALF_PAD + start, HALF_PAD, range(taps)
+                    )
         return 0
 
     lax.fori_loop(0, blocks // 2, pair, 0)
     for u in range(groups):
-        rows = slice(u * span, (u + 1) * span)
+        rows = slice(u * frames, (u + 1) * frames)
         total = hat[rows, 0:LANES]
         for cb in range(1, blocks):
             total = total + hat[rows, cb * LANES : (cb + 1) * LANES]
@@ -268,10 +247,10 @@
         outs = []
         for u in range(groups):
             limit = left_of(lengths, place, u, frames)
-            rows = slice(u * span, (u + 1) * span)
+            rows = slice(u * frames, (u + 1) * frames)
             normed = (hat[rows, lane(cb)] - mean[rows, :]) * inverse[rows, :]
             hat[rows, lane(cb)] = normed
-            pre = normed[HALF_PAD : HALF_PAD + frames] * (0.5 * gain[:, lane(cb)])
+            pre = normed * (0.5 * gain[:, lane(cb)])
             out = pre * jnp.tanh(pre) + pre
             row = lax.broadcasted_iota(jnp.int32, (frames, LANES), 0)
             outs.append(jnp.where(row < limit, out, 0.0).astype(BF16))
@@ -279,6 +258,57 @@
         return 0
 
     lax.fori_loop(0, blocks, normalize, 0)
+
+
+def fringe_kernel(
+    lengths, place, grad, slab, inside, across, weights, gain, w_out, out, held, swish, hat
+):
+    groups, blocks, span = out.shape[:3]
+    taps = weights.shape[0]
+    width = blocks * LANES
+    frames = span - 2 * HALF_PAD
+    for u in range(groups):
+        pieces = sides(place, inside, across, u, slice(PAD, PAD + HALF_PAD), slice(0, width))
+        for n, piece in enumerate(pieces):
+            at = (2 * u + n) * HALF_PAD
+            held[at : at + HALF_PAD, :] = piece.astype(BF16)
+
+    def pair(n, _):
+        at = pl.ds(pl.multiple_of(n * 2 * LANES, 2 * LANES), 2 * LANES)
+        swish[:, at] = lax.dot_general(
+            held[...], w_out[at, :], CONTRACT_COLUMNS, preferred_element_type=F32
+        )
+        for cb in (2 * n, 2 * n + 1):
+            weight = [weights[j : j + 1, lane(cb)] for j in range(taps)]
+            for u in range(groups):
+                for side, start in enumerate((0, span - HALF_PAD)):
+                    to = (2 * u + side) * HALF_PAD
+                    hat[to : to + HALF_PAD, lane(cb)] = depthwise(
+                        slab.at[u, cb], weight, start, HALF_PAD, range(taps)
+                    )
+        return 0
+
+    lax.fori_loop(0, blocks // 2, pair, 0)
+    for u in range(groups):
+        limit = left_of(lengths, place, u, frames)
+        for side, start in enumerate((0, span - HALF_PAD)):
+            at = slice((2 * u + side) * HALF_PAD, (2 * u + side + 1) * HALF_PAD)
+            values = hat[at, :]
+            centered = values - jnp.sum(values, axis=-1, keepdims=True) * (1.0 / width)
+            spread = jnp.sum(centered * centered, axis=-1, keepdims=True) * (1.0 / width)
+            inv = lax.rsqrt(spread + EPSILON)
+            normed = centered * inv
+            halved = normed * (0.5 * gain[...])
+            turn = jnp.tanh(halved)
+            gate = 0.5 * turn + 0.5
+            row = start - HALF_PAD + lax.broadcasted_iota(jnp.int32, (HALF_PAD, width), 0)
+            upstream = jnp.where(row < limit, swish[at, :], 0.0)
+            scaled = upstream * (gate * (1.0 + halved * (1.0 - turn))) * gain[...]
+            mean = jnp.sum(scaled, axis=-1, keepdims=True) * (1.0 / width)
+            slope = jnp.sum(scaled * normed, axis=-1, keepdims=True) * (1.0 / width)
+            result = (inv * (scaled - mean - normed * slope)).astype(BF16).astype(F32)
+            for cb in range(blocks):
+                out[u, cb, start : start + HALF_PAD, :] = result[:, cb * LANES : (cb + 1) * LANES]
 
 
 def product_kernel(place, near, cotangent, far, packed, out, scratch, held, sent):
@@ -336,15 +366,14 @@
     width = blocks * LANES
     frames = span - 2 * HALF_PAD
     sums[...] = jnp.zeros_like(sums)
-    part = span // 2
+    part = frames // 2
 
     def norm(n, _):
         u, start = n // 2, (n % 2) * part
         at = pl.ds(pl.multiple_of(n * part, TILE), part)
         limit = left_of(lengths, place, u, frames)
-        row = start - HALF_PAD + lax.broadcasted_iota(jnp.int32, (part, LANES), 0)
+        row = start + lax.broadcasted_iota(jnp.int32, (part, LANES), 0)
         keep = row < limit
-        inside = (row >= 0) & (row < frames)
         first = second = None
         for cb in range(blocks):
             here = slice(cb * LANES, (cb + 1) * LANES)
@@ -353,7 +382,7 @@
             turn = jnp.tanh(halved)
             gate = 0.5 * turn + 0.5
             grad_pre = jnp.where(keep, grad[at, here], 0.0) * (gate * (1.0 + halved * (1.0 - turn)))
-            term_part = jnp.where(inside, grad_pre * normed, 0.0)
+            term_part = grad_pre * normed
             sums[:, here] += jnp.sum(term_part.reshape(part // 8, 8, LANES), axis=0)
             scaled = grad_pre * gain[:, here]
             work[at, here] = scaled
@@ -365,7 +394,7 @@
         for cb in range(blocks):
             here = slice(cb * LANES, (cb + 1) * LANES)
             result = inv * (work[at, here] - mean - hat[at, here] * slope)
-            to = pl.ds(pl.multiple_of(start, TILE), part)
+            to = pl.ds(pl.multiple_of(HALF_PAD + start, TILE), part)
             slab[u, cb, to, :] = result.astype(BF16).astype(F32)
         return 0
 
@@ -541,44 +570,44 @@
     inside = lax.ppermute(inner_edge, "seq", swap)
     gain = conv_gain.reshape(1, width)
     slab_shape = shape((groups, blocks, length, LANES), F32)
-    wide_shape = shape((groups * span, width), F32)
-    gated, inner, swish, w_near = call(
+    wide_shape = shape((rows, width), F32)
+    gated, inner, swish = call(
         gate_kernel,
         [SMEM, SMEM] + [VMEM] * 3 + [HBM],
-        [slab_shape, wide_shape, wide_shape, shape((width, width), BF16)],
+        [slab_shape, wide_shape, wide_shape],
         [
+            pltpu.VMEM((width, width), BF16),
             pltpu.SemaphoreType.DMA((blocks // 2,)),
             pltpu.VMEM((groups, 3, 104, LANES), F32),
             pltpu.VMEM((groups, 88, LANES), F32),
             pltpu.VMEM((groups, 160, LANES), F32),
         ],
         conv_flops,
-        4,
+        10,
     )(lengths, spot, hidden, weights, flat, far_memory(w_out))
-    slab, hat, grad_swish, inverse, message = call(
+    slab, hat, inverse, message = call(
         forward_kernel,
-        [SMEM, SMEM] + [VMEM] * 9,
+        [SMEM, SMEM] + [VMEM] * 7,
         [
             slab_shape,
             wide_shape,
-            wide_shape,
-            shape((groups * span, LANES), F32),
+            shape((rows, LANES), F32),
             shape((width + half, rows), BF16),
         ],
-        [pltpu.VMEM((groups * span, LANES), F32), pltpu.VMEM((2 * groups * HALF_PAD, width), BF16)],
+        [pltpu.VMEM((rows, LANES), F32)],
         conv_flops,
         4,
-        {2: 0, 3: 1, 4: 2},
-    )(lengths, spot, gated, inner, swish, inside, across, weights, gain, flat, w_near)
+        {2: 0, 3: 1},
+    )(lengths, spot, gated, inner, inside, across, weights, gain, flat)
     far = lax.ppermute(message, "seq", swap)
     grad, term_conv = call(
         backward_kernel,
         [SMEM, SMEM] + [VMEM] * 4,
         [shape((groups, blocks, span, LANES), F32), shape((1, width), F32)],
-        [pltpu.VMEM((groups * span, width), F32), pltpu.VMEM((8, width), F32)],
+        [pltpu.VMEM((rows, width), F32), pltpu.VMEM((8, width), F32)],
         20 * rows * width,
         6,
-    )(lengths, spot, grad_swish, hat, inverse, gain)
+    )(lengths, spot, swish, hat, inverse, gain)
     packed = call(
         terms_kernel,
         [VMEM] * 3,
@@ -611,6 +640,19 @@
     )(spot, message, flat, far, packed)
     blocked = pieces.reshape(devices, tall // 4, 4, LANES)
     got = lax.all_to_all(blocked, AXES, 0, 0, tiled=True)
+    full = call(
+        fringe_kernel,
+        [SMEM, SMEM] + [VMEM] * 7,
+        shape((groups, blocks, span, LANES), F32),
+        [
+            pltpu.VMEM((2 * groups * HALF_PAD, width), BF16),
+            pltpu.VMEM((2 * groups * HALF_PAD, width), F32),
+            pltpu.VMEM((2 * groups * HALF_PAD, width), F32),
+        ],
+        conv_flops // 6,
+        6,
+        {2: 0},
+    )(lengths, spot, grad, slab, inside, across, weights, gain, w_out)
     grad_hidden = call(
         input_kernel,
         [SMEM, SMEM] + [VMEM] * 3,
@@ -618,7 +660,7 @@
         [],
         conv_flops,
         4,
-    )(lengths, spot, grad, hidden, weights)
+    )(lengths, spot, full, hidden, weights)
 
     factor = 1.0 / math.sqrt(groups * lax.axis_size("dp") * frames * seq_count)
     slots = 4

time: 80.2 us -> 77.6 us (0.968)
  waiting for transfers between devices: 24.2 us -> 16.2 us
  local copies, waits for them, and re-layouts: 1.81 us -> 6.07 us
  Pallas kernels: 37.6 us -> 38.5 us
    all_to_all x1, waiting for transfers between devices: 24.2 us -> 16.2 us  [local(): got = lax.all_to_all(blocked, AXES, 0, 0, tiled=True)]
    unnamed x16 -> x24, local copies, waits for them, and re-layouts: 1.8 us -> 6.07 us
    pallas_call x1 -> x2, Pallas kernels: 6.09 us -> 7.33 us  [the longest x1 3.74 us: local(): call(forward_kernel, [SMEM, SMEM] + [VMEM] * 7, [slab_shape, wide_shape,...]
  transfers between devices with their start and end apart: 4 -> 4, of which waited for: 1 -> 1; matrix products, arithmetic and copies ran while one was open for 0% -> 0% of each run, Pallas kernels for 30% -> 36%
where the time goes in v10:
time: 77.6 us; the launch traced here: 77.2 us
  Pallas kernels  38.5 us (50%)
  waiting for transfers between devices  16.2 us (21%)
  starting transfers between devices  15.5 us (20%)
  local copies, waits for them, and re-layouts  6.07 us (8%)
  between operations  0.88 us (1%)
    all_to_all x1, waiting for transfers between devices, local(): got = lax.all_to_all(blocked, AXES, 0, 0, tiled=True)  16.2 us
    all_to_all x1, starting transfers between devices, local(): got = lax.all_to_all(blocked, AXES, 0, 0, tiled=True)  10.4 us
    pallas_call x1, Pallas kernels, local(): call(input_kernel, [SMEM, SMEM] + [VMEM] * 3, shape((groups, frames, doub...  8.51 us
    pallas_call x1, Pallas kernels, local(): call(gate_kernel, [SMEM, SMEM] + [VMEM] * 3 + [HBM], [slab_shape, wide_sh...  7.57 us
    unnamed x24, local copies, waits for them, and re-layouts  6.07 us
    pallas_call x1, Pallas kernels, local(): call(terms_kernel, [VMEM] * 3, shape((devices // 2, 8, LANES), F32), [plt...  4.8 us
    pallas_call x1, Pallas kernels, local(): call(forward_kernel, [SMEM, SMEM] + [VMEM] * 7, [slab_shape, wide_shape,...  3.74 us
    pallas_call x1, Pallas kernels, local(): call(fringe_kernel, [SMEM, SMEM] + [VMEM] * 7, shape((groups, blocks, spa...  3.59 us
  transfers between devices with their start and end apart: 4, of which 1 were waited for; matrix products, arithmetic and copies ran while one was open for 0% of the time, Pallas kernels for 36%

profile of v10, /device:TPU:1, one launch (start us, length us, event | category | flops | bytes accessed | tf_op | source)
XLA Modules:
  0.0 77.2 jit_solution(2171458690960844073)
XLA Ops:
  0.7 0.0 copy-start.2
  0.7 0.0 copy-start.5
  0.7 1.6 %shard_map.93 = (bf16[2,48,1536]{2,1,0:T(8,128)(2,1)S(1)}, bf16[2,48,1536]{2,1,0:T(8,128)(2,1)S(1)}, f32[31,1536]{1,0:T(8,128)S(1)}) custom-call(s32[1]{0:T(128)} %bitcast.place, bf16[2,192,3072]{2,1,0:T(8,128)(2,1)} %hidden.5, bf16[2,192,1536]{2,1,0:T(8,128)(2,1)} %cotangent.1, f32[31,1536]{1,0:T(8,128)} %bitcast.10), custom_call_target="tpu_custom_call" | custom-call | flops 1048576 | bytes 8388608 | tf_op jit(solution)/shard_map/pallas_call | solution.py:555
  2.3 1.5 %collective-permute-start = (bf16[2,48,1536]{2,1,0:T(8,128)(2,1)S(1)}, bf16[2,48,1536]{2,1,0:T(8,128)(2,1)S(1)}, u32[]{:S(2)}, u32[]{:S(2)}) collective-permute-start(bf16[2,48,1536]{2,1,0:T(8,128)(2,1)S(1)} %get-tuple-element.23), channel_id=1, source_target_pairs={{0,1},{1,0},{2,3},{3,2},{4,5},{5,4},{6,7},{7,6},{8,9},{9,8},{10,11... | collective-permute-start | bytes 884744 | tf_op jit(solution)/shard_map/ppermute | solution.py:570
  3.7 3.6 %collective-permute-start.1 = (bf16[2,48,1536]{2,1,0:T(8,128)(2,1)S(1)}, bf16[2,48,1536]{2,1,0:T(8,128)(2,1)S(1)}, u32[]{:S(2)}, u32[]{:S(2)}) collective-permute-start(bf16[2,48,1536]{2,1,0:T(8,128)(2,1)S(1)} %get-tuple-element.24), channel_id=1, source_target_pairs={{1,2},{3,4},{5,6},{7,8},{9,10},{11,12},{13,14},{15,16},{17,18},{19... | collective-permute-start | bytes 884744 | tf_op jit(solution)/shard_map/ppermute | solution.py:569
  7.3 7.6 %shard_map.94 = (f32[2,12,256,128]{3,2,1,0:T(8,128)S(1)}, f32[384,1536]{1,0:T(8,128)S(1)}, f32[384,1536]{1,0:T(8,128)S(1)}) custom-call(s32[2]{0:T(128)S(1)} %copy-done.10, s32[1]{0:T(128)} %bitcast.place, bf16[2,192,3072]{2,1,0:T(8,128)(2,1)S(1)} %copy-done.2, f32[31,1536]{1,0:T(8,128)S(1)} %get-tuple-element.19.weights, bf16[384,1536]{1,0:T(8,128)(2,1)S(1)} %bitcast.6, ...), custom_call_target="tpu_custom_call" | custom-call | flops 36569088 | bytes 8388608 | tf_op jit(solution)/shard_map/pallas_call | solution.py:574
  14.9 0.0 collective-permute-done.inside
  14.9 0.0 copy-start.6
  14.9 0.0 collective-permute-done.1.across
  15.0 3.7 %shard_map.95 = (f32[2,12,256,128]{3,2,1,0:T(8,128)S(1)}, f32[384,1536]{1,0:T(8,128)S(1)}, f32[384,128]{1,0:T(8,128)S(1)}, bf16[2304,384]{1,0:T(8,128)(2,1)S(1)}) custom-call(s32[2]{0:T(128)S(1)} %copy-done.10, s32[1]{0:T(128)} %bitcast.place, f32[2,12,256,128]{3,2,1,0:T(8,128)S(1)} %get-tuple-element.21.gated, ...), custom_call_target="tpu_custom_call", output_to_operand_aliasing={{0}: (2, {}), {1}: (3, {})} | custom-call | flops 36569088 | bytes 8388608 | tf_op jit(solution)/shard_map/pallas_call | solution.py:588
  18.7 0.1 collective-permute-start.2
  18.8 3.0 %shard_map.96 = (f32[2,12,224,128]{3,2,1,0:T(8,128)S(1)}, f32[1,1536]{1,0:T(1,128)S(1)}) custom-call(s32[2]{0:T(128)S(1)} %copy-done.10, s32[1]{0:T(128)} %bitcast.place, f32[384,1536]{1,0:T(8,128)S(1)} %get-tuple-element.20.grad, f32[384,1536]{1,0:T(8,128)S(1)} %get-tuple-element.25.hat, f32[384,128]{1,0:T(8,128)S(1)} %get-tuple-element.26.inverse, ...), custom_call_target="tpu_custom_call" | custom-call | flops 11796480 | bytes 8388608 | tf_op jit(solution)/shard_map/pallas_call | solution.py:603
  21.8 4.8 %shard_map.99.packed = f32[64,8,128]{2,1,0:T(8,128)S(1)} custom-call(f32[2,12,224,128]{3,2,1,0:T(8,128)S(1)} %get-tuple-element.27.grad, f32[2,12,256,128]{3,2,1,0:T(8,128)S(1)} %get-tuple-element.28.slab, f32[1,1536]{1,0:T(1,128)S(1)} %get-tuple-element.30.term), custom_call_target="tpu_custom_call" | custom-call | flops 36569088 | bytes 8388608 | tf_op jit(solution)/shard_map/pallas_call | solution.py:611
  26.6 0.0 collective-permute-done.2.far
  26.6 3.3 %shard_map.100 = bf16[64,152,128]{2,1,0:T(8,128)(2,1)} custom-call(s32[1]{0:T(128)} %bitcast.place, bf16[2304,384]{1,0:T(8,128)(2,1)S(1)} %get-tuple-element.29.near, bf16[384,1536]{1,0:T(8,128)(2,1)S(1)} %bitcast.8, bf16[2304,384]{1,0:T(8,128)(2,1)S(1)} %collective-permute-done.2.far, f32[64,8,128]{2,1,0:T(8,128)S(1)} %shard_map.99.packed), custom_call_target="tpu_custom_call" | custom-call | flops 1811939328 | bytes 8388608 | tf_op jit(solution)/shard_map/pallas_call | solution.py:628
  29.9 10.4 %all-to-all-start = ((bf16[128,19,4,128]{3,2,1,0:T(4,128)(2,1)}), bf16[128,19,4,128]{3,2,1,0:T(4,128)(2,1)}, u32[]{:S(2)}, u32[]{:S(2)}) async-start(bf16[128,19,4,128]{3,2,1,0:T(4,128)(2,1)} %bitcast.9), calls=%async_computation | async-start | bytes 4980736 | tf_op jit(solution)/shard_map/all_to_all | solution.py:642
  40.3 1.8 %copy-done.1 = f32[2,12,224,128]{3,2,1,0:T(8,128)S(1)} copy-done((f32[2,12,224,128]{3,2,1,0:T(8,128)S(1)}, f32[2,12,224,128]{3,2,1,0:T(8,128)}, u32[]{:S(2)}) %copy-start.1) | copy-done | bytes 2752536
  42.1 2.3 %copy-done.4 = bf16[1536,1536]{1,0:T(8,128)(2,1)S(1)} copy-done((bf16[1536,1536]{1,0:T(8,128)(2,1)S(1)}, bf16[1536,1536]{1,0:T(8,128)(2,1)}, u32[]{:S(2)}) %copy-start.4) | copy-done | bytes 4718616
  44.5 1.0 %copy-done.7 = bf16[2,48,1536]{2,1,0:T(8,128)(2,1)S(1)} copy-done((bf16[2,48,1536]{2,1,0:T(8,128)(2,1)S(1)}, bf16[2,48,1536]{2,1,0:T(8,128)(2,1)}, u32[]{:S(2)}) %copy-start.7) | copy-done | bytes 294936
  45.4 1.0 %copy-done.9 = bf16[2,48,1536]{2,1,0:T(8,128)(2,1)S(1)} copy-done((bf16[2,48,1536]{2,1,0:T(8,128)(2,1)S(1)}, bf16[2,48,1536]{2,1,0:T(8,128)(2,1)}, u32[]{:S(2)}) %copy-start.9) | copy-done | bytes 294936
  46.4 3.6 %shard_map.97.grad = f32[2,12,224,128]{3,2,1,0:T(8,128)S(1)} custom-call(s32[2]{0:T(128)S(1)} %copy-done.10, s32[1]{0:T(128)} %bitcast.place, f32[2,12,224,128]{3,2,1,0:T(8,128)S(1)} %copy-done.1, f32[2,12,256,128]{3,2,1,0:T(8,128)S(1)} %get-tuple-element.28.slab, bf16[2,48,1536]{2,1,0:T(8,128)(2,1)S(1)} %copy-done.7, ...), custom_call_target="tpu_custom_call", output_to_operand_aliasing={{}: (2, {})} | custom-call | flops 6094848 | bytes 8388608 | tf_op jit(solution)/shard_map/pallas_call | solution.py:643
  50.0 8.5 %shard_map.98 = bf16[2,192,3072]{2,1,0:T(8,128)(2,1)} custom-call(s32[2]{0:T(128)S(1)} %copy-done.10, s32[1]{0:T(128)} %bitcast.place, f32[2,12,224,128]{3,2,1,0:T(8,128)S(1)} %shard_map.97.grad, bf16[2,192,3072]{2,1,0:T(8,128)(2,1)S(1)} %copy-done.3, f32[31,1536]{1,0:T(8,128)S(1)} %get-tuple-element.19.weights), custom_call_target="tpu_custom_call" | custom-call | flops 36569088 | bytes 8388608 | tf_op jit(solution)/shard_map/pallas_call | solution.py:656
  58.5 16.2 %all-to-all-done = bf16[128,19,4,128]{3,2,1,0:T(4,128)(2,1)} async-done(((bf16[128,19,4,128]{3,2,1,0:T(4,128)(2,1)}), bf16[128,19,4,128]{3,2,1,0:T(4,128)(2,1)}, u32[]{:S(2)}, u32[]{:S(2)}) %all-to-all-start) | async-done | bytes 2490400 | tf_op jit(solution)/shard_map/all_to_all | solution.py:642
  74.7 2.5 %shard_map.101 = (f32[12,1536]{1,0:T(8,128)}, f32[12,31]{1,0:T(8,128)}, f32[1,12]{1,0:T(1,128)}) custom-call(bf16[64,152,128]{2,1,0:T(8,128)(2,1)} %bitcast.4.got), custom_call_target="tpu_custom_call" | custom-call | flops 1048576 | bytes 8388608 | tf_op jit(solution)/shard_map/pallas_call | solution.py:667
  (18 shorter events, 0.0 us)
Async XLA Ops:
  0.6 6.7 %copy-start.11 = (f32[1536]{0:T(1024)S(1)}, f32[1536]{0:T(1024)}, u32[]{:S(2)}) copy-start(f32[1536]{0:T(1024)} %param.10) | copy-start | bytes 18436
  0.6 6.7 %copy-start.10 = (s32[2]{0:T(128)S(1)}, s32[2]{0:T(128)}, u32[]{:S(2)}) copy-start(s32[2]{0:T(128)} %lengths.9) | copy-start | bytes 28
  0.7 6.7 %copy-start.2 = (bf16[2,192,3072]{2,1,0:T(8,128)(2,1)S(1)}, bf16[2,192,3072]{2,1,0:T(8,128)(2,1)}, u32[]{:S(2)}) copy-start(bf16[2,192,3072]{2,1,0:T(8,128)(2,1)} %hidden.5) | copy-start | bytes 7077892
  0.7 6.7 %copy-start.5 = (bf16[2,192,1536]{2,1,0:T(8,128)(2,1)S(1)}, bf16[2,192,1536]{2,1,0:T(8,128)(2,1)}, u32[]{:S(2)}) copy-start(bf16[2,192,1536]{2,1,0:T(8,128)(2,1)} %cotangent.1) | copy-start | bytes 3538948
  2.3 12.7 %collective-permute-start = (bf16[2,48,1536]{2,1,0:T(8,128)(2,1)S(1)}, bf16[2,48,1536]{2,1,0:T(8,128)(2,1)S(1)}, u32[]{:S(2)}, u32[]{:S(2)}) collective-permute-start(bf16[2,48,1536]{2,1,0:T(8,128)(2,1)S(1)} %get-tuple-element.23), channel_id=1, source_target_pairs={{0,1},{1,0},{2,3},{3,2},{4,5},{5,4},{6,7},{7,6},{8,9},{9,8},{10,11... | collective-permute-start | bytes 884744 | tf_op jit(solution)/shard_map/ppermute | solution.py:570
  3.7 11.2 %collective-permute-start.1 = (bf16[2,48,1536]{2,1,0:T(8,128)(2,1)S(1)}, bf16[2,48,1536]{2,1,0:T(8,128)(2,1)S(1)}, u32[]{:S(2)}, u32[]{:S(2)}) collective-permute-start(bf16[2,48,1536]{2,1,0:T(8,128)(2,1)S(1)} %get-tuple-element.24), channel_id=1, source_target_pairs={{1,2},{3,4},{5,6},{7,8},{9,10},{11,12},{13,14},{15,16},{17,18},{19... | collective-permute-start | bytes 884744 | tf_op jit(solution)/shard_map/ppermute | solution.py:569
  14.9 3.8 %copy-start.6 = (bf16[2,48,1536]{2,1,0:T(8,128)(2,1)}, bf16[2,48,1536]{2,1,0:T(8,128)(2,1)S(1)}, u32[]{:S(2)}) copy-start(bf16[2,48,1536]{2,1,0:T(8,128)(2,1)S(1)} %collective-permute-done.inside) | copy-start | bytes 884740
  15.0 3.8 %copy-start.8 = (bf16[2,48,1536]{2,1,0:T(8,128)(2,1)}, bf16[2,48,1536]{2,1,0:T(8,128)(2,1)S(1)}, u32[]{:S(2)}) copy-start(bf16[2,48,1536]{2,1,0:T(8,128)(2,1)S(1)} %collective-permute-done.1.across) | copy-start | bytes 884740
  18.7 7.9 %collective-permute-start.2 = (bf16[2304,384]{1,0:T(8,128)(2,1)S(1)}, bf16[2304,384]{1,0:T(8,128)(2,1)S(1)}, u32[]{:S(2)}, u32[]{:S(2)}) collective-permute-start(bf16[2304,384]{1,0:T(8,128)(2,1)S(1)} %get-tuple-element.29.near), channel_id=1, source_target_pairs={{0,1},{1,0},{2,3},{3,2},{4,5},{5,4},{6,7},{7,6},{8,9},{9,8},{10,11... | collective-permute-start | bytes 5308424 | tf_op jit(solution)/shard_map/ppermute | solution.py:602
  21.8 4.8 %copy-start = (f32[2,12,224,128]{3,2,1,0:T(8,128)}, f32[2,12,224,128]{3,2,1,0:T(8,128)S(1)}, u32[]{:S(2)}) copy-start(f32[2,12,224,128]{3,2,1,0:T(8,128)S(1)} %get-tuple-element.27.grad) | copy-start | bytes 8257540
  29.9 44.8 %all-to-all-start = ((bf16[128,19,4,128]{3,2,1,0:T(4,128)(2,1)}), bf16[128,19,4,128]{3,2,1,0:T(4,128)(2,1)}, u32[]{:S(2)}, u32[]{:S(2)}) async-start(bf16[128,19,4,128]{3,2,1,0:T(4,128)(2,1)} %bitcast.9), calls=%async_computation | async-start | bytes 4980736 | tf_op jit(solution)/shard_map/all_to_all | solution.py:642
  40.3 1.8 %copy-start.1 = (f32[2,12,224,128]{3,2,1,0:T(8,128)S(1)}, f32[2,12,224,128]{3,2,1,0:T(8,128)}, u32[]{:S(2)}) copy-start(f32[2,12,224,128]{3,2,1,0:T(8,128)} %copy-done) | copy-start | bytes 8257540
  42.1 2.3 %copy-start.4 = (bf16[1536,1536]{1,0:T(8,128)(2,1)S(1)}, bf16[1536,1536]{1,0:T(8,128)(2,1)}, u32[]{:S(2)}) copy-start(bf16[1536,1536]{1,0:T(8,128)(2,1)} %w_out.1) | copy-start | bytes 14155780
  44.5 1.0 %copy-start.7 = (bf16[2,48,1536]{2,1,0:T(8,128)(2,1)S(1)}, bf16[2,48,1536]{2,1,0:T(8,128)(2,1)}, u32[]{:S(2)}) copy-start(bf16[2,48,1536]{2,1,0:T(8,128)(2,1)} %copy-done.6) | copy-start | bytes 884740
  45.4 1.0 %copy-start.9 = (bf16[2,48,1536]{2,1,0:T(8,128)(2,1)S(1)}, bf16[2,48,1536]{2,1,0:T(8,128)(2,1)}, u32[]{:S(2)}) copy-start(bf16[2,48,1536]{2,1,0:T(8,128)(2,1)} %copy-done.8) | copy-start | bytes 884740
  46.4 3.6 %copy-start.3 = (bf16[2,192,3072]{2,1,0:T(8,128)(2,1)S(1)}, bf16[2,192,3072]{2,1,0:T(8,128)(2,1)}, u32[]{:S(2)}) copy-start(bf16[2,192,3072]{2,1,0:T(8,128)(2,1)} %hidden.5) | copy-start | bytes 7077892

commit v11 on v10

--- a/solution.py
+++ b/solution.py
@@ -322,8 +322,11 @@
     roll = lambda a: pltpu.roll(a, 4, 1)
     mine = pl.ds(pl.multiple_of((place[0] & 1) * half, LANES), half)
 
-    def copy(s):
-        return pltpu.make_async_copy(held.at[s], out.at[pl.ds(s * pairs, pairs)], sent.at[s])
+    part = pairs // 4
+
+    def copy(s, n):
+        at = pl.ds(s * pairs + n * part, part)
+        return pltpu.make_async_copy(held.at[s, pl.ds(n * part, part)], out.at[at], sent.at[s, n])
 
     def chunk(s, _):
         at = pl.ds(pl.multiple_of(s * step, step), step)
@@ -352,13 +355,15 @@
                 scratch[:, spot : spot + 8, :] = tile
             before = rf
         scratch[:, 2 * split : 2 * split + 8, :] = pick(before, small)
-        held[s] = scratch[...].astype(BF16)
-        copy(s).start()
+        for n in range(4):
+            held[s, n * part : (n + 1) * part] = scratch[n * part : (n + 1) * part].astype(BF16)
+            copy(s, n).start()
         return 0
 
     lax.fori_loop(0, width // step, chunk, 0)
     for s in range(width // step):
-        copy(s).wait()
+        for n in range(4):
+            copy(s, n).wait()
 
 
 def backward_kernel(lengths, place, grad, hat, inverse, gain, slab, term, work, sums):
@@ -468,6 +473,12 @@
         packed[p] = jnp.where(row < 3, upper, jnp.where((row > 3) & (row < 7), lower, 0.0))
 
 
+def gradient_kernel(lengths, place, swish, hat, inverse, gain, slab, grad, packed, term, *scratch):
+    work, sums, *rest = scratch
+    backward_kernel(lengths, place, swish, hat, inverse, gain, grad, term, work, sums)
+    terms_kernel(grad, slab, term, packed, *rest)
+
+
 def input_kernel(lengths, place, grad, hidden, weights, out):
     groups, frames, _ = hidden.shape
     blocks = grad.shape[1]
@@ -600,19 +611,17 @@
         {2: 0, 3: 1},
     )(lengths, spot, gated, inner, inside, across, weights, gain, flat)
     far = lax.ppermute(message, "seq", swap)
-    grad, term_conv = call(
-        backward_kernel,
-        [SMEM, SMEM] + [VMEM] * 4,
-        [shape((groups, blocks, span, LANES), F32), shape((1, width), F32)],
-        [pltpu.VMEM((rows, width), F32), pltpu.VMEM((8, width), F32)],
-        20 * rows * width,
-        6,
-    )(lengths, spot, swish, hat, inverse, gain)
-    packed = call(
-        terms_kernel,
-        [VMEM] * 3,
-        shape((devices // 2, 8, LANES), F32),
-        [
+    grad, packed = call(
+        gradient_kernel,
+        [SMEM, SMEM] + [VMEM] * 5,
+        [
+            shape((groups, blocks, span, LANES), F32),
+            shape((devices // 2, 8, LANES), F32),
+        ],
+        [
+            pltpu.VMEM((1, width), F32),
+            pltpu.VMEM((rows, width), F32),
+            pltpu.VMEM((8, width), F32),
             pltpu.VMEM((blocks, 32, LANES), F32),
             pltpu.VMEM((blocks // 4, LANES, LANES), F32),
             pltpu.VMEM((width // 4 + 16, LANES), F32),
@@ -621,8 +630,8 @@
             pltpu.VMEM((3, 128, LANES), F32),
         ],
         conv_flops,
-        6,
-    )(grad, slab, term_conv)
+        10,
+    )(lengths, spot, swish, hat, inverse, gain, slab)
     pairs = 32
     steps = devices // (2 * pairs)
     pieces = call(
@@ -632,7 +641,7 @@
         [
             pltpu.VMEM((pairs, 2 * tall, LANES), F32),
             pltpu.VMEM((steps, pairs, 2 * tall, LANES), BF16),
-            pltpu.SemaphoreType.DMA((steps,)),
+            pltpu.SemaphoreType.DMA((steps, 4)),
         ],
         4 * rows * width * half,
         10,
@@ -663,7 +672,7 @@
     )(lengths, spot, full, hidden, weights)
 
     factor = 1.0 / math.sqrt(groups * lax.axis_size("dp") * frames * seq_count)
-    slots = 4
+    slots = 8
     grad_w, grad_kernel, grad_gain = call(
         functools.partial(sum_kernel, factor),
         [HBM],

time: 77.6 us -> 77.4 us (level)
    pallas_call x2 -> x1, Pallas kernels: 7.77 us -> 7.73 us  [local(): call(gradient_kernel, [SMEM, SMEM] + [VMEM] * 5, [shape((groups, blocks,...]
  transfers between devices with their start and end apart: 4 -> 4, of which waited for: 1 -> 1; matrix products, arithmetic and copies ran while one was open for 0% -> 0% of each run, Pallas kernels for 36% -> 35%
where the time goes in v11:
time: 77.4 us; the launch traced here: 77 us
  Pallas kernels  38.1 us (49%)
  waiting for transfers between devices  16.5 us (21%)
  starting transfers between devices  15.5 us (20%)
  local copies, waits for them, and re-layouts  6.07 us (8%)
  between operations  0.87 us (1%)
    all_to_all x1, waiting for transfers between devices, local(): got = lax.all_to_all(blocked, AXES, 0, 0, tiled=True)  16.5 us
    all_to_all x1, starting transfers between devices, local(): got = lax.all_to_all(blocked, AXES, 0, 0, tiled=True)  10.4 us
    pallas_call x1, Pallas kernels, local(): call(input_kernel, [SMEM, SMEM] + [VMEM] * 3, shape((groups, frames, doub...  8.23 us
    pallas_call x1, Pallas kernels, local(): call(gradient_kernel, [SMEM, SMEM] + [VMEM] * 5, [shape((groups, blocks,...  7.73 us
    pallas_call x1, Pallas kernels, local(): call(gate_kernel, [SMEM, SMEM] + [VMEM] * 3 + [HBM], [slab_shape, wide_sh...  7.58 us
    unnamed x24, local copies, waits for them, and re-layouts  6.07 us
    pallas_call x1, Pallas kernels, local(): call(forward_kernel, [SMEM, SMEM] + [VMEM] * 7, [slab_shape, wide_shape,...  3.74 us
    pallas_call x1, Pallas kernels, local(): call(fringe_kernel, [SMEM, SMEM] + [VMEM] * 7, shape((groups, blocks, spa...  3.59 us
  transfers between devices with their start and end apart: 4, of which 1 were waited for; matrix products, arithmetic and copies ran while one was open for 0% of the time, Pallas kernels for 35%

profile of v11, /device:TPU:1, one launch (start us, length us, event | category | flops | bytes accessed | tf_op | source)
XLA Modules:
  0.0 77.0 jit_solution(12364581659981259103)
XLA Ops:
  0.7 0.0 copy-start
  0.7 0.0 copy-start.3
  0.7 1.6 %shard_map.93 = (bf16[2,48,1536]{2,1,0:T(8,128)(2,1)S(1)}, bf16[2,48,1536]{2,1,0:T(8,128)(2,1)S(1)}, f32[31,1536]{1,0:T(8,128)S(1)}) custom-call(s32[1]{0:T(128)} %bitcast.place, bf16[2,192,3072]{2,1,0:T(8,128)(2,1)} %hidden.5, bf16[2,192,1536]{2,1,0:T(8,128)(2,1)} %cotangent.1, f32[31,1536]{1,0:T(8,128)} %bitcast.10), custom_call_target="tpu_custom_call" | custom-call | flops 1048576 | bytes 8388608 | tf_op jit(solution)/shard_map/pallas_call | solution.py:566
  2.3 1.5 %collective-permute-start = (bf16[2,48,1536]{2,1,0:T(8,128)(2,1)S(1)}, bf16[2,48,1536]{2,1,0:T(8,128)(2,1)S(1)}, u32[]{:S(2)}, u32[]{:S(2)}) collective-permute-start(bf16[2,48,1536]{2,1,0:T(8,128)(2,1)S(1)} %get-tuple-element.23), channel_id=1, source_target_pairs={{0,1},{1,0},{2,3},{3,2},{4,5},{5,4},{6,7},{7,6},{8,9},{9,8},{10,11... | collective-permute-start | bytes 884744 | tf_op jit(solution)/shard_map/ppermute | solution.py:581
  3.7 3.6 %collective-permute-start.1 = (bf16[2,48,1536]{2,1,0:T(8,128)(2,1)S(1)}, bf16[2,48,1536]{2,1,0:T(8,128)(2,1)S(1)}, u32[]{:S(2)}, u32[]{:S(2)}) collective-permute-start(bf16[2,48,1536]{2,1,0:T(8,128)(2,1)S(1)} %get-tuple-element.24), channel_id=1, source_target_pairs={{1,2},{3,4},{5,6},{7,8},{9,10},{11,12},{13,14},{15,16},{17,18},{19... | collective-permute-start | bytes 884744 | tf_op jit(solution)/shard_map/ppermute | solution.py:580
  7.3 7.6 %shard_map.94 = (f32[2,12,256,128]{3,2,1,0:T(8,128)S(1)}, f32[384,1536]{1,0:T(8,128)S(1)}, f32[384,1536]{1,0:T(8,128)S(1)}) custom-call(s32[2]{0:T(128)S(1)} %copy-done.10, s32[1]{0:T(128)} %bitcast.place, bf16[2,192,3072]{2,1,0:T(8,128)(2,1)S(1)} %copy-done, f32[31,1536]{1,0:T(8,128)S(1)} %get-tuple-element.19.weights, bf16[384,1536]{1,0:T(8,128)(2,1)S(1)} %bitcast.6, ...), custom_call_target="tpu_custom_call" | custom-call | flops 36569088 | bytes 8388608 | tf_op jit(solution)/shard_map/pallas_call | solution.py:585
  14.9 0.0 collective-permute-done.inside
  14.9 0.0 copy-start.6
  15.0 0.0 collective-permute-done.1.across
  15.0 3.7 %shard_map.95 = (f32[2,12,256,128]{3,2,1,0:T(8,128)S(1)}, f32[384,1536]{1,0:T(8,128)S(1)}, f32[384,128]{1,0:T(8,128)S(1)}, bf16[2304,384]{1,0:T(8,128)(2,1)S(1)}) custom-call(s32[2]{0:T(128)S(1)} %copy-done.10, s32[1]{0:T(128)} %bitcast.place, f32[2,12,256,128]{3,2,1,0:T(8,128)S(1)} %get-tuple-element.21.gated, ...), custom_call_target="tpu_custom_call", output_to_operand_aliasing={{0}: (2, {}), {1}: (3, {})} | custom-call | flops 36569088 | bytes 8388608 | tf_op jit(solution)/shard_map/pallas_call | solution.py:599
  18.7 0.1 collective-permute-start.2
  18.8 7.7 %shard_map.96 = (f32[2,12,224,128]{3,2,1,0:T(8,128)S(1)}, f32[64,8,128]{2,1,0:T(8,128)S(1)}) custom-call(s32[2]{0:T(128)S(1)} %copy-done.10, s32[1]{0:T(128)} %bitcast.place, f32[384,1536]{1,0:T(8,128)S(1)} %get-tuple-element.20.swish, f32[384,1536]{1,0:T(8,128)S(1)} %get-tuple-element.25.hat, f32[384,128]{1,0:T(8,128)S(1)} %get-tuple-element.26.inverse, ...), custom_call_target="tpu_custom_call" | custom-call | flops 36569088 | bytes 8388608 | tf_op jit(solution)/shard_map/pallas_call | solution.py:614
  26.6 0.0 collective-permute-done.2.far
  26.6 3.2 %shard_map.99 = bf16[64,152,128]{2,1,0:T(8,128)(2,1)} custom-call(s32[1]{0:T(128)} %bitcast.place, bf16[2304,384]{1,0:T(8,128)(2,1)S(1)} %get-tuple-element.29.near, bf16[384,1536]{1,0:T(8,128)(2,1)S(1)} %bitcast.8, bf16[2304,384]{1,0:T(8,128)(2,1)S(1)} %collective-permute-done.2.far, f32[64,8,128]{2,1,0:T(8,128)S(1)} %get-tuple-element.30.packed), custom_call_target="tpu_custom_call" | custom-call | flops 1811939328 | bytes 8388608 | tf_op jit(solution)/shard_map/pallas_call | solution.py:637
  29.8 10.4 %all-to-all-start = ((bf16[128,19,4,128]{3,2,1,0:T(4,128)(2,1)}), bf16[128,19,4,128]{3,2,1,0:T(4,128)(2,1)}, u32[]{:S(2)}, u32[]{:S(2)}) async-start(bf16[128,19,4,128]{3,2,1,0:T(4,128)(2,1)} %bitcast.9), calls=%async_computation | async-start | bytes 4980736 | tf_op jit(solution)/shard_map/all_to_all | solution.py:651
  40.2 0.0 copy-start.2
  40.2 2.3 %copy-done.2 = bf16[1536,1536]{1,0:T(8,128)(2,1)S(1)} copy-done((bf16[1536,1536]{1,0:T(8,128)(2,1)S(1)}, bf16[1536,1536]{1,0:T(8,128)(2,1)}, u32[]{:S(2)}) %copy-start.2) | copy-done | bytes 4718616
  42.6 1.8 %copy-done.5 = f32[2,12,224,128]{3,2,1,0:T(8,128)S(1)} copy-done((f32[2,12,224,128]{3,2,1,0:T(8,128)S(1)}, f32[2,12,224,128]{3,2,1,0:T(8,128)}, u32[]{:S(2)}) %copy-start.5) | copy-done | bytes 2752536
  44.3 1.0 %copy-done.7 = bf16[2,48,1536]{2,1,0:T(8,128)(2,1)S(1)} copy-done((bf16[2,48,1536]{2,1,0:T(8,128)(2,1)S(1)}, bf16[2,48,1536]{2,1,0:T(8,128)(2,1)}, u32[]{:S(2)}) %copy-start.7) | copy-done | bytes 294936
  45.3 1.0 %copy-done.9 = bf16[2,48,1536]{2,1,0:T(8,128)(2,1)S(1)} copy-done((bf16[2,48,1536]{2,1,0:T(8,128)(2,1)S(1)}, bf16[2,48,1536]{2,1,0:T(8,128)(2,1)}, u32[]{:S(2)}) %copy-start.9) | copy-done | bytes 294936
  46.3 3.6 %shard_map.97.grad = f32[2,12,224,128]{3,2,1,0:T(8,128)S(1)} custom-call(s32[2]{0:T(128)S(1)} %copy-done.10, s32[1]{0:T(128)} %bitcast.place, f32[2,12,224,128]{3,2,1,0:T(8,128)S(1)} %copy-done.5, f32[2,12,256,128]{3,2,1,0:T(8,128)S(1)} %get-tuple-element.27.slab, bf16[2,48,1536]{2,1,0:T(8,128)(2,1)S(1)} %copy-done.7, ...), custom_call_target="tpu_custom_call", output_to_operand_aliasing={{}: (2, {})} | custom-call | flops 6094848 | bytes 8388608 | tf_op jit(solution)/shard_map/pallas_call | solution.py:652
  49.9 8.2 %shard_map.98 = bf16[2,192,3072]{2,1,0:T(8,128)(2,1)} custom-call(s32[2]{0:T(128)S(1)} %copy-done.10, s32[1]{0:T(128)} %bitcast.place, f32[2,12,224,128]{3,2,1,0:T(8,128)S(1)} %shard_map.97.grad, bf16[2,192,3072]{2,1,0:T(8,128)(2,1)S(1)} %copy-done.1, f32[31,1536]{1,0:T(8,128)S(1)} %get-tuple-element.19.weights), custom_call_target="tpu_custom_call" | custom-call | flops 36569088 | bytes 8388608 | tf_op jit(solution)/shard_map/pallas_call | solution.py:665
  58.1 16.5 %all-to-all-done = bf16[128,19,4,128]{3,2,1,0:T(4,128)(2,1)} async-done(((bf16[128,19,4,128]{3,2,1,0:T(4,128)(2,1)}), bf16[128,19,4,128]{3,2,1,0:T(4,128)(2,1)}, u32[]{:S(2)}, u32[]{:S(2)}) %all-to-all-start) | async-done | bytes 2490400 | tf_op jit(solution)/shard_map/all_to_all | solution.py:651
  74.6 2.5 %shard_map.100 = (f32[12,1536]{1,0:T(8,128)}, f32[12,31]{1,0:T(8,128)}, f32[1,12]{1,0:T(1,128)}) custom-call(bf16[64,152,128]{2,1,0:T(8,128)(2,1)} %bitcast.4.got), custom_call_target="tpu_custom_call" | custom-call | flops 1048576 | bytes 8388608 | tf_op jit(solution)/shard_map/pallas_call | solution.py:676
  (17 shorter events, 0.0 us)
Async XLA Ops:
  0.6 6.7 %copy-start.11 = (f32[1536]{0:T(1024)S(1)}, f32[1536]{0:T(1024)}, u32[]{:S(2)}) copy-start(f32[1536]{0:T(1024)} %param.10) | copy-start | bytes 18436
  0.6 6.7 %copy-start.10 = (s32[2]{0:T(128)S(1)}, s32[2]{0:T(128)}, u32[]{:S(2)}) copy-start(s32[2]{0:T(128)} %lengths.9) | copy-start | bytes 28
  0.7 6.7 %copy-start = (bf16[2,192,3072]{2,1,0:T(8,128)(2,1)S(1)}, bf16[2,192,3072]{2,1,0:T(8,128)(2,1)}, u32[]{:S(2)}) copy-start(bf16[2,192,3072]{2,1,0:T(8,128)(2,1)} %hidden.5) | copy-start | bytes 7077892
  0.7 6.7 %copy-start.3 = (bf16[2,192,1536]{2,1,0:T(8,128)(2,1)S(1)}, bf16[2,192,1536]{2,1,0:T(8,128)(2,1)}, u32[]{:S(2)}) copy-start(bf16[2,192,1536]{2,1,0:T(8,128)(2,1)} %cotangent.1) | copy-start | bytes 3538948
  2.3 12.7 %collective-permute-start = (bf16[2,48,1536]{2,1,0:T(8,128)(2,1)S(1)}, bf16[2,48,1536]{2,1,0:T(8,128)(2,1)S(1)}, u32[]{:S(2)}, u32[]{:S(2)}) collective-permute-start(bf16[2,48,1536]{2,1,0:T(8,128)(2,1)S(1)} %get-tuple-element.23), channel_id=1, source_target_pairs={{0,1},{1,0},{2,3},{3,2},{4,5},{5,4},{6,7},{7,6},{8,9},{9,8},{10,11... | collective-permute-start | bytes 884744 | tf_op jit(solution)/shard_map/ppermute | solution.py:581
  3.7 11.2 %collective-permute-start.1 = (bf16[2,48,1536]{2,1,0:T(8,128)(2,1)S(1)}, bf16[2,48,1536]{2,1,0:T(8,128)(2,1)S(1)}, u32[]{:S(2)}, u32[]{:S(2)}) collective-permute-start(bf16[2,48,1536]{2,1,0:T(8,128)(2,1)S(1)} %get-tuple-element.24), channel_id=1, source_target_pairs={{1,2},{3,4},{5,6},{7,8},{9,10},{11,12},{13,14},{15,16},{17,18},{19... | collective-permute-start | bytes 884744 | tf_op jit(solution)/shard_map/ppermute | solution.py:580
  14.9 3.8 %copy-start.6 = (bf16[2,48,1536]{2,1,0:T(8,128)(2,1)}, bf16[2,48,1536]{2,1,0:T(8,128)(2,1)S(1)}, u32[]{:S(2)}) copy-start(bf16[2,48,1536]{2,1,0:T(8,128)(2,1)S(1)} %collective-permute-done.inside) | copy-start | bytes 884740
  15.0 3.8 %copy-start.8 = (bf16[2,48,1536]{2,1,0:T(8,128)(2,1)}, bf16[2,48,1536]{2,1,0:T(8,128)(2,1)S(1)}, u32[]{:S(2)}) copy-start(bf16[2,48,1536]{2,1,0:T(8,128)(2,1)S(1)} %collective-permute-done.1.across) | copy-start | bytes 884740
  18.7 7.8 %collective-permute-start.2 = (bf16[2304,384]{1,0:T(8,128)(2,1)S(1)}, bf16[2304,384]{1,0:T(8,128)(2,1)S(1)}, u32[]{:S(2)}, u32[]{:S(2)}) collective-permute-start(bf16[2304,384]{1,0:T(8,128)(2,1)S(1)} %get-tuple-element.29.near), channel_id=1, source_target_pairs={{0,1},{1,0},{2,3},{3,2},{4,5},{5,4},{6,7},{7,6},{8,9},{9,8},{10,11... | collective-permute-start | bytes 5308424 | tf_op jit(solution)/shard_map/ppermute | solution.py:613
  26.6 3.2 %copy-start.4 = (f32[2,12,224,128]{3,2,1,0:T(8,128)}, f32[2,12,224,128]{3,2,1,0:T(8,128)S(1)}, u32[]{:S(2)}) copy-start(f32[2,12,224,128]{3,2,1,0:T(8,128)S(1)} %get-tuple-element.28.grad) | copy-start | bytes 8257540
  29.8 44.8 %all-to-all-start = ((bf16[128,19,4,128]{3,2,1,0:T(4,128)(2,1)}), bf16[128,19,4,128]{3,2,1,0:T(4,128)(2,1)}, u32[]{:S(2)}, u32[]{:S(2)}) async-start(bf16[128,19,4,128]{3,2,1,0:T(4,128)(2,1)} %bitcast.9), calls=%async_computation | async-start | bytes 4980736 | tf_op jit(solution)/shard_map/all_to_all | solution.py:651
  40.2 2.3 %copy-start.2 = (bf16[1536,1536]{1,0:T(8,128)(2,1)S(1)}, bf16[1536,1536]{1,0:T(8,128)(2,1)}, u32[]{:S(2)}) copy-start(bf16[1536,1536]{1,0:T(8,128)(2,1)} %w_out.1) | copy-start | bytes 14155780
  42.5 1.8 %copy-start.5 = (f32[2,12,224,128]{3,2,1,0:T(8,128)S(1)}, f32[2,12,224,128]{3,2,1,0:T(8,128)}, u32[]{:S(2)}) copy-start(f32[2,12,224,128]{3,2,1,0:T(8,128)} %copy-done.4) | copy-start | bytes 8257540
  44.3 1.0 %copy-start.7 = (bf16[2,48,1536]{2,1,0:T(8,128)(2,1)S(1)}, bf16[2,48,1536]{2,1,0:T(8,128)(2,1)}, u32[]{:S(2)}) copy-start(bf16[2,48,1536]{2,1,0:T(8,128)(2,1)} %copy-done.6) | copy-start | bytes 884740
  45.3 1.0 %copy-start.9 = (bf16[2,48,1536]{2,1,0:T(8,128)(2,1)S(1)}, bf16[2,48,1536]{2,1,0:T(8,128)(2,1)}, u32[]{:S(2)}) copy-start(bf16[2,48,1536]{2,1,0:T(8,128)(2,1)} %copy-done.8) | copy-start | bytes 884740
  46.3 3.6 %copy-start.1 = (bf16[2,192,3072]{2,1,0:T(8,128)(2,1)S(1)}, bf16[2,192,3072]{2,1,0:T(8,128)(2,1)}, u32[]{:S(2)}) copy-start(bf16[2,192,3072]{2,1,0:T(8,128)(2,1)} %hidden.5) | copy-start | bytes 7077892

commit v12 on v11

--- a/solution.py
+++ b/solution.py
@@ -371,10 +371,10 @@
     width = blocks * LANES
     frames = span - 2 * HALF_PAD
     sums[...] = jnp.zeros_like(sums)
-    part = frames // 2
+    part = frames // 4
 
     def norm(n, _):
-        u, start = n // 2, (n % 2) * part
+        u, start = n // 4, (n % 4) * part
         at = pl.ds(pl.multiple_of(n * part, TILE), part)
         limit = left_of(lengths, place, u, frames)
         row = start + lax.broadcasted_iota(jnp.int32, (part, LANES), 0)
@@ -403,7 +403,7 @@
             slab[u, cb, to, :] = result.astype(BF16).astype(F32)
         return 0
 
-    lax.fori_loop(0, 2 * groups, norm, 0)
+    lax.fori_loop(0, 4 * groups, norm, 0)
     term[...] = jnp.sum(sums[...], axis=0, keepdims=True)
 
 

time: 77.4 us -> 77.2 us (level)
  no operation moved by 1% of the time
where the time goes in v12:
time: 77.2 us; the launch traced here: 76.8 us
  Pallas kernels  37.8 us (49%)
  waiting for transfers between devices  16.5 us (21%)
  starting transfers between devices  15.5 us (20%)
  local copies, waits for them, and re-layouts  6.07 us (8%)
  between operations  0.87 us (1%)
    all_to_all x1, waiting for transfers between devices, local(): got = lax.all_to_all(blocked, AXES, 0, 0, tiled=True)  16.5 us
    all_to_all x1, starting transfers between devices, local(): got = lax.all_to_all(blocked, AXES, 0, 0, tiled=True)  10.4 us
    pallas_call x1, Pallas kernels, local(): call(input_kernel, [SMEM, SMEM] + [VMEM] * 3, shape((groups, frames, doub...  8.23 us
    pallas_call x1, Pallas kernels, local(): call(gate_kernel, [SMEM, SMEM] + [VMEM] * 3 + [HBM], [slab_shape, wide_sh...  7.58 us
    pallas_call x1, Pallas kernels, local(): call(gradient_kernel, [SMEM, SMEM] + [VMEM] * 5, [shape((groups, blocks,...  7.48 us
    unnamed x24, local copies, waits for them, and re-layouts  6.07 us
    pallas_call x1, Pallas kernels, local(): call(forward_kernel, [SMEM, SMEM] + [VMEM] * 7, [slab_shape, wide_shape,...  3.74 us
    pallas_call x1, Pallas kernels, local(): call(fringe_kernel, [SMEM, SMEM] + [VMEM] * 7, shape((groups, blocks, spa...  3.59 us
  transfers between devices with their start and end apart: 4, of which 1 were waited for; matrix products, arithmetic and copies ran while one was open for 0% of the time, Pallas kernels for 35%

profile of v12, /device:TPU:1, one launch (start us, length us, event | category | flops | bytes accessed | tf_op | source)
XLA Modules:
  0.0 76.8 jit_solution(14437347834085204175)
XLA Ops:
  0.7 0.0 copy-start
  0.7 0.0 copy-start.3
  0.7 1.6 %shard_map.93 = (bf16[2,48,1536]{2,1,0:T(8,128)(2,1)S(1)}, bf16[2,48,1536]{2,1,0:T(8,128)(2,1)S(1)}, f32[31,1536]{1,0:T(8,128)S(1)}) custom-call(s32[1]{0:T(128)} %bitcast.place, bf16[2,192,3072]{2,1,0:T(8,128)(2,1)} %hidden.5, bf16[2,192,1536]{2,1,0:T(8,128)(2,1)} %cotangent.1, f32[31,1536]{1,0:T(8,128)} %bitcast.10), custom_call_target="tpu_custom_call" | custom-call | flops 1048576 | bytes 8388608 | tf_op jit(solution)/shard_map/pallas_call | solution.py:566
  2.3 1.5 %collective-permute-start = (bf16[2,48,1536]{2,1,0:T(8,128)(2,1)S(1)}, bf16[2,48,1536]{2,1,0:T(8,128)(2,1)S(1)}, u32[]{:S(2)}, u32[]{:S(2)}) collective-permute-start(bf16[2,48,1536]{2,1,0:T(8,128)(2,1)S(1)} %get-tuple-element.23), channel_id=1, source_target_pairs={{0,1},{1,0},{2,3},{3,2},{4,5},{5,4},{6,7},{7,6},{8,9},{9,8},{10,11... | collective-permute-start | bytes 884744 | tf_op jit(solution)/shard_map/ppermute | solution.py:581
  3.7 3.6 %collective-permute-start.1 = (bf16[2,48,1536]{2,1,0:T(8,128)(2,1)S(1)}, bf16[2,48,1536]{2,1,0:T(8,128)(2,1)S(1)}, u32[]{:S(2)}, u32[]{:S(2)}) collective-permute-start(bf16[2,48,1536]{2,1,0:T(8,128)(2,1)S(1)} %get-tuple-element.24), channel_id=1, source_target_pairs={{1,2},{3,4},{5,6},{7,8},{9,10},{11,12},{13,14},{15,16},{17,18},{19... | collective-permute-start | bytes 884744 | tf_op jit(solution)/shard_map/ppermute | solution.py:580
  7.3 7.6 %shard_map.94 = (f32[2,12,256,128]{3,2,1,0:T(8,128)S(1)}, f32[384,1536]{1,0:T(8,128)S(1)}, f32[384,1536]{1,0:T(8,128)S(1)}) custom-call(s32[2]{0:T(128)S(1)} %copy-done.10, s32[1]{0:T(128)} %bitcast.place, bf16[2,192,3072]{2,1,0:T(8,128)(2,1)S(1)} %copy-done, f32[31,1536]{1,0:T(8,128)S(1)} %get-tuple-element.19.weights, bf16[384,1536]{1,0:T(8,128)(2,1)S(1)} %bitcast.6, ...), custom_call_target="tpu_custom_call" | custom-call | flops 36569088 | bytes 8388608 | tf_op jit(solution)/shard_map/pallas_call | solution.py:585
  14.9 0.0 collective-permute-done.inside
  14.9 0.0 copy-start.6
  15.0 0.0 collective-permute-done.1.across
  15.0 3.7 %shard_map.95 = (f32[2,12,256,128]{3,2,1,0:T(8,128)S(1)}, f32[384,1536]{1,0:T(8,128)S(1)}, f32[384,128]{1,0:T(8,128)S(1)}, bf16[2304,384]{1,0:T(8,128)(2,1)S(1)}) custom-call(s32[2]{0:T(128)S(1)} %copy-done.10, s32[1]{0:T(128)} %bitcast.place, f32[2,12,256,128]{3,2,1,0:T(8,128)S(1)} %get-tuple-element.21.gated, ...), custom_call_target="tpu_custom_call", output_to_operand_aliasing={{0}: (2, {}), {1}: (3, {})} | custom-call | flops 36569088 | bytes 8388608 | tf_op jit(solution)/shard_map/pallas_call | solution.py:599
  18.7 0.1 collective-permute-start.2
  18.8 7.5 %shard_map.96 = (f32[2,12,224,128]{3,2,1,0:T(8,128)S(1)}, f32[64,8,128]{2,1,0:T(8,128)S(1)}) custom-call(s32[2]{0:T(128)S(1)} %copy-done.10, s32[1]{0:T(128)} %bitcast.place, f32[384,1536]{1,0:T(8,128)S(1)} %get-tuple-element.20.swish, f32[384,1536]{1,0:T(8,128)S(1)} %get-tuple-element.25.hat, f32[384,128]{1,0:T(8,128)S(1)} %get-tuple-element.26.inverse, ...), custom_call_target="tpu_custom_call" | custom-call | flops 36569088 | bytes 8388608 | tf_op jit(solution)/shard_map/pallas_call | solution.py:614
  26.3 0.0 collective-permute-done.2.far
  26.3 3.2 %shard_map.99 = bf16[64,152,128]{2,1,0:T(8,128)(2,1)} custom-call(s32[1]{0:T(128)} %bitcast.place, bf16[2304,384]{1,0:T(8,128)(2,1)S(1)} %get-tuple-element.29.near, bf16[384,1536]{1,0:T(8,128)(2,1)S(1)} %bitcast.8, bf16[2304,384]{1,0:T(8,128)(2,1)S(1)} %collective-permute-done.2.far, f32[64,8,128]{2,1,0:T(8,128)S(1)} %get-tuple-element.30.packed), custom_call_target="tpu_custom_call" | custom-call | flops 1811939328 | bytes 8388608 | tf_op jit(solution)/shard_map/pallas_call | solution.py:637
  29.5 10.4 %all-to-all-start = ((bf16[128,19,4,128]{3,2,1,0:T(4,128)(2,1)}), bf16[128,19,4,128]{3,2,1,0:T(4,128)(2,1)}, u32[]{:S(2)}, u32[]{:S(2)}) async-start(bf16[128,19,4,128]{3,2,1,0:T(4,128)(2,1)} %bitcast.9), calls=%async_computation | async-start | bytes 4980736 | tf_op jit(solution)/shard_map/all_to_all | solution.py:651
  40.0 0.0 copy-start.2
  40.0 2.3 %copy-done.2 = bf16[1536,1536]{1,0:T(8,128)(2,1)S(1)} copy-done((bf16[1536,1536]{1,0:T(8,128)(2,1)S(1)}, bf16[1536,1536]{1,0:T(8,128)(2,1)}, u32[]{:S(2)}) %copy-start.2) | copy-done | bytes 4718616
  42.3 1.8 %copy-done.5 = f32[2,12,224,128]{3,2,1,0:T(8,128)S(1)} copy-done((f32[2,12,224,128]{3,2,1,0:T(8,128)S(1)}, f32[2,12,224,128]{3,2,1,0:T(8,128)}, u32[]{:S(2)}) %copy-start.5) | copy-done | bytes 2752536
  44.1 1.0 %copy-done.7 = bf16[2,48,1536]{2,1,0:T(8,128)(2,1)S(1)} copy-done((bf16[2,48,1536]{2,1,0:T(8,128)(2,1)S(1)}, bf16[2,48,1536]{2,1,0:T(8,128)(2,1)}, u32[]{:S(2)}) %copy-start.7) | copy-done | bytes 294936
  45.0 1.0 %copy-done.9 = bf16[2,48,1536]{2,1,0:T(8,128)(2,1)S(1)} copy-done((bf16[2,48,1536]{2,1,0:T(8,128)(2,1)S(1)}, bf16[2,48,1536]{2,1,0:T(8,128)(2,1)}, u32[]{:S(2)}) %copy-start.9) | copy-done | bytes 294936
  46.0 3.6 %shard_map.97.grad = f32[2,12,224,128]{3,2,1,0:T(8,128)S(1)} custom-call(s32[2]{0:T(128)S(1)} %copy-done.10, s32[1]{0:T(128)} %bitcast.place, f32[2,12,224,128]{3,2,1,0:T(8,128)S(1)} %copy-done.5, f32[2,12,256,128]{3,2,1,0:T(8,128)S(1)} %get-tuple-element.27.slab, bf16[2,48,1536]{2,1,0:T(8,128)(2,1)S(1)} %copy-done.7, ...), custom_call_target="tpu_custom_call", output_to_operand_aliasing={{}: (2, {})} | custom-call | flops 6094848 | bytes 8388608 | tf_op jit(solution)/shard_map/pallas_call | solution.py:652
  49.6 8.2 %shard_map.98 = bf16[2,192,3072]{2,1,0:T(8,128)(2,1)} custom-call(s32[2]{0:T(128)S(1)} %copy-done.10, s32[1]{0:T(128)} %bitcast.place, f32[2,12,224,128]{3,2,1,0:T(8,128)S(1)} %shard_map.97.grad, bf16[2,192,3072]{2,1,0:T(8,128)(2,1)S(1)} %copy-done.1, f32[31,1536]{1,0:T(8,128)S(1)} %get-tuple-element.19.weights), custom_call_target="tpu_custom_call" | custom-call | flops 36569088 | bytes 8388608 | tf_op jit(solution)/shard_map/pallas_call | solution.py:665
  57.8 16.5 %all-to-all-done = bf16[128,19,4,128]{3,2,1,0:T(4,128)(2,1)} async-done(((bf16[128,19,4,128]{3,2,1,0:T(4,128)(2,1)}), bf16[128,19,4,128]{3,2,1,0:T(4,128)(2,1)}, u32[]{:S(2)}, u32[]{:S(2)}) %all-to-all-start) | async-done | bytes 2490400 | tf_op jit(solution)/shard_map/all_to_all | solution.py:651
  74.3 2.5 %shard_map.100 = (f32[12,1536]{1,0:T(8,128)}, f32[12,31]{1,0:T(8,128)}, f32[1,12]{1,0:T(1,128)}) custom-call(bf16[64,152,128]{2,1,0:T(8,128)(2,1)} %bitcast.4.got), custom_call_target="tpu_custom_call" | custom-call | flops 1048576 | bytes 8388608 | tf_op jit(solution)/shard_map/pallas_call | solution.py:676
  (17 shorter events, 0.0 us)
Async XLA Ops:
  0.6 6.7 %copy-start.11 = (f32[1536]{0:T(1024)S(1)}, f32[1536]{0:T(1024)}, u32[]{:S(2)}) copy-start(f32[1536]{0:T(1024)} %param.10) | copy-start | bytes 18436
  0.6 6.7 %copy-start.10 = (s32[2]{0:T(128)S(1)}, s32[2]{0:T(128)}, u32[]{:S(2)}) copy-start(s32[2]{0:T(128)} %lengths.9) | copy-start | bytes 28
  0.7 6.7 %copy-start = (bf16[2,192,3072]{2,1,0:T(8,128)(2,1)S(1)}, bf16[2,192,3072]{2,1,0:T(8,128)(2,1)}, u32[]{:S(2)}) copy-start(bf16[2,192,3072]{2,1,0:T(8,128)(2,1)} %hidden.5) | copy-start | bytes 7077892
  0.7 6.7 %copy-start.3 = (bf16[2,192,1536]{2,1,0:T(8,128)(2,1)S(1)}, bf16[2,192,1536]{2,1,0:T(8,128)(2,1)}, u32[]{:S(2)}) copy-start(bf16[2,192,1536]{2,1,0:T(8,128)(2,1)} %cotangent.1) | copy-start | bytes 3538948
  2.3 12.7 %collective-permute-start = (bf16[2,48,1536]{2,1,0:T(8,128)(2,1)S(1)}, bf16[2,48,1536]{2,1,0:T(8,128)(2,1)S(1)}, u32[]{:S(2)}, u32[]{:S(2)}) collective-permute-start(bf16[2,48,1536]{2,1,0:T(8,128)(2,1)S(1)} %get-tuple-element.23), channel_id=1, source_target_pairs={{0,1},{1,0},{2,3},{3,2},{4,5},{5,4},{6,7},{7,6},{8,9},{9,8},{10,11... | collective-permute-start | bytes 884744 | tf_op jit(solution)/shard_map/ppermute | solution.py:581
  3.7 11.2 %collective-permute-start.1 = (bf16[2,48,1536]{2,1,0:T(8,128)(2,1)S(1)}, bf16[2,48,1536]{2,1,0:T(8,128)(2,1)S(1)}, u32[]{:S(2)}, u32[]{:S(2)}) collective-permute-start(bf16[2,48,1536]{2,1,0:T(8,128)(2,1)S(1)} %get-tuple-element.24), channel_id=1, source_target_pairs={{1,2},{3,4},{5,6},{7,8},{9,10},{11,12},{13,14},{15,16},{17,18},{19... | collective-permute-start | bytes 884744 | tf_op jit(solution)/shard_map/ppermute | solution.py:580
  14.9 3.8 %copy-start.6 = (bf16[2,48,1536]{2,1,0:T(8,128)(2,1)}, bf16[2,48,1536]{2,1,0:T(8,128)(2,1)S(1)}, u32[]{:S(2)}) copy-start(bf16[2,48,1536]{2,1,0:T(8,128)(2,1)S(1)} %collective-permute-done.inside) | copy-start | bytes 884740
  15.0 3.8 %copy-start.8 = (bf16[2,48,1536]{2,1,0:T(8,128)(2,1)}, bf16[2,48,1536]{2,1,0:T(8,128)(2,1)S(1)}, u32[]{:S(2)}) copy-start(bf16[2,48,1536]{2,1,0:T(8,128)(2,1)S(1)} %collective-permute-done.1.across) | copy-start | bytes 884740
  18.7 7.6 %collective-permute-start.2 = (bf16[2304,384]{1,0:T(8,128)(2,1)S(1)}, bf16[2304,384]{1,0:T(8,128)(2,1)S(1)}, u32[]{:S(2)}, u32[]{:S(2)}) collective-permute-start(bf16[2304,384]{1,0:T(8,128)(2,1)S(1)} %get-tuple-element.29.near), channel_id=1, source_target_pairs={{0,1},{1,0},{2,3},{3,2},{4,5},{5,4},{6,7},{7,6},{8,9},{9,8},{10,11... | collective-permute-start | bytes 5308424 | tf_op jit(solution)/shard_map/ppermute | solution.py:613
  26.3 3.2 %copy-start.4 = (f32[2,12,224,128]{3,2,1,0:T(8,128)}, f32[2,12,224,128]{3,2,1,0:T(8,128)S(1)}, u32[]{:S(2)}) copy-start(f32[2,12,224,128]{3,2,1,0:T(8,128)S(1)} %get-tuple-element.28.grad) | copy-start | bytes 8257540
  29.5 44.8 %all-to-all-start = ((bf16[128,19,4,128]{3,2,1,0:T(4,128)(2,1)}), bf16[128,19,4,128]{3,2,1,0:T(4,128)(2,1)}, u32[]{:S(2)}, u32[]{:S(2)}) async-start(bf16[128,19,4,128]{3,2,1,0:T(4,128)(2,1)} %bitcast.9), calls=%async_computation | async-start | bytes 4980736 | tf_op jit(solution)/shard_map/all_to_all | solution.py:651
  40.0 2.3 %copy-start.2 = (bf16[1536,1536]{1,0:T(8,128)(2,1)S(1)}, bf16[1536,1536]{1,0:T(8,128)(2,1)}, u32[]{:S(2)}) copy-start(bf16[1536,1536]{1,0:T(8,128)(2,1)} %w_out.1) | copy-start | bytes 14155780
  42.3 1.8 %copy-start.5 = (f32[2,12,224,128]{3,2,1,0:T(8,128)S(1)}, f32[2,12,224,128]{3,2,1,0:T(8,128)}, u32[]{:S(2)}) copy-start(f32[2,12,224,128]{3,2,1,0:T(8,128)} %copy-done.4) | copy-start | bytes 8257540
  44.1 1.0 %copy-start.7 = (bf16[2,48,1536]{2,1,0:T(8,128)(2,1)S(1)}, bf16[2,48,1536]{2,1,0:T(8,128)(2,1)}, u32[]{:S(2)}) copy-start(bf16[2,48,1536]{2,1,0:T(8,128)(2,1)} %copy-done.6) | copy-start | bytes 884740
  45.0 1.0 %copy-start.9 = (bf16[2,48,1536]{2,1,0:T(8,128)(2,1)S(1)}, bf16[2,48,1536]{2,1,0:T(8,128)(2,1)}, u32[]{:S(2)}) copy-start(bf16[2,48,1536]{2,1,0:T(8,128)(2,1)} %copy-done.8) | copy-start | bytes 884740
  46.0 3.6 %copy-start.1 = (bf16[2,192,3072]{2,1,0:T(8,128)(2,1)S(1)}, bf16[2,192,3072]{2,1,0:T(8,128)(2,1)}, u32[]{:S(2)}) copy-start(bf16[2,192,3072]{2,1,0:T(8,128)(2,1)} %hidden.5) | copy-start | bytes 7077892
